TPU v7x, 32 devices: a whole 2x2x4 slice. The times are simulated.
32 devices in a mesh: group: 2 (over y), chan: 4 (over x, core), tm: 4 (over z).
Axes of the slice: x: 2, y: 2, z: 4, core: 2. Of those that a mesh axis runs over, the one named last changes fastest.
Arguments:
- voltages: bfloat16 [2, 32, 1024, 1024], P(None, ('group', 'tm'), 'chan'), parts along dimension 1, may hold values from -6 to 6
- feed_position: int32 [1024, 2], replicated, may hold values from 0 to 63
- beam_steering: int32 [256, 2], P('group'), parts along dimension 0, may hold values from 0 to 63
- synthesis_taps: float32 [4, 1024], replicated, may hold values from 0.2 to 1
Outputs:
- synthesized: bfloat16 [2, 128, 32, 1024], P(None, 'chan', ('group', 'tm')), parts along dimension 2
There are 2 independent parts, one for each index of `group`. A program takes and returns all parts, laid end to end along the dimension named above; an argument that names none is the same for every part. Nothing has to cross between parts.
All inputs are finite; a program needn't handle non-finite values.
Results may differ from a plain program's by a relative error of at most 0.0085.
Values may be sent and summed in bfloat16 or wider, within the bound.
No kernel may reach another device: no remote copies, remote signals or barrier semaphores. Data moves between devices by JAX's collectives and lax.ppermute only.
A program may use at most 64 MiB of HBM per device.

v0:
```python
import math

import jax
import jax.numpy as jnp
from jax import lax
from jax.sharding import PartitionSpec as P

F = 1024
C = 1024
BEAMS = 128
TAPS = 4
PHASES = 4096


def passed_along(value, axis, steps):
    count = lax.axis_size(axis)
    initial, last = (max(0, -steps), min(count, count - steps))
    return lax.ppermute(value, axis, [(source, source + steps) for source in range(initial, last)])


def compute_delays(feed_position, beam_steering):
    first = feed_position[:, 0:1] * beam_steering[:, 0][None, :]
    second = feed_position[:, 1:2] * beam_steering[:, 1][None, :]
    return (first + second) % PHASES


def make_weights(delays, channel_ids):
    phases = channel_ids[:, None, None] * delays[None, :, :] % PHASES
    angles = phases.astype(jnp.float32) * (2.0 * math.pi / PHASES)
    return jnp.concatenate([jnp.cos(angles), jnp.sin(angles)], axis=-1).astype(jnp.bfloat16)


def combine(product):
    half = product.shape[-1] // 2
    real_part = product[0, ..., :half] - product[1, ..., half:]
    imag_part = product[0, ..., half:] + product[1, ..., :half]
    return (jnp.stack([real_part, imag_part]) * (1.0 / math.sqrt(F))).astype(jnp.bfloat16)


def make_basis():
    rows = lax.iota(jnp.int32, C)
    products = rows[:, None] * rows[None, :] % C
    angles = products.astype(jnp.float32) * (2.0 * math.pi / C)
    cosine = jnp.cos(angles)
    sine = jnp.sin(angles)
    upper = jnp.concatenate([cosine, sine], axis=1)
    lower = jnp.concatenate([-sine, cosine], axis=1)
    return jnp.stack([upper, lower]).astype(jnp.bfloat16)


def beamform(turned, delays, channel_ids):
    chan_count = turned.shape[3]
    width = math.gcd(chan_count, 8)
    count = chan_count // width

    def one_block(block_index, result):
        offset = block_index * width
        slab = lax.dynamic_slice_in_dim(turned, offset, width, 3)
        block_ids = lax.dynamic_slice_in_dim(channel_ids, offset, width, 0)
        weights = make_weights(delays, block_ids)
        product = jnp.einsum("stfc,cfk->stck", slab, weights, preferred_element_type=jnp.float32)
        return lax.dynamic_update_slice_in_dim(result, combine(product), offset, 2)

    initial = jnp.zeros((2, turned.shape[1], chan_count, BEAMS), jnp.bfloat16)
    return lax.fori_loop(0, count, one_block, initial)


def synthesize(beamed, basis):
    frames = jnp.einsum("stcb,scn->tbn", beamed, basis, preferred_element_type=jnp.float32)
    return (frames * (1.0 / math.sqrt(C))).astype(jnp.bfloat16)


def apply_taps(extended, synthesis_taps):
    frame_count = extended.shape[0] - (TAPS - 1)
    widened = extended.astype(jnp.float32)
    doubled = jnp.concatenate([synthesis_taps, synthesis_taps], axis=1)
    total = jnp.zeros((frame_count,) + extended.shape[1:], jnp.float32)
    for tap_index in range(TAPS):
        begin = TAPS - 1 - tap_index
        total = total + doubled[tap_index][None, None, :] * widened[begin : begin + frame_count]
    output = total.astype(jnp.bfloat16).reshape(frame_count, extended.shape[1], 2, C)
    return jnp.transpose(output, (2, 1, 0, 3))


def on_device(voltages, feed_position, beam_steering, synthesis_taps):
    devices_chan = lax.axis_size("chan")
    chan_count = C // devices_chan
    chan_start = lax.axis_index("chan") * chan_count
    delays = compute_delays(feed_position, beam_steering)
    turned = lax.all_to_all(voltages, "chan", split_axis=3, concat_axis=2, tiled=True)
    channel_ids = chan_start + lax.iota(jnp.int32, chan_count)
    beamed = beamform(turned, delays, channel_ids)
    regrouped = lax.all_to_all(beamed, "chan", split_axis=3, concat_axis=2, tiled=True)
    basis = make_basis()
    frames = synthesize(regrouped, basis)
    carried = passed_along(frames[frames.shape[0] - (TAPS - 1) :], "tm", 1)
    extended = jnp.concatenate([carried, frames], axis=0)
    return apply_taps(extended, synthesis_taps)


def solution(mesh):
    return jax.shard_map(
        on_device,
        mesh=mesh,
        in_specs=(P(None, ("group", "tm"), "chan", None), P(), P("group", None), P()),
        out_specs=P(None, "chan", ("group", "tm"), None),
        check_vma=False,
    )
```

profile of v0, /device:TPU:0, one launch (start us, length us, event | category | flops | bytes accessed | tf_op | source)
XLA Modules:
  0.0 706.7 jit_solution(326471014404015039)
XLA Ops:
  28.7 17.8 %negate_convert_fusion = (bf16[1024,1024]{1,0:T(8,128)(2,1)}, bf16[1024,1024]{1,0:T(8,128)(2,1)}) fusion(), kind=kLoop, calls=%fused_computation.36 | loop fusion | flops 17825792 | bytes 4194304 | tf_op jit(solution)/shard_map/convert.5
  68.5 605.1 %while.16 = (s32[]{:T(128)}, bf16[2,4,256,128]{3,1,0,2:T(4,128)(2,1)S(1)}, s32[256]{0:T(256)S(1)}, bf16[2,4,1024,256]{2,1,0,3:T(4,128)(2,1)}, s32[128]{0:T(128)S...) while((s32[]{:T(128)}, ...), condition=%wide.region_1.2_spmd.clone, body=%wide.region_0.1_spmd.clone.sunk | while | flops 60588036 | bytes 9790735 | solution.py:65
  68.9 16.8 %cosine_convert_fusion.3 = (bf16[8,1024,128]{2,1,0:T(8,128)(2,1)S(1)}, bf16[8,1024,128]{2,1,0:T(8,128)(2,1)S(1)}) fusion(s32[1024,128]{1,0:T(8,128)S(1)} %add_select_fusion.4, s32[8]{0:T(128)S(1)} %dynamic_slice.27), kind=kLoop, calls=%fused_computation.11.clone.1 | loop fusion | flops 16777216 | bytes 4718624 | tf_op jit(solution)/shard_map/convert
  87.8 16.8 %cosine_convert_fusion.3 = (bf16[8,1024,128]{2,1,0:T(8,128)(2,1)S(1)}, bf16[8,1024,128]{2,1,0:T(8,128)(2,1)S(1)}) fusion(s32[1024,128]{1,0:T(8,128)S(1)} %add_select_fusion.4, s32[8]{0:T(128)S(1)} %dynamic_slice.27), kind=kLoop, calls=%fused_computation.11.clone.1 | loop fusion | flops 16777216 | bytes 4718624 | tf_op jit(solution)/shard_map/convert
  106.7 16.8 %cosine_convert_fusion.3 = (bf16[8,1024,128]{2,1,0:T(8,128)(2,1)S(1)}, bf16[8,1024,128]{2,1,0:T(8,128)(2,1)S(1)}) fusion(s32[1024,128]{1,0:T(8,128)S(1)} %add_select_fusion.4, s32[8]{0:T(128)S(1)} %dynamic_slice.27), kind=kLoop, calls=%fused_computation.11.clone.1 | loop fusion | flops 16777216 | bytes 4718624 | tf_op jit(solution)/shard_map/convert
  125.6 16.8 %cosine_convert_fusion.3 = (bf16[8,1024,128]{2,1,0:T(8,128)(2,1)S(1)}, bf16[8,1024,128]{2,1,0:T(8,128)(2,1)S(1)}) fusion(s32[1024,128]{1,0:T(8,128)S(1)} %add_select_fusion.4, s32[8]{0:T(128)S(1)} %dynamic_slice.27), kind=kLoop, calls=%fused_computation.11.clone.1 | loop fusion | flops 16777216 | bytes 4718624 | tf_op jit(solution)/shard_map/convert
  144.5 16.8 %cosine_convert_fusion.3 = (bf16[8,1024,128]{2,1,0:T(8,128)(2,1)S(1)}, bf16[8,1024,128]{2,1,0:T(8,128)(2,1)S(1)}) fusion(s32[1024,128]{1,0:T(8,128)S(1)} %add_select_fusion.4, s32[8]{0:T(128)S(1)} %dynamic_slice.27), kind=kLoop, calls=%fused_computation.11.clone.1 | loop fusion | flops 16777216 | bytes 4718624 | tf_op jit(solution)/shard_map/convert
  163.5 16.8 %cosine_convert_fusion.3 = (bf16[8,1024,128]{2,1,0:T(8,128)(2,1)S(1)}, bf16[8,1024,128]{2,1,0:T(8,128)(2,1)S(1)}) fusion(s32[1024,128]{1,0:T(8,128)S(1)} %add_select_fusion.4, s32[8]{0:T(128)S(1)} %dynamic_slice.27), kind=kLoop, calls=%fused_computation.11.clone.1 | loop fusion | flops 16777216 | bytes 4718624 | tf_op jit(solution)/shard_map/convert
  182.4 16.8 %cosine_convert_fusion.3 = (bf16[8,1024,128]{2,1,0:T(8,128)(2,1)S(1)}, bf16[8,1024,128]{2,1,0:T(8,128)(2,1)S(1)}) fusion(s32[1024,128]{1,0:T(8,128)S(1)} %add_select_fusion.4, s32[8]{0:T(128)S(1)} %dynamic_slice.27), kind=kLoop, calls=%fused_computation.11.clone.1 | loop fusion | flops 16777216 | bytes 4718624 | tf_op jit(solution)/shard_map/convert
  201.3 16.8 %cosine_convert_fusion.3 = (bf16[8,1024,128]{2,1,0:T(8,128)(2,1)S(1)}, bf16[8,1024,128]{2,1,0:T(8,128)(2,1)S(1)}) fusion(s32[1024,128]{1,0:T(8,128)S(1)} %add_select_fusion.4, s32[8]{0:T(128)S(1)} %dynamic_slice.27), kind=kLoop, calls=%fused_computation.11.clone.1 | loop fusion | flops 16777216 | bytes 4718624 | tf_op jit(solution)/shard_map/convert
  220.2 16.8 %cosine_convert_fusion.3 = (bf16[8,1024,128]{2,1,0:T(8,128)(2,1)S(1)}, bf16[8,1024,128]{2,1,0:T(8,128)(2,1)S(1)}) fusion(s32[1024,128]{1,0:T(8,128)S(1)} %add_select_fusion.4, s32[8]{0:T(128)S(1)} %dynamic_slice.27), kind=kLoop, calls=%fused_computation.11.clone.1 | loop fusion | flops 16777216 | bytes 4718624 | tf_op jit(solution)/shard_map/convert
  239.1 16.8 %cosine_convert_fusion.3 = (bf16[8,1024,128]{2,1,0:T(8,128)(2,1)S(1)}, bf16[8,1024,128]{2,1,0:T(8,128)(2,1)S(1)}) fusion(s32[1024,128]{1,0:T(8,128)S(1)} %add_select_fusion.4, s32[8]{0:T(128)S(1)} %dynamic_slice.27), kind=kLoop, calls=%fused_computation.11.clone.1 | loop fusion | flops 16777216 | bytes 4718624 | tf_op jit(solution)/shard_map/convert
  258.0 16.8 %cosine_convert_fusion.3 = (bf16[8,1024,128]{2,1,0:T(8,128)(2,1)S(1)}, bf16[8,1024,128]{2,1,0:T(8,128)(2,1)S(1)}) fusion(s32[1024,128]{1,0:T(8,128)S(1)} %add_select_fusion.4, s32[8]{0:T(128)S(1)} %dynamic_slice.27), kind=kLoop, calls=%fused_computation.11.clone.1 | loop fusion | flops 16777216 | bytes 4718624 | tf_op jit(solution)/shard_map/convert
  276.9 16.8 %cosine_convert_fusion.3 = (bf16[8,1024,128]{2,1,0:T(8,128)(2,1)S(1)}, bf16[8,1024,128]{2,1,0:T(8,128)(2,1)S(1)}) fusion(s32[1024,128]{1,0:T(8,128)S(1)} %add_select_fusion.4, s32[8]{0:T(128)S(1)} %dynamic_slice.27), kind=kLoop, calls=%fused_computation.11.clone.1 | loop fusion | flops 16777216 | bytes 4718624 | tf_op jit(solution)/shard_map/convert
  295.8 16.8 %cosine_convert_fusion.3 = (bf16[8,1024,128]{2,1,0:T(8,128)(2,1)S(1)}, bf16[8,1024,128]{2,1,0:T(8,128)(2,1)S(1)}) fusion(s32[1024,128]{1,0:T(8,128)S(1)} %add_select_fusion.4, s32[8]{0:T(128)S(1)} %dynamic_slice.27), kind=kLoop, calls=%fused_computation.11.clone.1 | loop fusion | flops 16777216 | bytes 4718624 | tf_op jit(solution)/shard_map/convert
  314.7 16.8 %cosine_convert_fusion.3 = (bf16[8,1024,128]{2,1,0:T(8,128)(2,1)S(1)}, bf16[8,1024,128]{2,1,0:T(8,128)(2,1)S(1)}) fusion(s32[1024,128]{1,0:T(8,128)S(1)} %add_select_fusion.4, s32[8]{0:T(128)S(1)} %dynamic_slice.27), kind=kLoop, calls=%fused_computation.11.clone.1 | loop fusion | flops 16777216 | bytes 4718624 | tf_op jit(solution)/shard_map/convert
  333.6 16.8 %cosine_convert_fusion.3 = (bf16[8,1024,128]{2,1,0:T(8,128)(2,1)S(1)}, bf16[8,1024,128]{2,1,0:T(8,128)(2,1)S(1)}) fusion(s32[1024,128]{1,0:T(8,128)S(1)} %add_select_fusion.4, s32[8]{0:T(128)S(1)} %dynamic_slice.27), kind=kLoop, calls=%fused_computation.11.clone.1 | loop fusion | flops 16777216 | bytes 4718624 | tf_op jit(solution)/shard_map/convert
  352.6 16.8 %cosine_convert_fusion.3 = (bf16[8,1024,128]{2,1,0:T(8,128)(2,1)S(1)}, bf16[8,1024,128]{2,1,0:T(8,128)(2,1)S(1)}) fusion(s32[1024,128]{1,0:T(8,128)S(1)} %add_select_fusion.4, s32[8]{0:T(128)S(1)} %dynamic_slice.27), kind=kLoop, calls=%fused_computation.11.clone.1 | loop fusion | flops 16777216 | bytes 4718624 | tf_op jit(solution)/shard_map/convert
  371.5 16.8 %cosine_convert_fusion.3 = (bf16[8,1024,128]{2,1,0:T(8,128)(2,1)S(1)}, bf16[8,1024,128]{2,1,0:T(8,128)(2,1)S(1)}) fusion(s32[1024,128]{1,0:T(8,128)S(1)} %add_select_fusion.4, s32[8]{0:T(128)S(1)} %dynamic_slice.27), kind=kLoop, calls=%fused_computation.11.clone.1 | loop fusion | flops 16777216 | bytes 4718624 | tf_op jit(solution)/shard_map/convert
  390.4 16.8 %cosine_convert_fusion.3 = (bf16[8,1024,128]{2,1,0:T(8,128)(2,1)S(1)}, bf16[8,1024,128]{2,1,0:T(8,128)(2,1)S(1)}) fusion(s32[1024,128]{1,0:T(8,128)S(1)} %add_select_fusion.4, s32[8]{0:T(128)S(1)} %dynamic_slice.27), kind=kLoop, calls=%fused_computation.11.clone.1 | loop fusion | flops 16777216 | bytes 4718624 | tf_op jit(solution)/shard_map/convert
  409.3 16.8 %cosine_convert_fusion.3 = (bf16[8,1024,128]{2,1,0:T(8,128)(2,1)S(1)}, bf16[8,1024,128]{2,1,0:T(8,128)(2,1)S(1)}) fusion(s32[1024,128]{1,0:T(8,128)S(1)} %add_select_fusion.4, s32[8]{0:T(128)S(1)} %dynamic_slice.27), kind=kLoop, calls=%fused_computation.11.clone.1 | loop fusion | flops 16777216 | bytes 4718624 | tf_op jit(solution)/shard_map/convert
  428.2 16.8 %cosine_convert_fusion.3 = (bf16[8,1024,128]{2,1,0:T(8,128)(2,1)S(1)}, bf16[8,1024,128]{2,1,0:T(8,128)(2,1)S(1)}) fusion(s32[1024,128]{1,0:T(8,128)S(1)} %add_select_fusion.4, s32[8]{0:T(128)S(1)} %dynamic_slice.27), kind=kLoop, calls=%fused_computation.11.clone.1 | loop fusion | flops 16777216 | bytes 4718624 | tf_op jit(solution)/shard_map/convert
  447.1 16.8 %cosine_convert_fusion.3 = (bf16[8,1024,128]{2,1,0:T(8,128)(2,1)S(1)}, bf16[8,1024,128]{2,1,0:T(8,128)(2,1)S(1)}) fusion(s32[1024,128]{1,0:T(8,128)S(1)} %add_select_fusion.4, s32[8]{0:T(128)S(1)} %dynamic_slice.27), kind=kLoop, calls=%fused_computation.11.clone.1 | loop fusion | flops 16777216 | bytes 4718624 | tf_op jit(solution)/shard_map/convert
  466.0 16.8 %cosine_convert_fusion.3 = (bf16[8,1024,128]{2,1,0:T(8,128)(2,1)S(1)}, bf16[8,1024,128]{2,1,0:T(8,128)(2,1)S(1)}) fusion(s32[1024,128]{1,0:T(8,128)S(1)} %add_select_fusion.4, s32[8]{0:T(128)S(1)} %dynamic_slice.27), kind=kLoop, calls=%fused_computation.11.clone.1 | loop fusion | flops 16777216 | bytes 4718624 | tf_op jit(solution)/shard_map/convert
  (203 shorter events, 316.6 us)
Async XLA Ops:
  7.9 5.0 copy-start
  7.9 5.1 copy-start.2
  7.9 5.1 copy-start.1
  7.9 53.9 %all-to-all-start = ((bf16[2,4,256,1024]{2,1,0,3:T(4,128)(2,1)}), bf16[2,4,256,1024]{2,1,0,3:T(4,128)(2,1)}, u32[]{:S(2)}, u32[]{:S(2)}) async-start(bf16[2,4,256,1024]{2,1,0,3:T(4,128)(2,1)} %copy.12), calls=%async_computation | async-start | bytes 8388608 | tf_op jit(solution)/shard_map/all_to_all | solution.py:90
  674.9 12.3 %all-to-all-start.1 = ((bf16[2,4,256,128]{2,1,0,3:T(4,128)(2,1)}), bf16[2,4,256,128]{2,1,0,3:T(4,128)(2,1)S(1)}, u32[]{:S(2)}, u32[]{:S(2)}) async-start(bf16[2,4,256,128]{2,1,0,3:T(4,128)(2,1)} %copy.14), calls=%async_computation.1 | async-start | bytes 1048576 | tf_op jit(solution)/shard_map/all_to_all | solution.py:93
  692.4 12.3 %collective-permute-start = (bf16[3,32,2048]{2,1,0:T(8,128)(2,1)S(1)}, bf16[3,32,2048]{2,1,0:T(8,128)(2,1)S(1)}, u32[]{:S(2)}, u32[]{:S(2)}) collective-permute-start(bf16[3,32,2048]{2,1,0:T(8,128)(2,1)S(1)} %slice.101), channel_id=1, source_target_pairs={{0,1},{1,2},{2,3},{4,5},{5,6},{6,7},{8,9},{9,10},{10,11},{12,13},{... | collective-permute-start | bytes 1179656 | tf_op jit(solution)/shard_map/ppermute | solution.py:18
where the time goes:
time: 708 us; the launch traced here: 707 us
  other arithmetic  591 us (83%)
  matrix products  54.3 us (8%)
  waiting for transfers between devices  25.5 us (4%)
  local copies, waits for them, and re-layouts  20.9 us (3%)
  starting transfers between devices  12.9 us (2%)
    another operation x34, other arithmetic  573 us
    dot_general x32, matrix products, one_block(): jnp.einsum('stfc,cfk->stck', slab, weights, preferred_element_type=jnp.fl...  50 us
    all_to_all x1, waiting for transfers between devices, on_device(): lax.all_to_all(voltages, 'chan', split_axis=3, concat_axis=2, tiled=True)  15.3 us
  transfers between devices with their start and end apart: 3, of which 3 were waited for; matrix products, arithmetic and copies ran while one was open for 6% of the time, Pallas kernels for 0%

commit v1 on v0

v1 whole, which is shorter than its diff:
```python
import math

import jax
import jax.numpy as jnp
from jax import lax
from jax.experimental import pallas as pl
from jax.experimental.pallas import tpu as pltpu
from jax.sharding import PartitionSpec as P

PHASES = 4096
LANES = 128
HALF = 32


def turn(phase, steps):
    quarter = steps // 4
    quadrant = (phase + quarter // 2) // quarter
    rest = (phase - quadrant * quarter).astype(jnp.float32) * (2.0 * math.pi / steps)
    square = rest * rest
    sine = rest * (1.0 + square * (-1.6666666e-1 + square * (8.3333310e-3 + square * (-1.9840874e-4 + square * 2.7525562e-6))))
    cosine = 1.0 + square * (-0.5 + square * (4.1666666e-2 + square * (-1.3888889e-3 + square * (2.4801587e-5 - square * 2.7557319e-7))))
    odd = (quadrant & 1) == 1
    real = jnp.where(odd, sine, cosine)
    imag = jnp.where(odd, cosine, sine)
    real = jnp.where(((quadrant + 1) & 2) == 2, -real, real)
    imag = jnp.where((quadrant & 2) == 2, -imag, imag)
    return real, imag


def times(a, b):
    return a[0] * b[0] - a[1] * b[1], a[0] * b[1] + a[1] * b[0]


def beam_kernel(position, steering, voltages, keep, send, delays, centre_tables, offset_tables, rows, turned_rows, sums):
    feeds, beams = delays.shape
    frames = voltages.shape[1]
    stride = 2 * frames
    block = voltages.shape[3]
    devices = 2 * keep.shape[0]
    own_beams = beams // devices
    centres = centre_tables.shape[1]
    step = pl.program_id(0)
    here = lax.axis_index("chan")

    @pl.when(step == 0)
    def _():
        def column(axis):
            first = here * feeds if position.shape[1] > feeds else 0
            row = position[axis : axis + 1, pl.ds(pl.multiple_of(first, LANES), feeds)].astype(jnp.float32)
            return jnp.transpose(jnp.broadcast_to(row, (beams, feeds))).astype(jnp.int32)

        total = column(0) * steering[0:1, :] + column(1) * steering[1:2, :]
        delays[...] = total & (PHASES - 1)

        def one_slab(index, carry):
            at = pl.multiple_of(index * 16, 16)
            delay = delays[pl.ds(at, 16), :]
            half_step = turn(delay, 2 * PHASES)
            state = half_step
            advance = times(half_step, half_step)
            for offset in range(HALF):
                offset_tables[0, offset, pl.ds(at, 16), :] = state[0].astype(jnp.bfloat16)
                offset_tables[1, offset, pl.ds(at, 16), :] = state[1].astype(jnp.bfloat16)
                if offset + 1 < HALF:
                    state = times(state, advance)
            state = turn(((2 * HALF - 1) * delay) & (2 * PHASES - 1), 2 * PHASES)
            advance = turn((4 * HALF * delay) & (2 * PHASES - 1), 2 * PHASES)
            for centre in range(centres):
                centre_tables[0, centre, pl.ds(at, 16), :] = state[0].astype(jnp.bfloat16)
                centre_tables[1, centre, pl.ds(at, 16), :] = state[1].astype(jnp.bfloat16)
                centre_tables[2, centre, pl.ds(at, 16), :] = (-state[1]).astype(jnp.bfloat16)
                if centre + 1 < centres:
                    state = times(state, advance)
            return carry

        lax.fori_loop(0, feeds // 16, one_slab, 0)

    width = min(feeds, LANES)
    for part in range(2):
        for frame in range(frames):
            slot = part * frames + frame
            other = (1 - part) * frames + frame
            for at in range(feeds // width):
                piece = voltages[part, frame, at * width : (at + 1) * width, :].astype(jnp.float32)
                if width < LANES:
                    piece = jnp.concatenate([piece, jnp.zeros((LANES - width, block), jnp.float32)], axis=0)
                piece = jnp.transpose(piece)
                rows[at, pl.ds(slot, block, stride=stride), :] = piece
                turned_rows[at, pl.ds(other, block, stride=stride), :] = piece if part == 0 else -piece

    def lhs(scratch, upper, lower):
        pieces = []
        for at in range(feeds // width):
            top = scratch[at, pl.ds(pl.multiple_of(upper * stride, stride), stride), :]
            bottom = scratch[at, pl.ds(pl.multiple_of(lower * stride, stride), stride), :]
            pieces.append(jnp.concatenate([top, bottom], axis=0))
        return jnp.concatenate(pieces, axis=1).astype(jnp.bfloat16)[:, :feeds]

    def one_pair(index, carry):
        local = index // HALF
        offset = index % HALF
        centre = step * (block // (2 * HALF)) + local
        upper = local * 2 * HALF + HALF + offset
        lower = local * 2 * HALF + HALF - 1 - offset
        cosine = centre_tables[0, centre]
        sine = centre_tables[1, centre]
        minus = centre_tables[2, centre]
        small_cosine = offset_tables[0, offset]
        small_sine = offset_tables[1, offset]
        first = jnp.concatenate([cosine * small_cosine, minus * small_sine], axis=1)
        second = jnp.concatenate([sine * small_cosine, cosine * small_sine], axis=1)
        total = jnp.dot(lhs(rows, upper, lower), first, preferred_element_type=jnp.float32)
        total = total + jnp.dot(lhs(turned_rows, upper, lower), second, preferred_element_type=jnp.float32)
        sums[pl.ds(pl.multiple_of(upper * stride, stride), stride), :] = total[:stride, :beams] + total[:stride, beams:]
        sums[pl.ds(pl.multiple_of(lower * stride, stride), stride), :] = total[stride:, :beams] - total[stride:, beams:]
        return carry

    lax.fori_loop(0, block // 2, one_pair, 0, unroll=2)

    scale = 1.0 / math.sqrt(feeds * devices)
    for part in range(2):
        for frame in range(frames):
            slot = part * frames + frame
            piece = jnp.transpose(sums[pl.ds(slot, block, stride=stride), :] * scale)
            for target in range(devices):
                value = piece[target * own_beams : (target + 1) * own_beams, :].astype(jnp.bfloat16)
                relative = target ^ here

                @pl.when(relative % 2 == 0)
                def _():
                    keep[relative // 2, frame, part] = value

                @pl.when(relative % 2 == 1)
                def _():
                    send[relative // 2, frame, part] = value


def beamform(voltages, position, steering, devices):
    _, frames, feeds, channels = voltages.shape
    beams = steering.shape[1]
    block = LANES
    width = min(feeds, LANES)
    shape = jax.ShapeDtypeStruct((devices // 2, frames, 2, beams // devices, channels), jnp.bfloat16)
    spec = pl.BlockSpec((devices // 2, frames, 2, beams // devices, block), lambda i: (0, 0, 0, 0, i))
    return pl.pallas_call(
        beam_kernel,
        grid=(channels // block,),
        in_specs=[
            pl.BlockSpec(position.shape, lambda i: (0, 0)),
            pl.BlockSpec(steering.shape, lambda i: (0, 0)),
            pl.BlockSpec((2, frames, feeds, block), lambda i: (0, 0, 0, i)),
        ],
        out_specs=[spec, spec],
        out_shape=[shape, shape],
        scratch_shapes=[
            pltpu.VMEM((feeds, beams), jnp.int32),
            pltpu.VMEM((3, channels // (2 * HALF), feeds, beams), jnp.bfloat16),
            pltpu.VMEM((2, HALF, feeds, beams), jnp.bfloat16),
            pltpu.VMEM((feeds // width, block * 2 * frames, LANES), jnp.float32),
            pltpu.VMEM((feeds // width, block * 2 * frames, LANES), jnp.float32),
            pltpu.VMEM((block * 2 * frames, beams), jnp.float32),
        ],
        compiler_params=pltpu.CompilerParams(vmem_limit_bytes=48 * 2**20),
        name="beam",
    )(position, steering, voltages)


def synth_kernel(own, halo, taps, out, basis_real, basis_imag, small):
    frames, _, beams, channels = own.shape
    before = halo.shape[0]
    width = out.shape[3]
    first = pl.program_id(0) * width
    group = small.shape[1]

    def phases(rows, factor):
        row = lax.broadcasted_iota(jnp.int32, (rows, width), 0) * factor
        column = first + lax.broadcasted_iota(jnp.int32, (rows, width), 1)
        return (row * column) & (channels - 1)

    real, imag = turn(phases(group, 1), channels)
    small[0] = real
    small[1] = imag
    count = channels // group
    large = turn(phases(count, group), channels)
    for index in range(count):
        a = (large[0][index : index + 1], large[1][index : index + 1])
        value = times(a, (small[0], small[1]))
        basis_real[index * group : (index + 1) * group, :] = value[0].astype(jnp.bfloat16)
        basis_imag[index * group : (index + 1) * group, :] = value[1].astype(jnp.bfloat16)

    def gather(part):
        pieces = [halo[t, part] for t in range(before)] + [own[t, part] for t in range(frames)]
        return jnp.concatenate(pieces, axis=0)

    beams_real = gather(0)
    beams_imag = gather(1)

    def dot(a, b):
        return jnp.dot(a, b[...], preferred_element_type=jnp.float32)

    scale = 1.0 / math.sqrt(channels)
    total_real = (dot(beams_real, basis_real) - dot(beams_imag, basis_imag)) * scale
    total_imag = (dot(beams_real, basis_imag) + dot(beams_imag, basis_real)) * scale
    count_taps = taps.shape[0]
    for part, total in enumerate((total_real, total_imag)):
        rounded = total.astype(jnp.bfloat16).astype(jnp.float32)
        for t in range(frames):
            value = jnp.zeros((beams, width), jnp.float32)
            for k in range(count_taps):
                at = before + t - k
                value = value + taps[k : k + 1, :] * rounded[at * beams : (at + 1) * beams]
            out[part, t] = value.astype(jnp.bfloat16)


def synthesize(own, halo, taps):
    frames, _, beams, channels = own.shape
    width = min(256, channels)
    return pl.pallas_call(
        synth_kernel,
        grid=(channels // width,),
        in_specs=[
            pl.BlockSpec(own.shape, lambda i: (0, 0, 0, 0)),
            pl.BlockSpec(halo.shape, lambda i: (0, 0, 0, 0)),
            pl.BlockSpec((taps.shape[0], width), lambda i: (0, i)),
        ],
        out_specs=pl.BlockSpec((2, frames, beams, width), lambda i: (0, 0, 0, i)),
        out_shape=jax.ShapeDtypeStruct((2, frames, beams, channels), jnp.bfloat16),
        scratch_shapes=[
            pltpu.VMEM((channels, width), jnp.bfloat16),
            pltpu.VMEM((channels, width), jnp.bfloat16),
            pltpu.VMEM((2, 32, width), jnp.float32),
        ],
        compiler_params=pltpu.CompilerParams(vmem_limit_bytes=48 * 2**20),
        name="synth",
    )(own, halo, taps)


def added(*terms):
    return sum(term.astype(jnp.float32) for term in terms).astype(jnp.bfloat16)


def on_device(voltages, feed_position, beam_steering, synthesis_taps):
    devices = lax.axis_size("chan")
    steps = lax.axis_size("tm")
    taps = synthesis_taps.shape[0]
    feeds = voltages.shape[2]
    position = feed_position.T
    if feeds % LANES:
        position = lax.dynamic_slice_in_dim(position, lax.axis_index("chan") * feeds, feeds, 1)
    keep, send = beamform(voltages, position, beam_steering.T, devices)
    mask = 1
    while True:
        arrived = lax.ppermute(send, "chan", [(i, i ^ mask) for i in range(devices)])
        mask *= 2
        if mask == devices:
            break
        send = added(keep[1::2], arrived[1::2])
        keep = added(keep[0::2], arrived[0::2])
    own = added(keep[0], arrived[0])
    halo = lax.ppermute(own[own.shape[0] - (taps - 1) :], "tm", [(i, i + 1) for i in range(steps - 1)])
    out = synthesize(own, halo, synthesis_taps)
    return jnp.transpose(out, (0, 2, 1, 3))


def solution(mesh):
    return jax.shard_map(
        on_device,
        mesh=mesh,
        in_specs=(P(None, ("group", "tm"), "chan", None), P(), P("group", None), P()),
        out_specs=P(None, "chan", ("group", "tm"), None),
        check_vma=False,
    )
```

time: 708 us -> 107 us (0.15)
  other arithmetic: 591 us -> 0.46 us
  Pallas kernels: 0 us -> 74.2 us
  matrix products: 54.3 us -> 0 us
  local copies, waits for them, and re-layouts: 20.9 us -> 2.61 us
    another operation x35 -> x0, other arithmetic: 579 us -> none
    pallas_call x0 -> x2, Pallas kernels: none -> 74.2 us  [the longest x1 70.8 us: beamform(): pl.pallas_call(beam_kernel, grid=(channels // block,), in_specs=[pl.Block...]
    dot_general x33 -> x0, matrix products: 54.3 us -> none  [the longest x32 50 us: one_block(): jnp.einsum('stfc,cfk->stck', slab, weights, preferred_element_type=jnp.fl...]
    all_to_all x2 -> x0, waiting for transfers between devices: 17.5 us -> none  [the longest x1 15.3 us: on_device(): lax.all_to_all(voltages, 'chan', split_axis=3, concat_axis=2, tiled=True)]
    ppermute x1 -> x3, waiting for transfers between devices: 7.99 us -> 22.4 us  [the longest x2 14.6 us: on_device(): lax.ppermute(send, 'chan', [(i, i ^ mask) for i in range(devices)])]
    select_n x32 -> x0, other arithmetic: 10.9 us -> none  [compute_delays(): return (first + second) % PHASES]
    all_to_all x2 -> x0, starting transfers between devices: 8.64 us -> none  [the longest x1 4.99 us: on_device(): lax.all_to_all(voltages, 'chan', split_axis=3, concat_axis=2, tiled=True)]
    all_to_all x4 -> x0, local copies, waits for them, and re-layouts: 7.44 us -> none  [the longest x1 6.56 us: on_device(): lax.all_to_all(voltages, 'chan', split_axis=3, concat_axis=2, tiled=True)]
  transfers between devices with their start and end apart: 3 -> 3, of which waited for: 3 -> 3; matrix products, arithmetic and copies ran while one was open for 6% -> 0% of each run, Pallas kernels for 0% -> 0%
where the time goes in v1:
time: 107 us
  Pallas kernels  74.2 us (69%)
  waiting for transfers between devices  22.4 us (21%)
  starting transfers between devices  7.1 us (7%)
  local copies, waits for them, and re-layouts  2.61 us (2%)
    pallas_call x1, Pallas kernels, beamform(): pl.pallas_call(beam_kernel, grid=(channels // block,), in_specs=[pl.Block...  70.8 us
    ppermute x2, waiting for transfers between devices, on_device(): lax.ppermute(send, 'chan', [(i, i ^ mask) for i in range(devices)])  14.6 us
    ppermute x1, waiting for transfers between devices, on_device(): lax.ppermute(own[own.shape[0] - (taps - 1):], 'tm', [(i, i + 1) for i in...  7.78 us
    ppermute x1, starting transfers between devices, on_device(): lax.ppermute(own[own.shape[0] - (taps - 1):], 'tm', [(i, i + 1) for i in...  3.75 us
    pallas_call x1, Pallas kernels, synthesize(): pl.pallas_call(synth_kernel, grid=(channels // width,), in_specs=[pl.Bloc...  3.41 us
    ppermute x2, starting transfers between devices, on_device(): lax.ppermute(send, 'chan', [(i, i ^ mask) for i in range(devices)])  3.34 us
  transfers between devices with their start and end apart: 3, of which 3 were waited for; matrix products, arithmetic and copies ran while one was open for 0% of the time, Pallas kernels for 0%

profile of v1, /device:TPU:0, one launch (start us, length us, event | category | flops | bytes accessed | tf_op | source)
XLA Modules:
  0.0 106.9 jit_solution(16665611377369935052)
XLA Ops:
  0.0 0.0 copy-start.1
  0.0 0.7 copy-done.1
  0.7 0.0 copy-start.2
  0.7 0.7 copy-done.2
  1.4 0.0 copy-start
  1.4 70.8 %beam.1 = (bf16[2,4,2,32,1024]{4,3,2,1,0:T(8,128)(2,1)S(1)}, bf16[2,4,2,32,1024]{4,3,2,1,0:T(8,128)(2,1)S(1)}) custom-call(s32[2,1024]{1,0:T(2,128)S(1)} %bitcast.8, s32[2,128]{1,0:T(2,128)S(1)} %bitcast.9, bf16[2,4,256,1024]{3,2,1,0:T(8,128)(2,1)} %voltages.1), custom_call_target="tpu_custom_call" | custom-call | tf_op jit(solution)/shard_map/beam/pallas_call | solution.py:145
  72.2 0.3 collective-permute-start
  72.5 2.4 %collective-permute-done = bf16[2,4,2,32,1024]{4,3,2,1,0:T(8,128)(2,1)S(1)} collective-permute-done((bf16[2,4,2,32,1024]{4,3,2,1,0:T(8,128)(2,1)S(1)}, bf16[2,4,2,32,1024]{4,3,2,1,0:T(8,128)(2,1)S(1)}, u32[]{:S(2)}, u32[]{:S(2)}) %collective-permute-start) | collective-permute-done | bytes 1048608 | tf_op jit(solution)/shard_map/ppermute | solution.py:253
  74.9 0.2 add_convert_fusion.1
  75.1 3.0 %collective-permute-start.1 = (bf16[1,4,2,32,1024]{4,3,2,1,0:T(8,128)(2,1)S(1)}, bf16[1,4,2,32,1024]{4,3,2,1,0:T(8,128)(2,1)S(1)}, u32[]{:S(2)}, u32[]{:S(2)}) collective-permute-start(bf16[1,4,2,32,1024]{4,3,2,1,0:T(8,128)(2,1)S(1)} %add_convert_fusion.1), channel_id=1, source_target_pairs={{0,8},{4,12},{8,0},{12,4},{1,9},{5,13},{9,1},{13,5},{2,10},{6,14},... | collective-permute-start | bytes 1572872 | tf_op jit(solution)/shard_map/ppermute | solution.py:253
  78.2 12.2 %collective-permute-done.1 = bf16[1,4,2,32,1024]{4,3,2,1,0:T(8,128)(2,1)S(1)} collective-permute-done((bf16[1,4,2,32,1024]{4,3,2,1,0:T(8,128)(2,1)S(1)}, bf16[1,4,2,32,1024]{4,3,2,1,0:T(8,128)(2,1)S(1)}, u32[]{:S(2)}, u32[]{:S(2)}) %collective-permute-start.1) | collective-permute-done | bytes 524320 | tf_op jit(solution)/shard_map/ppermute | solution.py:253
  90.4 0.3 add_convert_fusion
  90.7 3.8 %collective-permute-start.2 = (bf16[3,2,32,1024]{3,2,1,0:T(8,128)(2,1)S(1)}, bf16[3,2,32,1024]{3,2,1,0:T(8,128)(2,1)S(1)}, u32[]{:S(2)}, u32[]{:S(2)}) collective-permute-start(bf16[3,2,32,1024]{3,2,1,0:T(8,128)(2,1)S(1)} %slice_bitcast_fusion), channel_id=1, source_target_pairs={{0,1},{1,2},{2,3},{4,5},{5,6},{6,7},{8,9},{9,10},{10,11},{12,13},{... | collective-permute-start | bytes 1179656 | tf_op jit(solution)/shard_map/ppermute | solution.py:260
  94.5 7.8 %collective-permute-done.2.halo = bf16[3,2,32,1024]{3,2,1,0:T(8,128)(2,1)S(1)} collective-permute-done((bf16[3,2,32,1024]{3,2,1,0:T(8,128)(2,1)S(1)}, bf16[3,2,32,1024]{3,2,1,0:T(8,128)(2,1)S(1)}, u32[]{:S(2)}, u32[]{:S(2)}) %collective-permute-start.2) | collective-permute-done | bytes 393248 | tf_op jit(solution)/shard_map/ppermute | solution.py:260
  102.3 0.0 copy-done
  102.3 3.4 %synth.1 = bf16[2,4,32,1024]{3,2,1,0:T(8,128)(2,1)S(1)} custom-call(bf16[4,2,32,1024]{3,2,1,0:T(8,128)(2,1)S(1)} %bitcast.6, bf16[3,2,32,1024]{3,2,1,0:T(8,128)(2,1)S(1)} %collective-permute-done.2.halo, f32[4,1024]{1,0:T(4,128)S(1)} %copy-done), custom_call_target="tpu_custom_call" | custom-call | tf_op jit(solution)/shard_map/synth/pallas_call | solution.py:218
  105.7 1.2 %copy.5 = bf16[2,32,4,1024]{3,2,1,0:T(4,128)(2,1)} copy(bf16[2,32,4,1024]{3,1,2,0:T(8,128)(2,1)S(1)} %bitcast.7) | data formatting | bytes 1048576 | tf_op jit(solution)/shard_map/transpose | solution.py:262
  (1 shorter events, 0.0 us)
Async XLA Ops:
  0.0 0.7 copy-start.1
  0.7 0.7 copy-start.2
  1.4 100.9 %copy-start = (f32[4,1024]{1,0:T(4,128)S(1)}, f32[4,1024]{1,0:T(4,128)}, u32[]{:S(2)}) copy-start(f32[4,1024]{1,0:T(4,128)} %taps.1) | copy-start | bytes 49156
  72.2 2.7 %collective-permute-start = (bf16[2,4,2,32,1024]{4,3,2,1,0:T(8,128)(2,1)S(1)}, bf16[2,4,2,32,1024]{4,3,2,1,0:T(8,128)(2,1)S(1)}, u32[]{:S(2)}, u32[]{:S(2)}) collective-permute-start(bf16[2,4,2,32,1024]{4,3,2,1,0:T(8,128)(2,1)S(1)} %get-tuple-element.8), channel_id=1, source_target_pairs={{0,4},{4,0},{8,12},{12,8},{1,5},{5,1},{9,13},{13,9},{2,6},{6,2},{1... | collective-permute-start | bytes 3145736 | tf_op jit(solution)/shard_map/ppermute | solution.py:253
  75.1 15.3 %collective-permute-start.1 = (bf16[1,4,2,32,1024]{4,3,2,1,0:T(8,128)(2,1)S(1)}, bf16[1,4,2,32,1024]{4,3,2,1,0:T(8,128)(2,1)S(1)}, u32[]{:S(2)}, u32[]{:S(2)}) collective-permute-start(bf16[1,4,2,32,1024]{4,3,2,1,0:T(8,128)(2,1)S(1)} %add_convert_fusion.1), channel_id=1, source_target_pairs={{0,8},{4,12},{8,0},{12,4},{1,9},{5,13},{9,1},{13,5},{2,10},{6,14},... | collective-permute-start | bytes 1572872 | tf_op jit(solution)/shard_map/ppermute | solution.py:253
  90.7 11.5 %collective-permute-start.2 = (bf16[3,2,32,1024]{3,2,1,0:T(8,128)(2,1)S(1)}, bf16[3,2,32,1024]{3,2,1,0:T(8,128)(2,1)S(1)}, u32[]{:S(2)}, u32[]{:S(2)}) collective-permute-start(bf16[3,2,32,1024]{3,2,1,0:T(8,128)(2,1)S(1)} %slice_bitcast_fusion), channel_id=1, source_target_pairs={{0,1},{1,2},{2,3},{4,5},{5,6},{6,7},{8,9},{9,10},{10,11},{12,13},{... | collective-permute-start | bytes 1179656 | tf_op jit(solution)/shard_map/ppermute | solution.py:260

commit v2 on v1

v2 whole, which is shorter than its diff:
```python
import functools
import math

import jax
import jax.numpy as jnp
from jax import lax
from jax.experimental import pallas as pl
from jax.experimental.pallas import tpu as pltpu
from jax.sharding import PartitionSpec as P

PHASES = 4096
LANES = 128
HALF = 32
SLAB = 16
TABLE = jnp.float32


def turn(phase, steps):
    quarter = steps // 4
    shift = quarter.bit_length() - 1
    quadrant = lax.shift_right_logical(phase + quarter // 2, shift)
    rest = (phase - lax.shift_left(quadrant, shift)).astype(jnp.float32) * (2.0 * math.pi / steps)
    square = rest * rest
    sine = rest * (1.0 + square * (-1.6666666e-1 + square * (8.3333310e-3 + square * (-1.9840874e-4 + square * 2.7525562e-6))))
    cosine = 1.0 + square * (-0.5 + square * (4.1666666e-2 + square * (-1.3888889e-3 + square * (2.4801587e-5 - square * 2.7557319e-7))))
    odd = (quadrant & 1) == 1
    real = jnp.where(odd, sine, cosine)
    imag = jnp.where(odd, cosine, sine)
    real = jnp.where(((quadrant + 1) & 2) == 2, -real, real)
    imag = jnp.where((quadrant & 2) == 2, -imag, imag)
    return real, imag


def times(a, b):
    return a[0] * b[0] - a[1] * b[1], a[0] * b[1] + a[1] * b[0]


def beam_kernel(first, position, steering, voltages, keep, send, staged, arrivals, centre_tables, offset_tables, rows_even, rows_odd, sums_even, sums_odd):
    feeds, beams = offset_tables.shape[2:]
    frames = voltages.shape[1]
    stride = 2 * frames
    block = rows_even.shape[1] // stride
    devices = 2 * keep.shape[0]
    own_beams = beams // devices
    centres = centre_tables.shape[1]
    blocks = staged.shape[0]
    here = lax.axis_index("chan")
    rows_of = (rows_even, rows_odd)
    sums_of = (sums_even, sums_odd)

    def arrival(index):
        source = voltages.at[:, :, :, pl.ds(first + index * block, block)]
        return pltpu.make_async_copy(source, staged.at[index], arrivals.at[index])

    for index in range(blocks):
        arrival(index).start()

    def column(axis):
        start = here * feeds if position.shape[1] > feeds else 0
        row = position[axis : axis + 1, pl.ds(pl.multiple_of(start, LANES), feeds)].astype(jnp.float32)
        return jnp.transpose(jnp.broadcast_to(row, (beams, feeds))).astype(jnp.int32)

    lane = lax.broadcasted_iota(jnp.int32, steering.shape, 1)
    aim = steering[...]
    size = own_beams
    while size < beams:
        upper = (lane & size) != 0
        swapped = jnp.where(upper, pltpu.roll(aim, size, 1), pltpu.roll(aim, beams - size, 1))
        aim = jnp.where((here & (size // own_beams)) != 0, swapped, aim)
        size *= 2
    total = column(0) * aim[0:1, :] + column(1) * aim[1:2, :]
    offset_tables[0, 0] = (total & (PHASES - 1)).astype(TABLE)

    def one_slab(index, carry):
        at = pl.multiple_of(index * SLAB, SLAB)
        delay = offset_tables[0, 0, pl.ds(at, SLAB), :].astype(jnp.int32)
        half_step = turn(delay, 2 * PHASES)
        state = half_step
        advance = times(half_step, half_step)
        for offset in range(HALF):
            offset_tables[0, offset, pl.ds(at, SLAB), :] = state[0].astype(TABLE)
            offset_tables[1, offset, pl.ds(at, SLAB), :] = state[1].astype(TABLE)
            if offset + 1 < HALF:
                state = times(state, advance)
        state = turn(((2 * first + 2 * HALF - 1) * delay) & (2 * PHASES - 1), 2 * PHASES)
        advance = turn((4 * HALF * delay) & (2 * PHASES - 1), 2 * PHASES)
        for centre in range(centres):
            centre_tables[0, centre, pl.ds(at, SLAB), :] = state[0].astype(TABLE)
            centre_tables[1, centre, pl.ds(at, SLAB), :] = state[1].astype(TABLE)
            if centre + 1 < centres:
                state = times(state, advance)
        return carry

    lax.fori_loop(0, feeds // SLAB, one_slab, 0)
    for index in range(blocks):
        arrival(index).wait()

    width = min(feeds, LANES)
    scale = 1.0 / math.sqrt(feeds * devices)
    sign = jnp.where(lax.broadcasted_iota(jnp.int32, (stride, beams), 0) < frames, -1.0, 1.0)

    def take(index, rows, slot):
        for at in range(feeds // width):
            piece = staged[index, slot // frames, slot % frames, at * width : (at + 1) * width, :].astype(jnp.float32)
            if width < LANES:
                piece = jnp.concatenate([piece, jnp.zeros((LANES - width, block), jnp.float32)], axis=0)
            rows[at, pl.ds(slot, block, stride=stride), :] = jnp.transpose(piece)

    def give(index, sums, slot):
        piece = jnp.transpose(sums[pl.ds(slot, block, stride=stride), :] * scale)
        for relative in range(devices):
            value = piece[relative * own_beams : (relative + 1) * own_beams, :].astype(jnp.bfloat16)
            out = send if relative % 2 else keep
            out[relative // 2, slot % frames, slot // frames, :, pl.ds(pl.multiple_of(index * block, block), block)] = value

    def quarter_turn(value):
        return pltpu.roll(value, frames, 0) * sign

    def dot(a, b):
        return jnp.dot(a, b, preferred_element_type=jnp.float32)

    def pair(rows, sums, cosine, sine, local, offset):
        upper = local * 2 * HALF + HALF + offset
        lower = local * 2 * HALF + HALF - 1 - offset
        pieces = []
        for at in range(feeds // width):
            top = rows[at, upper * stride : (upper + 1) * stride, :]
            bottom = rows[at, lower * stride : (lower + 1) * stride, :]
            pieces.append(jnp.concatenate([top, bottom], axis=0))
        left = jnp.concatenate(pieces, axis=1).astype(jnp.bfloat16)[:, :feeds]
        small_cosine = offset_tables[0, offset].astype(jnp.bfloat16)
        small_sine = offset_tables[1, offset].astype(jnp.bfloat16)
        straight = dot(left, jnp.concatenate([cosine * small_cosine, sine * small_sine], axis=1))
        crossed = dot(left, jnp.concatenate([sine * small_cosine, cosine * small_sine], axis=1))
        a, b, c, d = straight[:, :beams], straight[:, beams:], crossed[:, :beams], crossed[:, beams:]
        more = quarter_turn(c[:stride] + d[:stride])
        less = quarter_turn(c[stride:] - d[stride:])
        sums[upper * stride : (upper + 1) * stride, :] = a[:stride] - b[:stride] + more
        sums[lower * stride : (lower + 1) * stride, :] = a[stride:] + b[stride:] + less

    def one_block(index, parity):
        rows, sums = rows_of[parity], sums_of[parity]
        every = HALF * (block // (2 * HALF)) // stride
        for local in range(block // (2 * HALF)):
            centre = index * (block // (2 * HALF)) + local
            cosine = centre_tables[0, centre].astype(jnp.bfloat16)
            sine = centre_tables[1, centre].astype(jnp.bfloat16)
            for offset in range(HALF):
                count = local * HALF + offset
                if count % every == 0:
                    give(jnp.maximum(index - 1, 0), sums_of[1 - parity], count // every)
                    take(jnp.minimum(index + 1, blocks - 1), rows_of[1 - parity], count // every)
                pair(rows, sums, cosine, sine, local, offset)

    for slot in range(stride):
        take(0, rows_even, slot)

    def two_blocks(index, carry):
        one_block(2 * index, 0)
        one_block(2 * index + 1, 1)
        return carry

    lax.fori_loop(0, blocks // 2, two_blocks, 0)
    for slot in range(stride):
        give(blocks - 1, sums_odd, slot)


def beamform(voltages, position, steering, devices, first, count):
    _, frames, feeds, _ = voltages.shape
    beams = steering.shape[1]
    width = min(feeds, LANES)
    shape = jax.ShapeDtypeStruct((devices // 2, frames, 2, beams // devices, count), jnp.bfloat16)
    rows = pltpu.VMEM((feeds // width, LANES * 2 * frames, LANES), jnp.float32)
    sums = pltpu.VMEM((LANES * 2 * frames, beams), jnp.float32)
    work = 2 * frames * 2 * feeds * beams * count
    whole = pl.BlockSpec(memory_space=pltpu.VMEM)
    return pl.pallas_call(
        functools.partial(beam_kernel, first),
        in_specs=[whole, whole, pl.BlockSpec(memory_space=pl.ANY)],
        out_specs=[whole, whole],
        out_shape=[shape, shape],
        scratch_shapes=[
            pltpu.VMEM((count // LANES, 2, frames, feeds, LANES), jnp.bfloat16),
            pltpu.SemaphoreType.DMA((count // LANES,)),
            pltpu.VMEM((2, count // (2 * HALF), feeds, beams), TABLE),
            pltpu.VMEM((2, HALF, feeds, beams), TABLE),
            rows,
            rows,
            sums,
            sums,
        ],
        compiler_params=pltpu.CompilerParams(vmem_limit_bytes=48 * 2**20),
        cost_estimate=pl.CostEstimate(flops=32 * work, bytes_accessed=4 * 2 * frames * feeds * count, transcendentals=0),
        name="beam",
    )(position, steering, voltages)


def synth_kernel(own, halo, taps, out, basis_real, basis_imag, small):
    frames, _, beams, channels = own.shape
    before = halo.shape[0]
    width = out.shape[3]
    first = pl.program_id(0) * width
    group = small.shape[1]

    def phases(rows, factor):
        row = lax.broadcasted_iota(jnp.int32, (rows, width), 0) * factor
        column = first + lax.broadcasted_iota(jnp.int32, (rows, width), 1)
        return (row * column) & (channels - 1)

    real, imag = turn(phases(group, 1), channels)
    small[0] = real
    small[1] = imag
    count = channels // group
    large = turn(phases(count, group), channels)
    for index in range(count):
        a = (large[0][index : index + 1], large[1][index : index + 1])
        value = times(a, (small[0], small[1]))
        basis_real[index * group : (index + 1) * group, :] = value[0].astype(jnp.bfloat16)
        basis_imag[index * group : (index + 1) * group, :] = value[1].astype(jnp.bfloat16)

    def gather(part):
        pieces = [halo[t, part] for t in range(before)] + [own[t, part] for t in range(frames)]
        return jnp.concatenate(pieces, axis=0)

    beams_real = gather(0)
    beams_imag = gather(1)

    def dot(a, b):
        return jnp.dot(a, b[...], preferred_element_type=jnp.float32)

    scale = 1.0 / math.sqrt(channels)
    total_real = (dot(beams_real, basis_real) - dot(beams_imag, basis_imag)) * scale
    total_imag = (dot(beams_real, basis_imag) + dot(beams_imag, basis_real)) * scale
    count_taps = taps.shape[0]
    for part, total in enumerate((total_real, total_imag)):
        rounded = total.astype(jnp.bfloat16).astype(jnp.float32)
        for t in range(frames):
            value = jnp.zeros((beams, width), jnp.float32)
            for k in range(count_taps):
                at = before + t - k
                value = value + taps[k : k + 1, :] * rounded[at * beams : (at + 1) * beams]
            out[part, t] = value.astype(jnp.bfloat16)


def synthesize(own, halo, taps):
    frames, _, beams, channels = own.shape
    width = min(256, channels)
    return pl.pallas_call(
        synth_kernel,
        grid=(channels // width,),
        in_specs=[
            pl.BlockSpec(own.shape, lambda i: (0, 0, 0, 0)),
            pl.BlockSpec(halo.shape, lambda i: (0, 0, 0, 0)),
            pl.BlockSpec((taps.shape[0], width), lambda i: (0, i)),
        ],
        out_specs=pl.BlockSpec((2, frames, beams, width), lambda i: (0, 0, 0, i)),
        out_shape=jax.ShapeDtypeStruct((2, frames, beams, channels), jnp.bfloat16),
        scratch_shapes=[
            pltpu.VMEM((channels, width), jnp.bfloat16),
            pltpu.VMEM((channels, width), jnp.bfloat16),
            pltpu.VMEM((2, 32, width), jnp.float32),
        ],
        compiler_params=pltpu.CompilerParams(vmem_limit_bytes=48 * 2**20),
        name="synth",
    )(own, halo, taps)


def added(*terms):
    return sum(term.astype(jnp.float32) for term in terms).astype(jnp.bfloat16)


def on_device(voltages, feed_position, beam_steering, synthesis_taps):
    devices = lax.axis_size("chan")
    steps = lax.axis_size("tm")
    taps = synthesis_taps.shape[0]
    feeds = voltages.shape[2]
    position = feed_position.T
    if feeds % LANES:
        position = lax.dynamic_slice_in_dim(position, lax.axis_index("chan") * feeds, feeds, 1)
    keep, send = beamform(voltages, position, beam_steering.T, devices, 0, voltages.shape[3])
    mask = 1
    while True:
        arrived = lax.ppermute(send, "chan", [(i, i ^ mask) for i in range(devices)])
        mask *= 2
        if mask == devices:
            break
        send = added(keep[1::2], arrived[1::2])
        keep = added(keep[0::2], arrived[0::2])
    own = added(keep[0], arrived[0])
    halo = lax.ppermute(own[own.shape[0] - (taps - 1) :], "tm", [(i, i + 1) for i in range(steps - 1)])
    out = synthesize(own, halo, synthesis_taps)
    return jnp.transpose(out, (0, 2, 1, 3))


def solution(mesh):
    return jax.shard_map(
        on_device,
        mesh=mesh,
        in_specs=(P(None, ("group", "tm"), "chan", None), P(), P("group", None), P()),
        out_specs=P(None, "chan", ("group", "tm"), None),
        check_vma=False,
    )
```

time: 107 us -> 57.6 us (0.54)
  Pallas kernels: 74.2 us -> 24.7 us
    pallas_call x1, Pallas kernels: 70.8 us -> 21.5 us  [beamform(): pl.pallas_call(functools.partial(beam_kernel, first), in_specs=[whole, wh...]
where the time goes in v2:
time: 57.6 us; the launch traced here: 57.4 us
  Pallas kernels  24.7 us (43%)
  waiting for transfers between devices  22.3 us (39%)
  starting transfers between devices  7.22 us (13%)
  local copies, waits for them, and re-layouts  2.61 us (5%)
    pallas_call x1, Pallas kernels, beamform(): pl.pallas_call(functools.partial(beam_kernel, first), in_specs=[whole, wh...  21.5 us
    ppermute x2, waiting for transfers between devices, on_device(): lax.ppermute(send, 'chan', [(i, i ^ mask) for i in range(devices)])  14.5 us
    ppermute x1, waiting for transfers between devices, on_device(): lax.ppermute(own[own.shape[0] - (taps - 1):], 'tm', [(i, i + 1) for i in...  7.78 us
    ppermute x1, starting transfers between devices, on_device(): lax.ppermute(own[own.shape[0] - (taps - 1):], 'tm', [(i, i + 1) for i in...  3.75 us
    ppermute x2, starting transfers between devices, on_device(): lax.ppermute(send, 'chan', [(i, i ^ mask) for i in range(devices)])  3.47 us
    pallas_call x1, Pallas kernels, synthesize(): pl.pallas_call(synth_kernel, grid=(channels // width,), in_specs=[pl.Bloc...  3.21 us
    unnamed x6, local copies, waits for them, and re-layouts  1.38 us
    transpose x1, local copies, waits for them, and re-layouts, on_device(): return jnp.transpose(out, (0, 2, 1, 3))  1.2 us
  transfers between devices with their start and end apart: 3, of which 3 were waited for; matrix products, arithmetic and copies ran while one was open for 0% of the time, Pallas kernels for 0%

profile of v2, /device:TPU:0, one launch (start us, length us, event | category | flops | bytes accessed | tf_op | source)
XLA Modules:
  0.0 57.4 jit_solution(8953060325186446854)
XLA Ops:
  0.0 0.0 copy-start.1
  0.0 0.7 %copy-done.1 = s32[1024,2]{0,1:T(2,128)S(1)} copy-done((s32[1024,2]{0,1:T(2,128)S(1)}, s32[1024,2]{0,1:T(2,128)}, u32[]{:S(2)}) %copy-start.1) | copy-done | bytes 8216
  0.7 0.0 copy-start.2
  0.7 0.7 %copy-done.2 = s32[128,2]{0,1:T(2,128)S(1)} copy-done((s32[128,2]{0,1:T(2,128)S(1)}, s32[128,2]{0,1:T(2,128)}, u32[]{:S(2)}) %copy-start.2) | copy-done | bytes 1048
  1.4 21.5 %beam.1 = (bf16[2,4,2,32,1024]{4,3,2,1,0:T(8,128)(2,1)S(1)}, bf16[2,4,2,32,1024]{4,3,2,1,0:T(8,128)(2,1)S(1)}) custom-call(s32[2,1024]{1,0:T(2,128)S(1)} %bitcast.8, s32[2,128]{1,0:T(2,128)S(1)} %bitcast.9, bf16[2,4,256,1024]{3,2,1,0:T(8,128)(2,1)} %voltages.1), custom_call_target="tpu_custom_call" | custom-call | flops 17179869184 | bytes 8388608 | tf_op jit(solution)/shard_map/beam/pallas_call | solution.py:177
  22.9 0.0 copy-start
  22.9 0.6 collective-permute-start
  23.5 2.3 %collective-permute-done = bf16[2,4,2,32,1024]{4,3,2,1,0:T(8,128)(2,1)S(1)} collective-permute-done((bf16[2,4,2,32,1024]{4,3,2,1,0:T(8,128)(2,1)S(1)}, bf16[2,4,2,32,1024]{4,3,2,1,0:T(8,128)(2,1)S(1)}, u32[]{:S(2)}, u32[]{:S(2)}) %collective-permute-start) | collective-permute-done | bytes 1048608 | tf_op jit(solution)/shard_map/ppermute | solution.py:283
  25.8 0.2 add_convert_fusion.1
  26.0 2.9 %collective-permute-start.1 = (bf16[1,4,2,32,1024]{4,3,2,1,0:T(8,128)(2,1)S(1)}, bf16[1,4,2,32,1024]{4,3,2,1,0:T(8,128)(2,1)S(1)}, u32[]{:S(2)}, u32[]{:S(2)}) collective-permute-start(bf16[1,4,2,32,1024]{4,3,2,1,0:T(8,128)(2,1)S(1)} %add_convert_fusion.1), channel_id=1, source_target_pairs={{0,8},{4,12},{8,0},{12,4},{1,9},{5,13},{9,1},{13,5},{2,10},{6,14},... | collective-permute-start | bytes 1572872 | tf_op jit(solution)/shard_map/ppermute | solution.py:283
  28.9 12.2 %collective-permute-done.1 = bf16[1,4,2,32,1024]{4,3,2,1,0:T(8,128)(2,1)S(1)} collective-permute-done((bf16[1,4,2,32,1024]{4,3,2,1,0:T(8,128)(2,1)S(1)}, bf16[1,4,2,32,1024]{4,3,2,1,0:T(8,128)(2,1)S(1)}, u32[]{:S(2)}, u32[]{:S(2)}) %collective-permute-start.1) | collective-permute-done | bytes 524320 | tf_op jit(solution)/shard_map/ppermute | solution.py:283
  41.1 0.3 add_convert_fusion
  41.4 3.8 %collective-permute-start.2 = (bf16[3,2,32,1024]{3,2,1,0:T(8,128)(2,1)S(1)}, bf16[3,2,32,1024]{3,2,1,0:T(8,128)(2,1)S(1)}, u32[]{:S(2)}, u32[]{:S(2)}) collective-permute-start(bf16[3,2,32,1024]{3,2,1,0:T(8,128)(2,1)S(1)} %slice_bitcast_fusion), channel_id=1, source_target_pairs={{0,1},{1,2},{2,3},{4,5},{5,6},{6,7},{8,9},{9,10},{10,11},{12,13},{... | collective-permute-start | bytes 1179656 | tf_op jit(solution)/shard_map/ppermute | solution.py:290
  45.2 7.8 %collective-permute-done.2.halo = bf16[3,2,32,1024]{3,2,1,0:T(8,128)(2,1)S(1)} collective-permute-done((bf16[3,2,32,1024]{3,2,1,0:T(8,128)(2,1)S(1)}, bf16[3,2,32,1024]{3,2,1,0:T(8,128)(2,1)S(1)}, u32[]{:S(2)}, u32[]{:S(2)}) %collective-permute-start.2) | collective-permute-done | bytes 393248 | tf_op jit(solution)/shard_map/ppermute | solution.py:290
  53.0 0.0 copy-done
  53.0 3.2 %synth.1 = bf16[2,4,32,1024]{3,2,1,0:T(8,128)(2,1)S(1)} custom-call(bf16[4,2,32,1024]{3,2,1,0:T(8,128)(2,1)S(1)} %bitcast.6, bf16[3,2,32,1024]{3,2,1,0:T(8,128)(2,1)S(1)} %collective-permute-done.2.halo, f32[4,1024]{1,0:T(4,128)S(1)} %copy-done), custom_call_target="tpu_custom_call" | custom-call | tf_op jit(solution)/shard_map/synth/pallas_call | solution.py:248
  56.2 1.2 %copy.5 = bf16[2,32,4,1024]{3,2,1,0:T(4,128)(2,1)} copy(bf16[2,32,4,1024]{3,1,2,0:T(8,128)(2,1)S(1)} %bitcast.7) | data formatting | bytes 1048576 | tf_op jit(solution)/shard_map/transpose | solution.py:292
  (1 shorter events, 0.0 us)
Async XLA Ops:
  0.0 0.7 %copy-start.1 = (s32[1024,2]{0,1:T(2,128)S(1)}, s32[1024,2]{0,1:T(2,128)}, u32[]{:S(2)}) copy-start(s32[1024,2]{0,1:T(2,128)} %param.5) | copy-start | bytes 24580
  0.7 0.7 %copy-start.2 = (s32[128,2]{0,1:T(2,128)S(1)}, s32[128,2]{0,1:T(2,128)}, u32[]{:S(2)}) copy-start(s32[128,2]{0,1:T(2,128)} %param.6) | copy-start | bytes 3076
  22.9 30.1 %copy-start = (f32[4,1024]{1,0:T(4,128)S(1)}, f32[4,1024]{1,0:T(4,128)}, u32[]{:S(2)}) copy-start(f32[4,1024]{1,0:T(4,128)} %taps.1) | copy-start | bytes 49156
  22.9 2.8 %collective-permute-start = (bf16[2,4,2,32,1024]{4,3,2,1,0:T(8,128)(2,1)S(1)}, bf16[2,4,2,32,1024]{4,3,2,1,0:T(8,128)(2,1)S(1)}, u32[]{:S(2)}, u32[]{:S(2)}) collective-permute-start(bf16[2,4,2,32,1024]{4,3,2,1,0:T(8,128)(2,1)S(1)} %get-tuple-element.8), channel_id=1, source_target_pairs={{0,4},{4,0},{8,12},{12,8},{1,5},{5,1},{9,13},{13,9},{2,6},{6,2},{1... | collective-permute-start | bytes 3145736 | tf_op jit(solution)/shard_map/ppermute | solution.py:283
  26.0 15.1 %collective-permute-start.1 = (bf16[1,4,2,32,1024]{4,3,2,1,0:T(8,128)(2,1)S(1)}, bf16[1,4,2,32,1024]{4,3,2,1,0:T(8,128)(2,1)S(1)}, u32[]{:S(2)}, u32[]{:S(2)}) collective-permute-start(bf16[1,4,2,32,1024]{4,3,2,1,0:T(8,128)(2,1)S(1)} %add_convert_fusion.1), channel_id=1, source_target_pairs={{0,8},{4,12},{8,0},{12,4},{1,9},{5,13},{9,1},{13,5},{2,10},{6,14},... | collective-permute-start | bytes 1572872 | tf_op jit(solution)/shard_map/ppermute | solution.py:283
  41.4 11.5 %collective-permute-start.2 = (bf16[3,2,32,1024]{3,2,1,0:T(8,128)(2,1)S(1)}, bf16[3,2,32,1024]{3,2,1,0:T(8,128)(2,1)S(1)}, u32[]{:S(2)}, u32[]{:S(2)}) collective-permute-start(bf16[3,2,32,1024]{3,2,1,0:T(8,128)(2,1)S(1)} %slice_bitcast_fusion), channel_id=1, source_target_pairs={{0,1},{1,2},{2,3},{4,5},{5,6},{6,7},{8,9},{9,10},{10,11},{12,13},{... | collective-permute-start | bytes 1179656 | tf_op jit(solution)/shard_map/ppermute | solution.py:290

commit v3 on v2

--- a/solution.py
+++ b/solution.py
@@ -7,6 +7,7 @@
 from jax.experimental import pallas as pl
 from jax.experimental.pallas import tpu as pltpu
 from jax.sharding import PartitionSpec as P
+
 
 PHASES = 4096
 LANES = 128
@@ -35,7 +36,7 @@
     return a[0] * b[0] - a[1] * b[1], a[0] * b[1] + a[1] * b[0]
 
 
-def beam_kernel(first, position, steering, voltages, keep, send, staged, arrivals, centre_tables, offset_tables, rows_even, rows_odd, sums_even, sums_odd):
+def beam_kernel(first, position_hbm, steering_hbm, voltages, keep, send, position, steering, small_arrivals, staged, arrivals, centre_tables, offset_tables, rows_even, rows_odd, sums_even, sums_odd):
     feeds, beams = offset_tables.shape[2:]
     frames = voltages.shape[1]
     stride = 2 * frames
@@ -52,8 +53,14 @@
         source = voltages.at[:, :, :, pl.ds(first + index * block, block)]
         return pltpu.make_async_copy(source, staged.at[index], arrivals.at[index])
 
+    position_copy = pltpu.make_async_copy(position_hbm, position, small_arrivals.at[0])
+    steering_copy = pltpu.make_async_copy(steering_hbm, steering, small_arrivals.at[1])
+    position_copy.start()
+    steering_copy.start()
     for index in range(blocks):
         arrival(index).start()
+    position_copy.wait()
+    steering_copy.wait()
 
     def column(axis):
         start = here * feeds if position.shape[1] > feeds else 0
@@ -174,12 +181,16 @@
     sums = pltpu.VMEM((LANES * 2 * frames, beams), jnp.float32)
     work = 2 * frames * 2 * feeds * beams * count
     whole = pl.BlockSpec(memory_space=pltpu.VMEM)
+    anywhere = pl.BlockSpec(memory_space=pltpu.HBM)
     return pl.pallas_call(
         functools.partial(beam_kernel, first),
-        in_specs=[whole, whole, pl.BlockSpec(memory_space=pl.ANY)],
+        in_specs=[anywhere, anywhere, anywhere],
         out_specs=[whole, whole],
         out_shape=[shape, shape],
         scratch_shapes=[
+            pltpu.VMEM(position.shape, jnp.int32),
+            pltpu.VMEM(steering.shape, jnp.int32),
+            pltpu.SemaphoreType.DMA((2,)),
             pltpu.VMEM((count // LANES, 2, frames, feeds, LANES), jnp.bfloat16),
             pltpu.SemaphoreType.DMA((count // LANES,)),
             pltpu.VMEM((2, count // (2 * HALF), feeds, beams), TABLE),
@@ -195,81 +206,137 @@
     )(position, steering, voltages)
 
 
-def synth_kernel(own, halo, taps, out, basis_real, basis_imag, small):
-    frames, _, beams, channels = own.shape
-    before = halo.shape[0]
-    width = out.shape[3]
-    first = pl.program_id(0) * width
+def basis_kernel(basis, small):
+    channels = basis.shape[0]
+    width = small.shape[2]
     group = small.shape[1]
 
-    def phases(rows, factor):
-        row = lax.broadcasted_iota(jnp.int32, (rows, width), 0) * factor
-        column = first + lax.broadcasted_iota(jnp.int32, (rows, width), 1)
-        return (row * column) & (channels - 1)
-
-    real, imag = turn(phases(group, 1), channels)
-    small[0] = real
-    small[1] = imag
-    count = channels // group
-    large = turn(phases(count, group), channels)
-    for index in range(count):
-        a = (large[0][index : index + 1], large[1][index : index + 1])
-        value = times(a, (small[0], small[1]))
-        basis_real[index * group : (index + 1) * group, :] = value[0].astype(jnp.bfloat16)
-        basis_imag[index * group : (index + 1) * group, :] = value[1].astype(jnp.bfloat16)
-
-    def gather(part):
-        pieces = [halo[t, part] for t in range(before)] + [own[t, part] for t in range(frames)]
-        return jnp.concatenate(pieces, axis=0)
-
-    beams_real = gather(0)
-    beams_imag = gather(1)
-
-    def dot(a, b):
-        return jnp.dot(a, b[...], preferred_element_type=jnp.float32)
-
+    def one_slab(index, carry):
+        first = pl.multiple_of(index * width, width)
+
+        def phases(rows, factor):
+            row = lax.broadcasted_iota(jnp.int32, (rows, width), 0) * factor
+            column = first + lax.broadcasted_iota(jnp.int32, (rows, width), 1)
+            return (row * column) & (channels - 1)
+
+        small[0], small[1] = turn(phases(group, 1), channels)
+        count = channels // group
+        large = turn(phases(count, group), channels)
+        for at in range(count):
+            real, imag = times((large[0][at : at + 1], large[1][at : at + 1]), (small[0], small[1]))
+            basis[at * group : (at + 1) * group, pl.ds(first, width)] = real.astype(jnp.bfloat16)
+            basis[at * group : (at + 1) * group, pl.ds(pl.multiple_of(channels + first, width), width)] = imag.astype(jnp.bfloat16)
+        return carry
+
+    lax.fori_loop(0, channels // width, one_slab, 0)
+
+
+def make_basis(channels):
+    return pl.pallas_call(
+        basis_kernel,
+        out_specs=pl.BlockSpec(memory_space=pltpu.VMEM),
+        out_shape=jax.ShapeDtypeStruct((channels, 2 * channels), jnp.bfloat16),
+        scratch_shapes=[pltpu.VMEM((2, 32, 256), jnp.float32)],
+        compiler_params=pltpu.CompilerParams(vmem_limit_bytes=8 * 2**20),
+        cost_estimate=pl.CostEstimate(flops=2**30, bytes_accessed=4 * channels * channels, transcendentals=0),
+        name="basis",
+    )()
+
+
+def transform(pieces, basis, first, width):
+    frames, _, beams, _ = pieces[0].shape
+    channels = basis.shape[0]
+    total = None
+    start = 0
+    for piece in pieces:
+        count = piece.shape[3]
+        rows = [piece[t, part] for part in range(2) for t in range(frames)]
+        rows = jnp.concatenate(rows, axis=0)
+        for part in range(2):
+            columns = pl.ds(pl.multiple_of(part * channels + first, width), width)
+            product = jnp.dot(rows, basis[start : start + count, columns], preferred_element_type=jnp.float32)
+            total = [None, None] if total is None else total
+            total[part] = product if total[part] is None else total[part] + product
+        start += count
+    half = frames * beams
     scale = 1.0 / math.sqrt(channels)
-    total_real = (dot(beams_real, basis_real) - dot(beams_imag, basis_imag)) * scale
-    total_imag = (dot(beams_real, basis_imag) + dot(beams_imag, basis_real)) * scale
-    count_taps = taps.shape[0]
-    for part, total in enumerate((total_real, total_imag)):
-        rounded = total.astype(jnp.bfloat16).astype(jnp.float32)
-        for t in range(frames):
-            value = jnp.zeros((beams, width), jnp.float32)
-            for k in range(count_taps):
-                at = before + t - k
-                value = value + taps[k : k + 1, :] * rounded[at * beams : (at + 1) * beams]
-            out[part, t] = value.astype(jnp.bfloat16)
-
-
-def synthesize(own, halo, taps):
-    frames, _, beams, channels = own.shape
-    width = min(256, channels)
+    real = (total[0][:half] - total[1][half:]) * scale
+    imag = (total[1][:half] + total[0][half:]) * scale
+    return real.astype(jnp.bfloat16), imag.astype(jnp.bfloat16)
+
+
+def frames_kernel(*refs):
+    pieces, basis, out = refs[:-2], refs[-2], refs[-1]
+    width = min(256, out.shape[2])
+
+    def one_slab(index, carry):
+        first = pl.multiple_of(index * width, width)
+        real, imag = transform(pieces, basis, first, width)
+        out[0, :, pl.ds(first, width)] = real
+        out[1, :, pl.ds(first, width)] = imag
+        return carry
+
+    lax.fori_loop(0, out.shape[2] // width, one_slab, 0)
+
+
+def make_frames(pieces, basis):
+    frames, _, beams, _ = pieces[0].shape
+    channels = basis.shape[0]
+    whole = pl.BlockSpec(memory_space=pltpu.VMEM)
     return pl.pallas_call(
-        synth_kernel,
-        grid=(channels // width,),
-        in_specs=[
-            pl.BlockSpec(own.shape, lambda i: (0, 0, 0, 0)),
-            pl.BlockSpec(halo.shape, lambda i: (0, 0, 0, 0)),
-            pl.BlockSpec((taps.shape[0], width), lambda i: (0, i)),
-        ],
-        out_specs=pl.BlockSpec((2, frames, beams, width), lambda i: (0, 0, 0, i)),
+        frames_kernel,
+        in_specs=[whole] * (len(pieces) + 1),
+        out_specs=whole,
+        out_shape=jax.ShapeDtypeStruct((2, frames * beams, channels), jnp.bfloat16),
+        compiler_params=pltpu.CompilerParams(vmem_limit_bytes=16 * 2**20),
+        cost_estimate=pl.CostEstimate(flops=8 * frames * beams * channels**2, bytes_accessed=4 * channels * channels, transcendentals=0),
+        name="frames",
+    )(*pieces, basis)
+
+
+def taps_kernel(*refs):
+    halos, own, basis, taps, out = refs[:-4], refs[-4], refs[-3], refs[-2], refs[-1]
+    before, _, beams, _ = halos[0].shape
+    frames = own.shape[1] // beams
+    width = min(256, own.shape[2])
+
+    def one_slab(index, carry):
+        first = pl.multiple_of(index * width, width)
+        earlier = transform(halos, basis, first, width)
+        for part in range(2):
+            rows = [earlier[part][t * beams : (t + 1) * beams].astype(jnp.float32) for t in range(before)]
+            rows += [own[part, t * beams : (t + 1) * beams, pl.ds(first, width)].astype(jnp.float32) for t in range(frames)]
+            for t in range(frames):
+                value = jnp.zeros((beams, width), jnp.float32)
+                for k in range(taps.shape[0]):
+                    value = value + taps[k : k + 1, pl.ds(first, width)] * rows[before + t - k]
+                out[part, t, :, pl.ds(first, width)] = value.astype(jnp.bfloat16)
+        return carry
+
+    lax.fori_loop(0, own.shape[2] // width, one_slab, 0)
+
+
+def apply_taps(halos, own, basis, taps):
+    before, _, beams, _ = halos[0].shape
+    channels = basis.shape[0]
+    frames = own.shape[1] // beams
+    whole = pl.BlockSpec(memory_space=pltpu.VMEM)
+    return pl.pallas_call(
+        taps_kernel,
+        in_specs=[whole] * (len(halos) + 3),
+        out_specs=whole,
         out_shape=jax.ShapeDtypeStruct((2, frames, beams, channels), jnp.bfloat16),
-        scratch_shapes=[
-            pltpu.VMEM((channels, width), jnp.bfloat16),
-            pltpu.VMEM((channels, width), jnp.bfloat16),
-            pltpu.VMEM((2, 32, width), jnp.float32),
-        ],
-        compiler_params=pltpu.CompilerParams(vmem_limit_bytes=48 * 2**20),
-        name="synth",
-    )(own, halo, taps)
+        compiler_params=pltpu.CompilerParams(vmem_limit_bytes=16 * 2**20),
+        cost_estimate=pl.CostEstimate(flops=8 * before * beams * channels**2, bytes_accessed=4 * channels * channels, transcendentals=0),
+        name="taps",
+    )(*halos, own, basis, taps)
 
 
 def added(*terms):
     return sum(term.astype(jnp.float32) for term in terms).astype(jnp.bfloat16)
 
 
-def on_device(voltages, feed_position, beam_steering, synthesis_taps):
+def steps_on_device(voltages, feed_position, beam_steering, synthesis_taps):
     devices = lax.axis_size("chan")
     steps = lax.axis_size("tm")
     taps = synthesis_taps.shape[0]
@@ -277,24 +344,53 @@
     position = feed_position.T
     if feeds % LANES:
         position = lax.dynamic_slice_in_dim(position, lax.axis_index("chan") * feeds, feeds, 1)
-    keep, send = beamform(voltages, position, beam_steering.T, devices, 0, voltages.shape[3])
-    mask = 1
-    while True:
-        arrived = lax.ppermute(send, "chan", [(i, i ^ mask) for i in range(devices)])
-        mask *= 2
-        if mask == devices:
-            break
-        send = added(keep[1::2], arrived[1::2])
-        keep = added(keep[0::2], arrived[0::2])
-    own = added(keep[0], arrived[0])
-    halo = lax.ppermute(own[own.shape[0] - (taps - 1) :], "tm", [(i, i + 1) for i in range(steps - 1)])
-    out = synthesize(own, halo, synthesis_taps)
+    channels = voltages.shape[3]
+    parts = [(0, channels - channels // 4), (channels - channels // 4, channels // 4)]
+    basis = make_basis(channels)
+    steering = beam_steering.T
+    owns = []
+    halos = []
+
+    def across(value, mask):
+        return lax.ppermute(value, "chan", [(i, i ^ mask) for i in range(devices)])
+
+    def last_stage(keep, send):
+        terms = [keep]
+        mask = 1
+        while 2 * mask < devices:
+            terms.append(across(send, mask))
+            send = added(*[term[1::2] for term in terms])
+            terms = [term[0::2] for term in terms]
+            mask *= 2
+        return send, terms, mask
+
+    def ended(terms, arrived):
+        own = added(*[term[0] for term in terms], arrived[0])
+        return own, lax.ppermute(own[own.shape[0] - (taps - 1) :], "tm", [(i, i + 1) for i in range(steps - 1)])
+
+    waiting = None
+    voltages = pltpu.with_memory_space_constraint(voltages, pltpu.HBM)
+    for part in parts:
+        keep, send = beamform(voltages, position, steering, devices, *part)
+        send, terms, mask = last_stage(keep, send)
+        if waiting is not None:
+            arrived, send = lax.optimization_barrier((waiting[1], send))
+            own, halo = ended(waiting[0], arrived)
+            owns.append(own)
+            halos.append(halo)
+        position, send = lax.optimization_barrier((position, send))
+        waiting = (terms, across(send, mask))
+    own, halo = ended(*waiting)
+    owns.append(own)
+    halos.append(halo)
+    frames = make_frames(owns, basis)
+    out = apply_taps(halos, frames, basis, synthesis_taps)
     return jnp.transpose(out, (0, 2, 1, 3))
 
 
 def solution(mesh):
     return jax.shard_map(
-        on_device,
+        steps_on_device,
         mesh=mesh,
         in_specs=(P(None, ("group", "tm"), "chan", None), P(), P("group", None), P()),
         out_specs=P(None, "chan", ("group", "tm"), None),

time: 57.6 us -> 56.8 us (0.986)
  waiting for transfers between devices: 22.3 us -> 12 us
  starting transfers between devices: 7.22 us -> 12.3 us
  Pallas kernels: 24.7 us -> 29.2 us
    ppermute x3 -> x6, waiting for transfers between devices: 22.3 us -> 12 us  [the longest x4 9.66 us: across(): return lax.ppermute(value, 'chan', [(i, i ^ mask) for i in range(devices)])]
    ppermute x3 -> x6, starting transfers between devices: 7.22 us -> 12.3 us  [the longest x2 6.97 us: ended(): lax.ppermute(own[own.shape[0] - (taps - 1):], 'tm', [(i, i + 1) for i in...]
    pallas_call x2 -> x5, Pallas kernels: 24.7 us -> 29.2 us  [the longest x2 23.8 us: beamform(): pl.pallas_call(functools.partial(beam_kernel, first), in_specs=[anywhere,...]
  transfers between devices with their start and end apart: 3 -> 6, of which waited for: 3 -> 3; matrix products, arithmetic and copies ran while one was open for 0% -> 0% of each run, Pallas kernels for 0% -> 7%
where the time goes in v3:
time: 56.8 us; the launch traced here: 56.6 us
  Pallas kernels  29.2 us (51%)
  starting transfers between devices  12.3 us (22%)
  waiting for transfers between devices  12 us (21%)
  local copies, waits for them, and re-layouts  2.61 us (5%)
    pallas_call x2, Pallas kernels, beamform(): pl.pallas_call(functools.partial(beam_kernel, first), in_specs=[anywhere,...  23.8 us
    ppermute x4, waiting for transfers between devices, across(): return lax.ppermute(value, 'chan', [(i, i ^ mask) for i in range(devices)])  9.66 us
    ppermute x2, starting transfers between devices, ended(): lax.ppermute(own[own.shape[0] - (taps - 1):], 'tm', [(i, i + 1) for i in...  6.97 us
    ppermute x4, starting transfers between devices, across(): return lax.ppermute(value, 'chan', [(i, i ^ mask) for i in range(devices)])  5.35 us
    ppermute x2, waiting for transfers between devices, ended(): lax.ppermute(own[own.shape[0] - (taps - 1):], 'tm', [(i, i + 1) for i in...  2.32 us
    pallas_call x1, Pallas kernels, make_frames(): pl.pallas_call(frames_kernel, in_specs=[whole] * (len(pieces) + 1), out_s...  1.84 us
    pallas_call x1, Pallas kernels, make_basis(): pl.pallas_call(basis_kernel, out_specs=pl.BlockSpec(memory_space=pltpu.VM...  1.84 us
    pallas_call x1, Pallas kernels, apply_taps(): pl.pallas_call(taps_kernel, in_specs=[whole] * (len(halos) + 3), out_spec...  1.69 us
  transfers between devices with their start and end apart: 6, of which 3 were waited for; matrix products, arithmetic and copies ran while one was open for 0% of the time, Pallas kernels for 7%

profile of v3, /device:TPU:0, one launch (start us, length us, event | category | flops | bytes accessed | tf_op | source)
XLA Modules:
  0.0 56.6 jit_solution(11982701991855042276)
XLA Ops:
  0.0 0.7 %copy-done.1 = s32[1024,2]{0,1:T(2,128)S(1)} copy-done((s32[1024,2]{0,1:T(2,128)S(1)}, s32[1024,2]{0,1:T(2,128)}, u32[]{:S(2)}) %copy-start.1) | copy-done | bytes 8216
  0.7 0.7 %copy-done.2 = s32[128,2]{0,1:T(2,128)S(1)} copy-done((s32[128,2]{0,1:T(2,128)S(1)}, s32[128,2]{0,1:T(2,128)}, u32[]{:S(2)}) %copy-start.2) | copy-done | bytes 1048
  1.4 16.9 %beam.2 = (bf16[2,4,2,32,768]{4,3,2,1,0:T(8,128)(2,1)S(1)}, bf16[2,4,2,32,768]{4,3,2,1,0:T(8,128)(2,1)S(1)}) custom-call(s32[2,1024]{1,0:T(2,128)S(1)} %bitcast.12, s32[2,128]{1,0:T(2,128)S(1)} %bitcast.14, bf16[2,4,256,1024]{3,2,1,0:T(8,128)(2,1)} %voltages.3), custom_call_target="tpu_custom_call" | custom-call | flops 12884901888 | bytes 6291456 | tf_op jit(solution)/shard_map/beam/pallas_call | solution.py:185
  18.3 0.6 collective-permute-start
  18.9 1.9 %collective-permute-done = bf16[2,4,2,32,768]{4,3,2,1,0:T(8,128)(2,1)S(1)} collective-permute-done((bf16[2,4,2,32,768]{4,3,2,1,0:T(8,128)(2,1)S(1)}, bf16[2,4,2,32,768]{4,3,2,1,0:T(8,128)(2,1)S(1)}, u32[]{:S(2)}, u32[]{:S(2)}) %collective-permute-start) | collective-permute-done | bytes 786464 | tf_op jit(solution)/shard_map/ppermute | solution.py:355
  20.8 0.1 add_convert_fusion.1
  20.9 6.9 %beam.3 = (bf16[2,4,2,32,256]{4,3,2,1,0:T(8,128)(2,1)S(1)}, bf16[2,4,2,32,256]{4,3,2,1,0:T(8,128)(2,1)S(1)}) custom-call(s32[2,1024]{1,0:T(2,128)S(1)} %bitcast.13, s32[2,128]{1,0:T(2,128)S(1)} %bitcast.15, bf16[2,4,256,1024]{3,2,1,0:T(8,128)(2,1)} %voltages.3), custom_call_target="tpu_custom_call" | custom-call | flops 4294967296 | bytes 2097152 | tf_op jit(solution)/shard_map/beam/pallas_call | solution.py:185
  27.8 0.4 collective-permute-start.2
  28.2 2.6 %collective-permute-start.1 = (bf16[1,4,2,32,768]{4,3,2,1,0:T(8,128)(2,1)S(1)}, bf16[1,4,2,32,768]{4,3,2,1,0:T(8,128)(2,1)S(1)}, u32[]{:S(2)}, u32[]{:S(2)}) collective-permute-start(bf16[1,4,2,32,768]{4,3,2,1,0:T(8,128)(2,1)S(1)} %add_convert_fusion.1), channel_id=1, source_target_pairs={{0,8},{4,12},{8,0},{12,4},{1,9},{5,13},{9,1},{13,5},{2,10},{6,14},... | collective-permute-start | bytes 1179656 | tf_op jit(solution)/shard_map/ppermute | solution.py:355
  30.9 1.8 %basis.1.refs_2_.refs_3_ = bf16[1024,2048]{1,0:T(8,128)(2,1)S(1)} custom-call(), custom_call_target="tpu_custom_call" | custom-call | flops 1073741824 | bytes 4194304 | tf_op jit(solution)/shard_map/basis/pallas_call | solution.py:235
  32.7 0.0 collective-permute-done.2
  32.7 0.0 copy-start
  32.8 7.7 %collective-permute-done.1 = bf16[1,4,2,32,768]{4,3,2,1,0:T(8,128)(2,1)S(1)} collective-permute-done((bf16[1,4,2,32,768]{4,3,2,1,0:T(8,128)(2,1)S(1)}, bf16[1,4,2,32,768]{4,3,2,1,0:T(8,128)(2,1)S(1)}, u32[]{:S(2)}, u32[]{:S(2)}) %collective-permute-start.1) | collective-permute-done | bytes 393248 | tf_op jit(solution)/shard_map/ppermute | solution.py:355
  40.5 1.7 %collective-permute-start.4 = (bf16[1,4,2,32,256]{4,3,2,1,0:T(8,128)(2,1)S(1)}, bf16[1,4,2,32,256]{4,3,2,1,0:T(8,128)(2,1)S(1)}, u32[]{:S(2)}, u32[]{:S(2)}) collective-permute-start(bf16[1,4,2,32,256]{4,3,2,1,0:T(8,128)(2,1)S(1)} %add_convert_fusion.3), channel_id=1, source_target_pairs={{0,8},{4,12},{8,0},{12,4},{1,9},{5,13},{9,1},{13,5},{2,10},{6,14},... | collective-permute-start | bytes 393224 | tf_op jit(solution)/shard_map/ppermute | solution.py:355
  42.3 0.2 add_convert_fusion
  42.4 3.5 %collective-permute-start.3 = (bf16[3,2,32,768]{3,2,1,0:T(8,128)(2,1)S(1)}, bf16[3,2,32,768]{3,2,1,0:T(8,128)(2,1)S(1)}, u32[]{:S(2)}, u32[]{:S(2)}) collective-permute-start(bf16[3,2,32,768]{3,2,1,0:T(8,128)(2,1)S(1)} %slice_bitcast_fusion), channel_id=1, source_target_pairs={{0,1},{1,2},{2,3},{4,5},{5,6},{6,7},{8,9},{9,10},{10,11},{12,13},{... | collective-permute-start | bytes 884744 | tf_op jit(solution)/shard_map/ppermute | solution.py:369
  45.9 0.0 collective-permute-done.4
  46.0 0.1 add_convert_fusion.2
  46.0 3.5 %collective-permute-start.5 = (bf16[3,2,32,256]{3,2,1,0:T(8,128)(2,1)S(1)}, bf16[3,2,32,256]{3,2,1,0:T(8,128)(2,1)S(1)}, u32[]{:S(2)}, u32[]{:S(2)}) collective-permute-start(bf16[3,2,32,256]{3,2,1,0:T(8,128)(2,1)S(1)} %slice_bitcast_fusion.1), channel_id=1, source_target_pairs={{0,1},{1,2},{2,3},{4,5},{5,6},{6,7},{8,9},{9,10},{10,11},{12,13},{... | collective-permute-start | bytes 294920 | tf_op jit(solution)/shard_map/ppermute | solution.py:369
  49.5 1.8 %frames.1.refs_2_ = bf16[2,128,1024]{2,1,0:T(8,128)(2,1)S(1)} custom-call(bf16[4,2,32,768]{3,2,1,0:T(8,128)(2,1)S(1)} %bitcast.9, bf16[4,2,32,256]{3,2,1,0:T(8,128)(2,1)S(1)} %bitcast.11, bf16[1024,2048]{1,0:T(8,128)(2,1)S(1)} %basis.1.refs_2_.refs_3_), custom_call_target="tpu_custom_call" | custom-call | flops 1073741824 | bytes 4194304 | tf_op jit(solution)/shard_map/frames/pallas_call | solution.py:286
  51.4 2.3 %collective-permute-done.5.refs_1_ = bf16[3,2,32,256]{3,2,1,0:T(8,128)(2,1)S(1)} collective-permute-done((bf16[3,2,32,256]{3,2,1,0:T(8,128)(2,1)S(1)}, bf16[3,2,32,256]{3,2,1,0:T(8,128)(2,1)S(1)}, u32[]{:S(2)}, u32[]{:S(2)}) %collective-permute-start.5) | collective-permute-done | bytes 98336 | tf_op jit(solution)/shard_map/ppermute | solution.py:369
  53.7 0.0 collective-permute-done.3.refs_0_
  53.7 1.7 %taps.1 = bf16[2,4,32,1024]{3,2,1,0:T(8,128)(2,1)S(1)} custom-call(bf16[3,2,32,768]{3,2,1,0:T(8,128)(2,1)S(1)} %collective-permute-done.3.refs_0_, bf16[3,2,32,256]{3,2,1,0:T(8,128)(2,1)S(1)} %collective-permute-done.5.refs_1_, bf16[2,128,1024]{2,1,0:T(8,128)(2,1)S(1)} %frames.1.refs_2_, bf16[1024,2048]{1,0:T(8,128)(2,1)S(1)} %basis.1.refs_2_.refs_3_, ...), custom_call_target="tpu_custom_call" | custom-call | flops 805306368 | bytes 4194304 | tf_op jit(solution)/shard_map/taps/pallas_call | solution.py:324
  55.4 1.2 %copy.5 = bf16[2,32,4,1024]{3,2,1,0:T(4,128)(2,1)} copy(bf16[2,32,4,1024]{3,1,2,0:T(8,128)(2,1)S(1)} %bitcast.10) | data formatting | bytes 1048576 | tf_op jit(solution)/shard_map/transpose | solution.py:388
  (6 shorter events, 0.1 us)
Async XLA Ops:
  0.0 0.7 %copy-start.1 = (s32[1024,2]{0,1:T(2,128)S(1)}, s32[1024,2]{0,1:T(2,128)}, u32[]{:S(2)}) copy-start(s32[1024,2]{0,1:T(2,128)} %param.5) | copy-start | bytes 24580
  0.7 0.7 %copy-start.2 = (s32[128,2]{0,1:T(2,128)S(1)}, s32[128,2]{0,1:T(2,128)}, u32[]{:S(2)}) copy-start(s32[128,2]{0,1:T(2,128)} %param.6) | copy-start | bytes 3076
  18.3 2.5 %collective-permute-start = (bf16[2,4,2,32,768]{4,3,2,1,0:T(8,128)(2,1)S(1)}, bf16[2,4,2,32,768]{4,3,2,1,0:T(8,128)(2,1)S(1)}, u32[]{:S(2)}, u32[]{:S(2)}) collective-permute-start(bf16[2,4,2,32,768]{4,3,2,1,0:T(8,128)(2,1)S(1)} %get-tuple-element.15), channel_id=1, source_target_pairs={{0,4},{4,0},{8,12},{12,8},{1,5},{5,1},{9,13},{13,9},{2,6},{6,2},{1... | collective-permute-start | bytes 2359304 | tf_op jit(solution)/shard_map/ppermute | solution.py:355
  27.8 4.9 %collective-permute-start.2 = (bf16[2,4,2,32,256]{4,3,2,1,0:T(8,128)(2,1)S(1)}, bf16[2,4,2,32,256]{4,3,2,1,0:T(8,128)(2,1)S(1)}, u32[]{:S(2)}, u32[]{:S(2)}) collective-permute-start(bf16[2,4,2,32,256]{4,3,2,1,0:T(8,128)(2,1)S(1)} %get-tuple-element.19), channel_id=1, source_target_pairs={{0,4},{4,0},{8,12},{12,8},{1,5},{5,1},{9,13},{13,9},{2,6},{6,2},{1... | collective-permute-start | bytes 786440 | tf_op jit(solution)/shard_map/ppermute | solution.py:355
  28.2 12.3 %collective-permute-start.1 = (bf16[1,4,2,32,768]{4,3,2,1,0:T(8,128)(2,1)S(1)}, bf16[1,4,2,32,768]{4,3,2,1,0:T(8,128)(2,1)S(1)}, u32[]{:S(2)}, u32[]{:S(2)}) collective-permute-start(bf16[1,4,2,32,768]{4,3,2,1,0:T(8,128)(2,1)S(1)} %add_convert_fusion.1), channel_id=1, source_target_pairs={{0,8},{4,12},{8,0},{12,4},{1,9},{5,13},{9,1},{13,5},{2,10},{6,14},... | collective-permute-start | bytes 1179656 | tf_op jit(solution)/shard_map/ppermute | solution.py:355
  32.7 21.0 %copy-start = (f32[4,1024]{1,0:T(4,128)S(1)}, f32[4,1024]{1,0:T(4,128)}, u32[]{:S(2)}) copy-start(f32[4,1024]{1,0:T(4,128)} %refs_4_.1) | copy-start | bytes 49156
  40.5 5.4 %collective-permute-start.4 = (bf16[1,4,2,32,256]{4,3,2,1,0:T(8,128)(2,1)S(1)}, bf16[1,4,2,32,256]{4,3,2,1,0:T(8,128)(2,1)S(1)}, u32[]{:S(2)}, u32[]{:S(2)}) collective-permute-start(bf16[1,4,2,32,256]{4,3,2,1,0:T(8,128)(2,1)S(1)} %add_convert_fusion.3), channel_id=1, source_target_pairs={{0,8},{4,12},{8,0},{12,4},{1,9},{5,13},{9,1},{13,5},{2,10},{6,14},... | collective-permute-start | bytes 393224 | tf_op jit(solution)/shard_map/ppermute | solution.py:355
  42.4 11.2 %collective-permute-start.3 = (bf16[3,2,32,768]{3,2,1,0:T(8,128)(2,1)S(1)}, bf16[3,2,32,768]{3,2,1,0:T(8,128)(2,1)S(1)}, u32[]{:S(2)}, u32[]{:S(2)}) collective-permute-start(bf16[3,2,32,768]{3,2,1,0:T(8,128)(2,1)S(1)} %slice_bitcast_fusion), channel_id=1, source_target_pairs={{0,1},{1,2},{2,3},{4,5},{5,6},{6,7},{8,9},{9,10},{10,11},{12,13},{... | collective-permute-start | bytes 884744 | tf_op jit(solution)/shard_map/ppermute | solution.py:369
  46.0 7.6 %collective-permute-start.5 = (bf16[3,2,32,256]{3,2,1,0:T(8,128)(2,1)S(1)}, bf16[3,2,32,256]{3,2,1,0:T(8,128)(2,1)S(1)}, u32[]{:S(2)}, u32[]{:S(2)}) collective-permute-start(bf16[3,2,32,256]{3,2,1,0:T(8,128)(2,1)S(1)} %slice_bitcast_fusion.1), channel_id=1, source_target_pairs={{0,1},{1,2},{2,3},{4,5},{5,6},{6,7},{8,9},{9,10},{10,11},{12,13},{... | collective-permute-start | bytes 294920 | tf_op jit(solution)/shard_map/ppermute | solution.py:369

commit v4 on v3

v4 whole, which is shorter than its diff:
```python
import functools
import math

import jax
import jax.numpy as jnp
from jax import lax
from jax.experimental import pallas as pl
from jax.experimental.pallas import tpu as pltpu
from jax.sharding import PartitionSpec as P


PHASES = 4096
LANES = 128
HALF = 32
SLAB = 16
TABLE = jnp.float32
BEAM_LIMIT = 24
AHEAD = 2


def turn(phase, steps):
    quarter = steps // 4
    shift = quarter.bit_length() - 1
    quadrant = lax.shift_right_logical(phase + quarter // 2, shift)
    rest = (phase - lax.shift_left(quadrant, shift)).astype(jnp.float32) * (2.0 * math.pi / steps)
    square = rest * rest
    sine = rest * (1.0 + square * (-1.6666666e-1 + square * (8.3333310e-3 + square * (-1.9840874e-4 + square * 2.7525562e-6))))
    cosine = 1.0 + square * (-0.5 + square * (4.1666666e-2 + square * (-1.3888889e-3 + square * (2.4801587e-5 - square * 2.7557319e-7))))
    odd = (quadrant & 1) == 1
    real = jnp.where(odd, sine, cosine)
    imag = jnp.where(odd, cosine, sine)
    real = jnp.where(((quadrant + 1) & 2) == 2, -real, real)
    imag = jnp.where((quadrant & 2) == 2, -imag, imag)
    return real, imag


def times(a, b):
    return a[0] * b[0] - a[1] * b[1], a[0] * b[1] + a[1] * b[0]


def table_kernel_part(copy, position_hbm, steering_hbm, position, steering, small_arrivals, offset_tables, centre_tables, own_beams):
    feeds, beams = offset_tables.shape[2:]
    centres = centre_tables.shape[1]
    here = lax.axis_index("chan")
    position_copy = pltpu.make_async_copy(position_hbm, position, small_arrivals.at[0])
    steering_copy = pltpu.make_async_copy(steering_hbm, steering, small_arrivals.at[1])
    position_copy.start()
    steering_copy.start()
    copy.start()
    position_copy.wait()
    steering_copy.wait()

    def column(axis):
        start = here * feeds if position.shape[1] > feeds else 0
        row = position[axis : axis + 1, pl.ds(pl.multiple_of(start, LANES), feeds)].astype(jnp.float32)
        return jnp.transpose(jnp.broadcast_to(row, (beams, feeds))).astype(jnp.int32)

    lane = lax.broadcasted_iota(jnp.int32, steering.shape, 1)
    aim = steering[...]
    size = own_beams
    while size < beams:
        upper = (lane & size) != 0
        swapped = jnp.where(upper, pltpu.roll(aim, size, 1), pltpu.roll(aim, beams - size, 1))
        aim = jnp.where((here & (size // own_beams)) != 0, swapped, aim)
        size *= 2
    total = column(0) * aim[0:1, :] + column(1) * aim[1:2, :]
    offset_tables[0, 0] = (total & (PHASES - 1)).astype(TABLE)

    def one_slab(index, carry):
        at = pl.multiple_of(index * SLAB, SLAB)
        delay = offset_tables[0, 0, pl.ds(at, SLAB), :].astype(jnp.int32)
        half_step = turn(delay, 2 * PHASES)
        state = half_step
        advance = times(half_step, half_step)
        for offset in range(HALF):
            offset_tables[0, offset, pl.ds(at, SLAB), :] = state[0].astype(TABLE)
            offset_tables[1, offset, pl.ds(at, SLAB), :] = state[1].astype(TABLE)
            if offset + 1 < HALF:
                state = times(state, advance)
        state = turn(((2 * HALF - 1) * delay) & (2 * PHASES - 1), 2 * PHASES)
        advance = turn((4 * HALF * delay) & (2 * PHASES - 1), 2 * PHASES)
        for centre in range(centres):
            centre_tables[0, centre, pl.ds(at, SLAB), :] = state[0].astype(TABLE)
            centre_tables[1, centre, pl.ds(at, SLAB), :] = state[1].astype(TABLE)
            if centre + 1 < centres:
                state = times(state, advance)
        return carry

    lax.fori_loop(0, feeds // SLAB, one_slab, 0)


def beam_kernel(first, make_tables, *refs):
    if make_tables:
        position_hbm, steering_hbm, voltages, keep, send, offset_tables, centre_tables, staged = refs[:8]
        position, steering, small_arrivals, arrivals = refs[8:12]
    else:
        offset_tables, centre_tables, staged, keep, send = refs[:5]
    both_rows, both_sums = refs[-2:]
    feeds, beams = offset_tables.shape[2:]
    frames = staged.shape[1]
    stride = 2 * frames
    block = LANES
    devices = 2 * keep.shape[0]
    own_beams = beams // devices
    before = first // block
    blocks = keep.shape[4] // block

    if make_tables:
        copy = pltpu.make_async_copy(voltages, staged, arrivals.at[0])
        table_kernel_part(copy, position_hbm, steering_hbm, position, steering, small_arrivals, offset_tables, centre_tables, own_beams)
        copy.wait()

    width = min(feeds, LANES)
    scale = 1.0 / math.sqrt(feeds * devices)
    sign = jnp.where(lax.broadcasted_iota(jnp.int32, (stride, beams), 0) < frames, -1.0, 1.0)

    def take(index, rows, slot):
        for at in range(feeds // width):
            lanes = pl.ds(pl.multiple_of((before + index) * block, block), block)
            piece = staged[slot // frames, slot % frames, at * width : (at + 1) * width, lanes].astype(jnp.float32)
            if width < LANES:
                piece = jnp.concatenate([piece, jnp.zeros((LANES - width, block), jnp.float32)], axis=0)
            rows[at, pl.ds(slot, block, stride=stride), :] = jnp.transpose(piece)

    def give(index, sums, slot):
        piece = jnp.transpose(sums[pl.ds(slot, block, stride=stride), :] * scale)
        for relative in range(devices):
            value = piece[relative * own_beams : (relative + 1) * own_beams, :].astype(jnp.bfloat16)
            out = send if relative % 2 else keep
            out[relative // 2, slot % frames, slot // frames, :, pl.ds(pl.multiple_of(index * block, block), block)] = value

    def quarter_turn(value):
        return pltpu.roll(value, frames, 0) * sign

    def dot(a, b):
        return jnp.dot(a, b, preferred_element_type=jnp.float32)

    def lhs(rows, local, offset):
        upper = local * 2 * HALF + HALF + offset
        lower = local * 2 * HALF + HALF - 1 - offset
        pieces = []
        for at in range(feeds // width):
            top = rows[at, upper * stride : (upper + 1) * stride, :]
            bottom = rows[at, lower * stride : (lower + 1) * stride, :]
            pieces.append(jnp.concatenate([top, bottom], axis=0))
        return jnp.concatenate(pieces, axis=1).astype(jnp.bfloat16)[:, :feeds]

    def pair(left, sums, cosine, sine, local, offset):
        upper = local * 2 * HALF + HALF + offset
        lower = local * 2 * HALF + HALF - 1 - offset
        small_cosine = offset_tables[0, offset].astype(jnp.bfloat16)
        small_sine = offset_tables[1, offset].astype(jnp.bfloat16)
        straight = dot(left, jnp.concatenate([cosine * small_cosine, sine * small_sine], axis=1))
        crossed = dot(left, jnp.concatenate([sine * small_cosine, cosine * small_sine], axis=1))
        a, b, c, d = straight[:, :beams], straight[:, beams:], crossed[:, :beams], crossed[:, beams:]
        more = quarter_turn(c[:stride] + d[:stride])
        less = quarter_turn(c[stride:] - d[stride:])
        sums[upper * stride : (upper + 1) * stride, :] = a[:stride] - b[:stride] + more
        sums[lower * stride : (lower + 1) * stride, :] = a[stride:] + b[stride:] + less

    def one_block(index, parity):
        rows, sums = both_rows.at[parity], both_sums.at[parity]
        other_rows, other_sums = both_rows.at[1 - parity], both_sums.at[1 - parity]
        locals_ = block // (2 * HALF)
        every = HALF * locals_ // stride
        lefts = [(local, offset) for local in range(locals_) for offset in range(HALF)]
        ready = [lhs(rows, *at) for at in lefts[:AHEAD]]
        for count, (local, offset) in enumerate(lefts):
            if offset == 0:
                centre = (before + index) * locals_ + local
                cosine = centre_tables[0, centre].astype(jnp.bfloat16)
                sine = centre_tables[1, centre].astype(jnp.bfloat16)
            if count % every == 0:
                give(jnp.maximum(index - 1, 0), other_sums, count // every)
                take(jnp.minimum(index + 1, blocks - 1), other_rows, count // every)
            if count + AHEAD < len(lefts):
                ready.append(lhs(rows, *lefts[count + AHEAD]))
            pair(ready[count], sums, cosine, sine, local, offset)

    for slot in range(stride):
        take(0, both_rows.at[0], slot)

    def two_blocks(index, carry):
        one_block(2 * index, 0)
        one_block(2 * index + 1, 1)
        return carry

    lax.fori_loop(0, blocks // 2, two_blocks, 0)
    if blocks % 2:
        one_block(blocks - 1, 0)
    for slot in range(stride):
        give(blocks - 1, both_sums.at[(blocks - 1) & 1], slot)


def beamform(voltages, position, steering, devices, first, count, tables):
    _, frames, feeds, channels = voltages.shape
    beams = steering.shape[1]
    width = min(feeds, LANES)
    shape = jax.ShapeDtypeStruct((devices // 2, frames, 2, beams // devices, count), jnp.bfloat16)
    rows = pltpu.VMEM((2, feeds // width, LANES * 2 * frames, LANES), jnp.float32)
    sums = pltpu.VMEM((2, LANES * 2 * frames, beams), jnp.float32)
    work = 2 * frames * 2 * feeds * beams * count
    whole = pl.BlockSpec(memory_space=pltpu.VMEM)
    anywhere = pl.BlockSpec(memory_space=pltpu.HBM)
    out_shape = [shape, shape]
    scratch = []
    if tables is None:
        out_shape += [
            jax.ShapeDtypeStruct((2, HALF, feeds, beams), TABLE),
            jax.ShapeDtypeStruct((2, channels // (2 * HALF), feeds, beams), TABLE),
            jax.ShapeDtypeStruct(voltages.shape, jnp.bfloat16),
        ]
        scratch += [
            pltpu.VMEM(position.shape, jnp.int32),
            pltpu.VMEM(steering.shape, jnp.int32),
            pltpu.SemaphoreType.DMA((2,)),
            pltpu.SemaphoreType.DMA((1,)),
        ]
        position = pltpu.with_memory_space_constraint(position, pltpu.HBM)
        steering = pltpu.with_memory_space_constraint(steering, pltpu.HBM)
        args, in_specs = (position, steering, voltages), [anywhere] * 3
    else:
        args, in_specs = tables, [whole] * 3
    out = pl.pallas_call(
        functools.partial(beam_kernel, first, tables is None),
        in_specs=in_specs,
        out_specs=[whole] * len(out_shape),
        out_shape=out_shape,
        scratch_shapes=scratch
        + [rows, sums],
        compiler_params=pltpu.CompilerParams(vmem_limit_bytes=BEAM_LIMIT * 2**20),
        cost_estimate=pl.CostEstimate(flops=32 * work, bytes_accessed=4 * 2 * frames * feeds * count, transcendentals=0),
        name="beam",
    )(*args)
    return out[0], out[1], out[2:] if tables is None else tables


def basis_kernel(basis, small):
    channels = basis.shape[0]
    width = small.shape[2]
    group = small.shape[1]

    def one_slab(index, carry):
        first = pl.multiple_of(index * width, width)

        def phases(rows, factor):
            row = lax.broadcasted_iota(jnp.int32, (rows, width), 0) * factor
            column = first + lax.broadcasted_iota(jnp.int32, (rows, width), 1)
            return (row * column) & (channels - 1)

        small[0], small[1] = turn(phases(group, 1), channels)
        count = channels // group
        large = turn(phases(count, group), channels)
        for at in range(count):
            real, imag = times((large[0][at : at + 1], large[1][at : at + 1]), (small[0], small[1]))
            basis[at * group : (at + 1) * group, pl.ds(first, width)] = real.astype(jnp.bfloat16)
            basis[at * group : (at + 1) * group, pl.ds(pl.multiple_of(channels + first, width), width)] = imag.astype(jnp.bfloat16)
        return carry

    lax.fori_loop(0, channels // width, one_slab, 0)


def make_basis(channels):
    return pl.pallas_call(
        basis_kernel,
        out_specs=pl.BlockSpec(memory_space=pltpu.VMEM),
        out_shape=jax.ShapeDtypeStruct((channels, 2 * channels), jnp.bfloat16),
        scratch_shapes=[pltpu.VMEM((2, 32, 256), jnp.float32)],
        compiler_params=pltpu.CompilerParams(vmem_limit_bytes=8 * 2**20),
        cost_estimate=pl.CostEstimate(flops=2**30, bytes_accessed=4 * channels * channels, transcendentals=0),
        name="basis",
    )()


def transform(pieces, starts, basis, first, width):
    frames, _, beams, _ = pieces[0].shape
    channels = basis.shape[0]
    total = None
    for piece, start in zip(pieces, starts):
        count = piece.shape[3]
        rows = jnp.concatenate([piece[t, part] for part in range(2) for t in range(frames)], axis=0)
        for part in range(2):
            columns = pl.ds(pl.multiple_of(part * channels + first, width), width)
            product = jnp.dot(rows, basis[start : start + count, columns], preferred_element_type=jnp.float32)
            total = [None, None] if total is None else total
            total[part] = product if total[part] is None else total[part] + product
    half = frames * beams
    return total[0][:half] - total[1][half:], total[1][:half] + total[0][half:]


def own_kernel(starts, *refs):
    pieces, basis, taps, out = refs[:-3], refs[-3], refs[-2], refs[-1]
    frames, _, beams, _ = pieces[0].shape
    channels = basis.shape[0]
    width = min(256, channels)
    scale = 1.0 / math.sqrt(channels)

    def one_slab(index, carry):
        first = pl.multiple_of(index * width, width)
        for part, value in enumerate(transform(pieces, starts, basis, first, width)):
            value = (value * scale).astype(jnp.bfloat16).astype(jnp.float32)
            for t in range(frames):
                total = None
                for k in range(min(t + 1, taps.shape[0])):
                    term = taps[k : k + 1, pl.ds(first, width)] * value[(t - k) * beams : (t - k + 1) * beams]
                    total = term if total is None else total + term
                out[part, t, :, pl.ds(first, width)] = total
        return carry

    lax.fori_loop(0, channels // width, one_slab, 0)


def halo_kernel(starts, *refs):
    pieces, basis, out = refs[:-2], refs[-2], refs[-1]
    channels = basis.shape[0]
    width = min(256, channels)

    def one_slab(index, carry):
        first = pl.multiple_of(index * width, width)
        for part, value in enumerate(transform(pieces, starts, basis, first, width)):
            out[part, :, pl.ds(first, width)] = value
        return carry

    lax.fori_loop(0, channels // width, one_slab, 0)


def taps_kernel(starts, *refs):
    pieces, others, own, basis, taps, out, turned = refs[:-6], refs[-6], refs[-5], refs[-4], refs[-3], refs[-2], refs[-1]
    before, _, beams, _ = pieces[0].shape
    channels = basis.shape[0]
    frames = own.shape[1]
    width = min(256, channels)
    scale = 1.0 / math.sqrt(channels)

    def one_slab(index, carry):
        first = pl.multiple_of(index * width, width)
        lanes = pl.ds(first, width)
        for part, value in enumerate(transform(pieces, starts, basis, first, width)):
            value = ((value + others[part, :, lanes]) * scale).astype(jnp.bfloat16).astype(jnp.float32)
            for t in range(frames):
                total = own[part, t, :, lanes]
                for k in range(t + 1, taps.shape[0]):
                    at = before + t - k
                    total = total + taps[k : k + 1, lanes] * value[at * beams : (at + 1) * beams]
                for at in range(width // LANES):
                    turned[part, at, pl.ds(t, beams, stride=frames), :] = total[:, at * LANES : (at + 1) * LANES]
            for at in range(width // LANES):
                start = pl.multiple_of(first + at * LANES, LANES)
                out[part, :, :, pl.ds(start, LANES)] = turned[part, at].reshape(beams, frames, LANES).astype(jnp.bfloat16)
        return carry

    lax.fori_loop(0, channels // width, one_slab, 0)


def small_call(kernel, rows, args, out_shape, scratch=()):
    channels = out_shape.shape[-1]
    whole = pl.BlockSpec(memory_space=pltpu.VMEM)
    return pl.pallas_call(
        kernel,
        in_specs=[whole] * len(args),
        out_specs=whole,
        out_shape=out_shape,
        scratch_shapes=scratch,
        compiler_params=pltpu.CompilerParams(vmem_limit_bytes=12 * 2**20),
        cost_estimate=pl.CostEstimate(flops=8 * rows * channels**2, bytes_accessed=4 * channels**2, transcendentals=0),
    )(*args)


def added(*terms):
    return sum(term.astype(jnp.float32) for term in terms).astype(jnp.bfloat16)


def steps_on_device(voltages, feed_position, beam_steering, synthesis_taps):
    devices = lax.axis_size("chan")
    steps = lax.axis_size("tm")
    taps = synthesis_taps.shape[0]
    feeds = voltages.shape[2]
    position = feed_position.T
    if feeds % LANES:
        position = lax.dynamic_slice_in_dim(position, lax.axis_index("chan") * feeds, feeds, 1)
    channels = voltages.shape[3]
    later = max(1, 3 * channels // (8 * LANES)) * LANES
    parts = [(0, channels - later), (channels - later, later)]
    basis = make_basis(channels)
    steering = beam_steering.T
    owns = []
    halos = []

    def across(value, mask):
        return lax.ppermute(value, "chan", [(i, i ^ mask) for i in range(devices)])

    def last_stage(keep, send):
        terms = [keep]
        mask = 1
        while 2 * mask < devices:
            terms.append(across(send, mask))
            send = added(*[term[1::2] for term in terms])
            terms = [term[0::2] for term in terms]
            mask *= 2
        return send, terms, mask

    def ended(terms, arrived):
        own = added(*[term[0] for term in terms], arrived[0])
        return own, lax.ppermute(own[own.shape[0] - (taps - 1) :], "tm", [(i, i + 1) for i in range(steps - 1)])

    waiting = None
    voltages = pltpu.with_memory_space_constraint(voltages, pltpu.HBM)
    waiting = None
    tables = None
    for part in parts:
        if waiting is not None:
            tables, send = lax.optimization_barrier((tables, waiting[1]))
            waiting = (waiting[0], send, waiting[2])
            waiting = (waiting[0], across(*waiting[1:]))
        keep, send, tables = beamform(voltages, position, steering, devices, *part, tables)
        send, terms, mask = last_stage(keep, send)
        if waiting is not None:
            arrived, send = lax.optimization_barrier((waiting[1], send))
            own, halo = ended(waiting[0], arrived)
            owns.append(own)
            halos.append(halo)
        waiting = (terms, send, mask)
    own, halo = ended(waiting[0], across(*waiting[1:]))
    owns.append(own)
    halos.append(halo)
    starts = [start for start, _ in parts]
    frames, _, beams, _ = own.shape
    before = taps - 1
    single = jnp.float32
    sums = jax.ShapeDtypeStruct((2, frames, beams, channels), single)
    filtered = small_call(functools.partial(own_kernel, starts), frames * beams, (*owns, basis, synthesis_taps), sums)
    part_sums = jax.ShapeDtypeStruct((2, before * beams, channels), single)
    others = small_call(functools.partial(halo_kernel, starts[:-1]), before * beams, (*halos[:-1], basis), part_sums)
    out_shape = jax.ShapeDtypeStruct((2, beams, frames, channels), jnp.bfloat16)
    turned = pltpu.VMEM((2, 256 // LANES, frames * beams, LANES), single)
    args = (*halos[-1:], others, filtered, basis, synthesis_taps)
    return small_call(functools.partial(taps_kernel, starts[-1:]), before * beams, args, out_shape, [turned])


def solution(mesh):
    return jax.shard_map(
        steps_on_device,
        mesh=mesh,
        in_specs=(P(None, ("group", "tm"), "chan", None), P(), P("group", None), P()),
        out_specs=P(None, "chan", ("group", "tm"), None),
        check_vma=False,
    )
```

time: 56.8 us -> 52.5 us (0.924)
  waiting for transfers between devices: 12 us -> 9.26 us
  local copies, waits for them, and re-layouts: 2.61 us -> 0.05 us
  Pallas kernels: 29.2 us -> 30.2 us
    ppermute x2, waiting for transfers between devices: 2.32 us -> 0.01 us  [ended(): lax.ppermute(own[own.shape[0] - (taps - 1):], 'tm', [(i, i + 1) for i in...]
    unnamed x6 -> x2, local copies, waits for them, and re-layouts: 1.38 us -> 0.01 us
    transpose x1 -> x0, local copies, waits for them, and re-layouts: 1.2 us -> none  [steps_on_device(): return jnp.transpose(out, (0, 2, 1, 3))]
    pallas_call x4 -> x5, Pallas kernels: 27.4 us -> 28.3 us  [the longest x2 22.9 us: beamform(): pl.pallas_call(functools.partial(beam_kernel, first, tables is None), in_...]
  transfers between devices with their start and end apart: 6 -> 6, of which waited for: 3 -> 3; matrix products, arithmetic and copies ran while one was open for 0% -> 1% of each run, Pallas kernels for 7% -> 10%
where the time goes in v4:
time: 52.5 us; the launch traced here: 52.3 us
  Pallas kernels  30.2 us (58%)
  starting transfers between devices  12.3 us (23%)
  waiting for transfers between devices  9.26 us (18%)
    pallas_call x2, Pallas kernels, beamform(): pl.pallas_call(functools.partial(beam_kernel, first, tables is None), in_...  22.9 us
    ppermute x4, waiting for transfers between devices, across(): return lax.ppermute(value, 'chan', [(i, i ^ mask) for i in range(devices)])  9.25 us
    ppermute x2, starting transfers between devices, ended(): lax.ppermute(own[own.shape[0] - (taps - 1):], 'tm', [(i, i + 1) for i in...  6.96 us
    pallas_call x3, Pallas kernels, small_call(): pl.pallas_call(kernel, in_specs=[whole] * len(args), out_specs=whole, out...  5.5 us
    ppermute x4, starting transfers between devices, across(): return lax.ppermute(value, 'chan', [(i, i ^ mask) for i in range(devices)])  5.35 us
    pallas_call x1, Pallas kernels, make_basis(): pl.pallas_call(basis_kernel, out_specs=pl.BlockSpec(memory_space=pltpu.VM...  1.84 us
  transfers between devices with their start and end apart: 6, of which 3 were waited for; matrix products, arithmetic and copies ran while one was open for 1% of the time, Pallas kernels for 10%

profile of v4, /device:TPU:0, one launch (start us, length us, event | category | flops | bytes accessed | tf_op | source)
XLA Modules:
  0.0 52.3 jit_solution(3195301705714737877)
XLA Ops:
  0.0 15.4 %beam.2 = (bf16[2,4,2,32,640]{4,3,2,1,0:T(8,128)(2,1)S(1)}, bf16[2,4,2,32,640]{4,3,2,1,0:T(8,128)(2,1)S(1)}, f32[2,32,256,128]{3,2,1,0:T(8,128)S(1)}, f32[2,16,2...) custom-call(s32[2,1024]{1,0:T(2,128)} %bitcast.10, s32[2,128]{1,0:T(2,128)} %bitcast.11, bf16[2,4,256,1024]{3,2,1,0:T(8,128)(2,1)} %refs_2_.1), custom_call_target="tpu_custom_call" | custom-call | flops 10737418240 | bytes 5242880 | tf_op jit(solution)/shard_map/beam/pallas_call | solution.py:224
  15.4 0.6 %collective-permute-start = (bf16[2,4,2,32,640]{4,3,2,1,0:T(8,128)(2,1)S(1)}, bf16[2,4,2,32,640]{4,3,2,1,0:T(8,128)(2,1)S(1)}, u32[]{:S(2)}, u32[]{:S(2)}) collective-permute-start(bf16[2,4,2,32,640]{4,3,2,1,0:T(8,128)(2,1)S(1)} %get-tuple-element.22), channel_id=1, source_target_pairs={{0,4},{4,0},{8,12},{12,8},{1,5},{5,1},{9,13},{13,9},{2,6},{6,2},{1... | collective-permute-start | bytes 1966088 | tf_op jit(solution)/shard_map/ppermute | solution.py:390
  16.0 1.7 %collective-permute-done = bf16[2,4,2,32,640]{4,3,2,1,0:T(8,128)(2,1)S(1)} collective-permute-done((bf16[2,4,2,32,640]{4,3,2,1,0:T(8,128)(2,1)S(1)}, bf16[2,4,2,32,640]{4,3,2,1,0:T(8,128)(2,1)S(1)}, u32[]{:S(2)}, u32[]{:S(2)}) %collective-permute-start) | collective-permute-done | bytes 655392 | tf_op jit(solution)/shard_map/ppermute | solution.py:390
  17.7 0.1 add_convert_fusion.1
  17.8 7.4 %beam.3 = (bf16[2,4,2,32,384]{4,3,2,1,0:T(8,128)(2,1)S(1)}, bf16[2,4,2,32,384]{4,3,2,1,0:T(8,128)(2,1)S(1)}) custom-call(f32[2,32,256,128]{3,2,1,0:T(8,128)S(1)} %get-tuple-element.23.refs_0_, f32[2,16,256,128]{3,2,1,0:T(8,128)S(1)} %get-tuple-element.24.refs_1_, bf16[2,4,256,1024]{3,2,1,0:T(8,128)(2,1)S(1)} %get-tuple-element.25.refs_2_), custom_call_target="tpu_custom_call" | custom-call | flops 6442450944 | bytes 3145728 | tf_op jit(solution)/shard_map/beam/pallas_call | solution.py:224
  25.2 0.0 copy-start
  25.2 0.4 collective-permute-start.1
  25.7 2.6 %collective-permute-start.2 = (bf16[1,4,2,32,640]{4,3,2,1,0:T(8,128)(2,1)S(1)}, bf16[1,4,2,32,640]{4,3,2,1,0:T(8,128)(2,1)S(1)}, u32[]{:S(2)}, u32[]{:S(2)}) collective-permute-start(bf16[1,4,2,32,640]{4,3,2,1,0:T(8,128)(2,1)S(1)} %add_convert_fusion.1), channel_id=1, source_target_pairs={{0,8},{4,12},{8,0},{12,4},{1,9},{5,13},{9,1},{13,5},{2,10},{6,14},... | collective-permute-start | bytes 983048 | tf_op jit(solution)/shard_map/ppermute | solution.py:390
  28.3 1.8 %basis.1.refs_1_.refs_2_.refs_3_ = bf16[1024,2048]{1,0:T(8,128)(2,1)S(1)} custom-call(), custom_call_target="tpu_custom_call" | custom-call | flops 1073741824 | bytes 4194304 | tf_op jit(solution)/shard_map/basis/pallas_call | solution.py:264
  30.2 0.0 collective-permute-done.1
  30.2 0.1 add_convert_fusion.3
  30.2 6.3 %collective-permute-done.2 = bf16[1,4,2,32,640]{4,3,2,1,0:T(8,128)(2,1)S(1)} collective-permute-done((bf16[1,4,2,32,640]{4,3,2,1,0:T(8,128)(2,1)S(1)}, bf16[1,4,2,32,640]{4,3,2,1,0:T(8,128)(2,1)S(1)}, u32[]{:S(2)}, u32[]{:S(2)}) %collective-permute-start.2) | collective-permute-done | bytes 327712 | tf_op jit(solution)/shard_map/ppermute | solution.py:390
  36.5 1.7 %collective-permute-start.3 = (bf16[1,4,2,32,384]{4,3,2,1,0:T(8,128)(2,1)S(1)}, bf16[1,4,2,32,384]{4,3,2,1,0:T(8,128)(2,1)S(1)}, u32[]{:S(2)}, u32[]{:S(2)}) collective-permute-start(bf16[1,4,2,32,384]{4,3,2,1,0:T(8,128)(2,1)S(1)} %add_convert_fusion.3), channel_id=1, source_target_pairs={{0,8},{4,12},{8,0},{12,4},{1,9},{5,13},{9,1},{13,5},{2,10},{6,14},... | collective-permute-start | bytes 589832 | tf_op jit(solution)/shard_map/ppermute | solution.py:390
  38.3 0.1 add_convert_fusion
  38.4 3.5 %collective-permute-start.5 = (bf16[3,2,32,640]{3,2,1,0:T(8,128)(2,1)S(1)}, bf16[3,2,32,640]{3,2,1,0:T(8,128)(2,1)S(1)}, u32[]{:S(2)}, u32[]{:S(2)}) collective-permute-start(bf16[3,2,32,640]{3,2,1,0:T(8,128)(2,1)S(1)} %slice_bitcast_fusion), channel_id=1, source_target_pairs={{0,1},{1,2},{2,3},{4,5},{5,6},{6,7},{8,9},{9,10},{10,11},{12,13},{... | collective-permute-start | bytes 737288 | tf_op jit(solution)/shard_map/ppermute | solution.py:404
  41.9 1.2 %collective-permute-done.3 = bf16[1,4,2,32,384]{4,3,2,1,0:T(8,128)(2,1)S(1)} collective-permute-done((bf16[1,4,2,32,384]{4,3,2,1,0:T(8,128)(2,1)S(1)}, bf16[1,4,2,32,384]{4,3,2,1,0:T(8,128)(2,1)S(1)}, u32[]{:S(2)}, u32[]{:S(2)}) %collective-permute-start.3) | collective-permute-done | bytes 196640 | tf_op jit(solution)/shard_map/ppermute | solution.py:390
  43.2 0.1 add_convert_fusion.2
  43.3 3.5 %collective-permute-start.4 = (bf16[3,2,32,384]{3,2,1,0:T(8,128)(2,1)S(1)}, bf16[3,2,32,384]{3,2,1,0:T(8,128)(2,1)S(1)}, u32[]{:S(2)}, u32[]{:S(2)}) collective-permute-start(bf16[3,2,32,384]{3,2,1,0:T(8,128)(2,1)S(1)} %slice_bitcast_fusion.1), channel_id=1, source_target_pairs={{0,1},{1,2},{2,3},{4,5},{5,6},{6,7},{8,9},{9,10},{10,11},{12,13},{... | collective-permute-start | bytes 442376 | tf_op jit(solution)/shard_map/ppermute | solution.py:404
  46.7 0.0 copy-done
  46.7 2.1 %shard_map.47.refs_2_ = f32[2,4,32,1024]{3,2,1,0:T(8,128)S(1)} custom-call(bf16[4,2,32,640]{3,2,1,0:T(8,128)(2,1)S(1)} %bitcast.8, bf16[4,2,32,384]{3,2,1,0:T(8,128)(2,1)S(1)} %bitcast.9, bf16[1024,2048]{1,0:T(8,128)(2,1)S(1)} %basis.1.refs_1_.refs_2_.refs_3_, f32[4,1024]{1,0:T(4,128)S(1)} %copy-done), custom_call_target="tpu_custom_call" | custom-call | flops 1073741824 | bytes 4194304 | tf_op jit(solution)/shard_map/pallas_call | solution.py:358
  48.8 0.0 collective-permute-done.5.refs_0_
  48.9 1.2 %shard_map.46.refs_1_ = f32[2,96,1024]{2,1,0:T(8,128)S(1)} custom-call(bf16[3,2,32,640]{3,2,1,0:T(8,128)(2,1)S(1)} %collective-permute-done.5.refs_0_, bf16[1024,2048]{1,0:T(8,128)(2,1)S(1)} %basis.1.refs_1_.refs_2_.refs_3_), custom_call_target="tpu_custom_call" | custom-call | flops 805306368 | bytes 4194304 | tf_op jit(solution)/shard_map/pallas_call | solution.py:358
  50.1 0.0 collective-permute-done.4.refs_0_
  50.1 2.2 %shard_map.48 = bf16[2,32,4,1024]{3,2,1,0:T(4,128)(2,1)} custom-call(bf16[3,2,32,384]{3,2,1,0:T(8,128)(2,1)S(1)} %collective-permute-done.4.refs_0_, f32[2,96,1024]{2,1,0:T(8,128)S(1)} %shard_map.46.refs_1_, f32[2,4,32,1024]{3,2,1,0:T(8,128)S(1)} %shard_map.47.refs_2_, bf16[1024,2048]{1,0:T(8,128)(2,1)S(1)} %basis.1.refs_1_.refs_2_.refs_3_, ...), custom_call_target="tpu_custom_call" | custom-call | flops 805306368 | bytes 4194304 | tf_op jit(solution)/shard_map/pallas_call | solution.py:358
  (2 shorter events, 0.0 us)
Async XLA Ops:
  15.4 2.3 %collective-permute-start = (bf16[2,4,2,32,640]{4,3,2,1,0:T(8,128)(2,1)S(1)}, bf16[2,4,2,32,640]{4,3,2,1,0:T(8,128)(2,1)S(1)}, u32[]{:S(2)}, u32[]{:S(2)}) collective-permute-start(bf16[2,4,2,32,640]{4,3,2,1,0:T(8,128)(2,1)S(1)} %get-tuple-element.22), channel_id=1, source_target_pairs={{0,4},{4,0},{8,12},{12,8},{1,5},{5,1},{9,13},{13,9},{2,6},{6,2},{1... | collective-permute-start | bytes 1966088 | tf_op jit(solution)/shard_map/ppermute | solution.py:390
  25.2 21.5 %copy-start = (f32[4,1024]{1,0:T(4,128)S(1)}, f32[4,1024]{1,0:T(4,128)}, u32[]{:S(2)}) copy-start(f32[4,1024]{1,0:T(4,128)} %refs_4_.1) | copy-start | bytes 49156
  25.2 4.9 %collective-permute-start.1 = (bf16[2,4,2,32,384]{4,3,2,1,0:T(8,128)(2,1)S(1)}, bf16[2,4,2,32,384]{4,3,2,1,0:T(8,128)(2,1)S(1)}, u32[]{:S(2)}, u32[]{:S(2)}) collective-permute-start(bf16[2,4,2,32,384]{4,3,2,1,0:T(8,128)(2,1)S(1)} %get-tuple-element.27), channel_id=1, source_target_pairs={{0,4},{4,0},{8,12},{12,8},{1,5},{5,1},{9,13},{13,9},{2,6},{6,2},{1... | collective-permute-start | bytes 1179656 | tf_op jit(solution)/shard_map/ppermute | solution.py:390
  25.7 10.9 %collective-permute-start.2 = (bf16[1,4,2,32,640]{4,3,2,1,0:T(8,128)(2,1)S(1)}, bf16[1,4,2,32,640]{4,3,2,1,0:T(8,128)(2,1)S(1)}, u32[]{:S(2)}, u32[]{:S(2)}) collective-permute-start(bf16[1,4,2,32,640]{4,3,2,1,0:T(8,128)(2,1)S(1)} %add_convert_fusion.1), channel_id=1, source_target_pairs={{0,8},{4,12},{8,0},{12,4},{1,9},{5,13},{9,1},{13,5},{2,10},{6,14},... | collective-permute-start | bytes 983048 | tf_op jit(solution)/shard_map/ppermute | solution.py:390
  36.5 6.6 %collective-permute-start.3 = (bf16[1,4,2,32,384]{4,3,2,1,0:T(8,128)(2,1)S(1)}, bf16[1,4,2,32,384]{4,3,2,1,0:T(8,128)(2,1)S(1)}, u32[]{:S(2)}, u32[]{:S(2)}) collective-permute-start(bf16[1,4,2,32,384]{4,3,2,1,0:T(8,128)(2,1)S(1)} %add_convert_fusion.3), channel_id=1, source_target_pairs={{0,8},{4,12},{8,0},{12,4},{1,9},{5,13},{9,1},{13,5},{2,10},{6,14},... | collective-permute-start | bytes 589832 | tf_op jit(solution)/shard_map/ppermute | solution.py:390
  38.4 10.4 %collective-permute-start.5 = (bf16[3,2,32,640]{3,2,1,0:T(8,128)(2,1)S(1)}, bf16[3,2,32,640]{3,2,1,0:T(8,128)(2,1)S(1)}, u32[]{:S(2)}, u32[]{:S(2)}) collective-permute-start(bf16[3,2,32,640]{3,2,1,0:T(8,128)(2,1)S(1)} %slice_bitcast_fusion), channel_id=1, source_target_pairs={{0,1},{1,2},{2,3},{4,5},{5,6},{6,7},{8,9},{9,10},{10,11},{12,13},{... | collective-permute-start | bytes 737288 | tf_op jit(solution)/shard_map/ppermute | solution.py:404
  43.3 6.8 %collective-permute-start.4 = (bf16[3,2,32,384]{3,2,1,0:T(8,128)(2,1)S(1)}, bf16[3,2,32,384]{3,2,1,0:T(8,128)(2,1)S(1)}, u32[]{:S(2)}, u32[]{:S(2)}) collective-permute-start(bf16[3,2,32,384]{3,2,1,0:T(8,128)(2,1)S(1)} %slice_bitcast_fusion.1), channel_id=1, source_target_pairs={{0,1},{1,2},{2,3},{4,5},{5,6},{6,7},{8,9},{9,10},{10,11},{12,13},{... | collective-permute-start | bytes 442376 | tf_op jit(solution)/shard_map/ppermute | solution.py:404

commit v5 on v4

--- a/solution.py
+++ b/solution.py
@@ -280,7 +280,8 @@
         count = piece.shape[3]
         rows = jnp.concatenate([piece[t, part] for part in range(2) for t in range(frames)], axis=0)
         for part in range(2):
-            columns = pl.ds(pl.multiple_of(part * channels + first, width), width)
+            column = part * channels + first
+            columns = pl.ds(column if isinstance(column, int) else pl.multiple_of(column, width), width)
             product = jnp.dot(rows, basis[start : start + count, columns], preferred_element_type=jnp.float32)
             total = [None, None] if total is None else total
             total[part] = product if total[part] is None else total[part] + product
@@ -289,7 +290,7 @@
 
 
 def own_kernel(starts, *refs):
-    pieces, basis, taps, out = refs[:-3], refs[-3], refs[-2], refs[-1]
+    pieces, others, basis, taps, out = refs[:-4], refs[-4], refs[-3], refs[-2], refs[-1]
     frames, _, beams, _ = pieces[0].shape
     channels = basis.shape[0]
     width = min(256, channels)
@@ -298,7 +299,7 @@
     def one_slab(index, carry):
         first = pl.multiple_of(index * width, width)
         for part, value in enumerate(transform(pieces, starts, basis, first, width)):
-            value = (value * scale).astype(jnp.bfloat16).astype(jnp.float32)
+            value = ((value + others[part, :, pl.ds(first, width)]) * scale).astype(jnp.bfloat16).astype(jnp.float32)
             for t in range(frames):
                 total = None
                 for k in range(min(t + 1, taps.shape[0])):
@@ -310,7 +311,7 @@
     lax.fori_loop(0, channels // width, one_slab, 0)
 
 
-def halo_kernel(starts, *refs):
+def part_kernel(starts, wraps, *refs):
     pieces, basis, out = refs[:-2], refs[-2], refs[-1]
     channels = basis.shape[0]
     width = min(256, channels)
@@ -318,24 +319,29 @@
     def one_slab(index, carry):
         first = pl.multiple_of(index * width, width)
         for part, value in enumerate(transform(pieces, starts, basis, first, width)):
-            out[part, :, pl.ds(first, width)] = value
+            out[part, :, pl.ds(first, width)] = jnp.where(lax.axis_index("tm") == 0, 0.0, value) if wraps else value
         return carry
 
     lax.fori_loop(0, channels // width, one_slab, 0)
 
 
 def taps_kernel(starts, *refs):
-    pieces, others, own, basis, taps, out, turned = refs[:-6], refs[-6], refs[-5], refs[-4], refs[-3], refs[-2], refs[-1]
+    pieces, others, own, basis, taps, out = refs[:-8], refs[-8], refs[-7], refs[-6], refs[-5], refs[-4]
+    turned, result, departures = refs[-3:]
     before, _, beams, _ = pieces[0].shape
     channels = basis.shape[0]
     frames = own.shape[1]
-    width = min(256, channels)
+    slabs = departures.shape[0]
+    width = channels // slabs
     scale = 1.0 / math.sqrt(channels)
 
-    def one_slab(index, carry):
-        first = pl.multiple_of(index * width, width)
-        lanes = pl.ds(first, width)
-        for part, value in enumerate(transform(pieces, starts, basis, first, width)):
+    def departure(index):
+        lanes = pl.ds(index * width, width)
+        return pltpu.make_async_copy(result.at[index], out.at[:, :, :, lanes], departures.at[index])
+
+    for index in range(slabs):
+        lanes = pl.ds(index * width, width)
+        for part, value in enumerate(transform(pieces, starts, basis, index * width, width)):
             value = ((value + others[part, :, lanes]) * scale).astype(jnp.bfloat16).astype(jnp.float32)
             for t in range(frames):
                 total = own[part, t, :, lanes]
@@ -343,22 +349,22 @@
                     at = before + t - k
                     total = total + taps[k : k + 1, lanes] * value[at * beams : (at + 1) * beams]
                 for at in range(width // LANES):
-                    turned[part, at, pl.ds(t, beams, stride=frames), :] = total[:, at * LANES : (at + 1) * LANES]
+                    turned[index, part, at, pl.ds(t, beams, stride=frames), :] = total[:, at * LANES : (at + 1) * LANES]
             for at in range(width // LANES):
-                start = pl.multiple_of(first + at * LANES, LANES)
-                out[part, :, :, pl.ds(start, LANES)] = turned[part, at].reshape(beams, frames, LANES).astype(jnp.bfloat16)
-        return carry
-
-    lax.fori_loop(0, channels // width, one_slab, 0)
-
-
-def small_call(kernel, rows, args, out_shape, scratch=()):
+                value = turned[index, part, at].reshape(beams, frames, LANES).astype(jnp.bfloat16)
+                result[index, part, :, :, at * LANES : (at + 1) * LANES] = value
+        departure(index).start()
+    for index in range(slabs):
+        departure(index).wait()
+
+
+def small_call(kernel, rows, args, out_shape, scratch=(), space=pltpu.VMEM):
     channels = out_shape.shape[-1]
     whole = pl.BlockSpec(memory_space=pltpu.VMEM)
     return pl.pallas_call(
         kernel,
         in_specs=[whole] * len(args),
-        out_specs=whole,
+        out_specs=pl.BlockSpec(memory_space=space),
         out_shape=out_shape,
         scratch_shapes=scratch,
         compiler_params=pltpu.CompilerParams(vmem_limit_bytes=12 * 2**20),
@@ -374,6 +380,7 @@
     devices = lax.axis_size("chan")
     steps = lax.axis_size("tm")
     taps = synthesis_taps.shape[0]
+    before = taps - 1
     feeds = voltages.shape[2]
     position = feed_position.T
     if feeds % LANES:
@@ -399,42 +406,50 @@
             mask *= 2
         return send, terms, mask
 
-    def ended(terms, arrived):
-        own = added(*[term[0] for term in terms], arrived[0])
-        return own, lax.ppermute(own[own.shape[0] - (taps - 1) :], "tm", [(i, i + 1) for i in range(steps - 1)])
-
-    waiting = None
+    def ended(terms, arrived, hops):
+        own = lax.optimization_barrier(added(*[term[0] for term in terms], arrived[0]))
+        return own, lax.ppermute(own[own.shape[0] - before :], "tm", hops)
+
     voltages = pltpu.with_memory_space_constraint(voltages, pltpu.HBM)
-    waiting = None
-    tables = None
-    for part in parts:
-        if waiting is not None:
-            tables, send = lax.optimization_barrier((tables, waiting[1]))
-            waiting = (waiting[0], send, waiting[2])
-            waiting = (waiting[0], across(*waiting[1:]))
-        keep, send, tables = beamform(voltages, position, steering, devices, *part, tables)
-        send, terms, mask = last_stage(keep, send)
-        if waiting is not None:
-            arrived, send = lax.optimization_barrier((waiting[1], send))
-            own, halo = ended(waiting[0], arrived)
-            owns.append(own)
-            halos.append(halo)
-        waiting = (terms, send, mask)
-    own, halo = ended(waiting[0], across(*waiting[1:]))
+    split = voltages.shape[1] - before
+    keep, send, tables = beamform(voltages, position, steering, devices, *parts[0], None)
+    send, first_terms, mask = last_stage(keep, send)
+    tables, send = lax.optimization_barrier((tables, send))
+    arrived = across(send, mask)
+    keep, send, tables = beamform(voltages, position, steering, devices, *parts[1], tables)
+    send, terms, mask = last_stage(keep, send)
+    send, early = send[:, :split], send[:, split:]
+    arrived, early = lax.optimization_barrier((arrived, early))
+    early_arrived = across(early, mask)
+    own, halo = ended(first_terms, arrived, [(i, (i + 1) % steps) for i in range(steps)])
+    send, own = lax.optimization_barrier((send, own))
+    late_arrived = across(send, mask)
     owns.append(own)
     halos.append(halo)
+    own, halo = ended([term[:, split:] for term in terms], early_arrived, [(i, i + 1) for i in range(steps - 1)])
+    late = added(*[term[0, :split] for term in terms], late_arrived[0])
+    owns.append(jnp.concatenate([late, own], axis=0))
+    halos.append(halo)
+    own = owns[-1]
     starts = [start for start, _ in parts]
     frames, _, beams, _ = own.shape
-    before = taps - 1
     single = jnp.float32
     sums = jax.ShapeDtypeStruct((2, frames, beams, channels), single)
-    filtered = small_call(functools.partial(own_kernel, starts), frames * beams, (*owns, basis, synthesis_taps), sums)
+    own_sums = jax.ShapeDtypeStruct((2, frames * beams, channels), single)
+    others = small_call(functools.partial(part_kernel, starts[:-1], False), frames * beams, (*owns[:-1], basis), own_sums)
+    args = (*owns[-1:], others, basis, synthesis_taps)
+    filtered = small_call(functools.partial(own_kernel, starts[-1:]), frames * beams, args, sums)
     part_sums = jax.ShapeDtypeStruct((2, before * beams, channels), single)
-    others = small_call(functools.partial(halo_kernel, starts[:-1]), before * beams, (*halos[:-1], basis), part_sums)
+    others = small_call(functools.partial(part_kernel, starts[:-1], True), before * beams, (*halos[:-1], basis), part_sums)
     out_shape = jax.ShapeDtypeStruct((2, beams, frames, channels), jnp.bfloat16)
-    turned = pltpu.VMEM((2, 256 // LANES, frames * beams, LANES), single)
+    slabs = channels // 256
+    scratch = [
+        pltpu.VMEM((slabs, 2, 256 // LANES, frames * beams, LANES), single),
+        pltpu.VMEM((slabs, 2, beams, frames, 256), jnp.bfloat16),
+        pltpu.SemaphoreType.DMA((slabs,)),
+    ]
     args = (*halos[-1:], others, filtered, basis, synthesis_taps)
-    return small_call(functools.partial(taps_kernel, starts[-1:]), before * beams, args, out_shape, [turned])
+    return small_call(functools.partial(taps_kernel, starts[-1:]), before * beams, args, out_shape, scratch, pltpu.HBM)
 
 
 def solution(mesh):

time: 52.5 us -> 52.4 us (level)
  starting transfers between devices: 12.3 us -> 11 us
  waiting for transfers between devices: 9.26 us -> 10.2 us
    ppermute x2, starting transfers between devices: 6.96 us -> 5.12 us  [ended(): return (own, lax.ppermute(own[own.shape[0] - before:], 'tm', hops))]
    ppermute x4 -> x5, waiting for transfers between devices: 9.25 us -> 10.1 us  [across(): return lax.ppermute(value, 'chan', [(i, i ^ mask) for i in range(devices)])]
    ppermute x4 -> x5, starting transfers between devices: 5.35 us -> 5.89 us  [across(): return lax.ppermute(value, 'chan', [(i, i ^ mask) for i in range(devices)])]
    pallas_call x3 -> x4, Pallas kernels: 5.5 us -> 5.61 us  [small_call(): pl.pallas_call(kernel, in_specs=[whole] * len(args), out_specs=pl.BlockSp...]
  transfers between devices with their start and end apart: 6 -> 7, of which waited for: 3 -> 3; matrix products, arithmetic and copies ran while one was open for 1% -> 1% of each run, Pallas kernels for 10% -> 11%
where the time goes in v5:
time: 52.4 us; the launch traced here: 52.2 us
  Pallas kernels  30.3 us (58%)
  starting transfers between devices  11 us (21%)
  waiting for transfers between devices  10.2 us (19%)
    pallas_call x2, Pallas kernels, beamform(): pl.pallas_call(functools.partial(beam_kernel, first, tables is None), in_...  22.9 us
    ppermute x5, waiting for transfers between devices, across(): return lax.ppermute(value, 'chan', [(i, i ^ mask) for i in range(devices)])  10.1 us
    ppermute x5, starting transfers between devices, across(): return lax.ppermute(value, 'chan', [(i, i ^ mask) for i in range(devices)])  5.89 us
    pallas_call x4, Pallas kernels, small_call(): pl.pallas_call(kernel, in_specs=[whole] * len(args), out_specs=pl.BlockSp...  5.61 us
    ppermute x2, starting transfers between devices, ended(): return (own, lax.ppermute(own[own.shape[0] - before:], 'tm', hops))  5.12 us
    pallas_call x1, Pallas kernels, make_basis(): pl.pallas_call(basis_kernel, out_specs=pl.BlockSpec(memory_space=pltpu.VM...  1.84 us
  transfers between devices with their start and end apart: 7, of which 3 were waited for; matrix products, arithmetic and copies ran while one was open for 1% of the time, Pallas kernels for 11%

profile of v5, /device:TPU:0, one launch (start us, length us, event | category | flops | bytes accessed | tf_op | source)
XLA Modules:
  0.0 52.2 jit_solution(14751355849409328167)
XLA Ops:
  0.0 15.4 %beam.2 = (bf16[2,4,2,32,640]{4,3,2,1,0:T(8,128)(2,1)S(1)}, bf16[2,4,2,32,640]{4,3,2,1,0:T(8,128)(2,1)S(1)}, f32[2,32,256,128]{3,2,1,0:T(8,128)S(1)}, f32[2,16,2...) custom-call(s32[2,1024]{1,0:T(2,128)} %bitcast.8, s32[2,128]{1,0:T(2,128)} %bitcast.9, bf16[2,4,256,1024]{3,2,1,0:T(8,128)(2,1)} %refs_2_.1), custom_call_target="tpu_custom_call" | custom-call | flops 10737418240 | bytes 5242880 | tf_op jit(solution)/shard_map/beam/pallas_call | solution.py:224
  15.4 0.6 %collective-permute-start = (bf16[2,4,2,32,640]{4,3,2,1,0:T(8,128)(2,1)S(1)}, bf16[2,4,2,32,640]{4,3,2,1,0:T(8,128)(2,1)S(1)}, u32[]{:S(2)}, u32[]{:S(2)}) collective-permute-start(bf16[2,4,2,32,640]{4,3,2,1,0:T(8,128)(2,1)S(1)} %get-tuple-element.24), channel_id=1, source_target_pairs={{0,4},{4,0},{8,12},{12,8},{1,5},{5,1},{9,13},{13,9},{2,6},{6,2},{1... | collective-permute-start | bytes 1966088 | tf_op jit(solution)/shard_map/ppermute | solution.py:397
  16.0 1.7 %collective-permute-done = bf16[2,4,2,32,640]{4,3,2,1,0:T(8,128)(2,1)S(1)} collective-permute-done((bf16[2,4,2,32,640]{4,3,2,1,0:T(8,128)(2,1)S(1)}, bf16[2,4,2,32,640]{4,3,2,1,0:T(8,128)(2,1)S(1)}, u32[]{:S(2)}, u32[]{:S(2)}) %collective-permute-start) | collective-permute-done | bytes 655392 | tf_op jit(solution)/shard_map/ppermute | solution.py:397
  17.7 0.1 add_convert_fusion.1
  17.8 7.4 %beam.3 = (bf16[2,4,2,32,384]{4,3,2,1,0:T(8,128)(2,1)S(1)}, bf16[2,4,2,32,384]{4,3,2,1,0:T(8,128)(2,1)S(1)}) custom-call(f32[2,32,256,128]{3,2,1,0:T(8,128)S(1)} %get-tuple-element.25.refs_0_, f32[2,16,256,128]{3,2,1,0:T(8,128)S(1)} %get-tuple-element.26.refs_1_, bf16[2,4,256,1024]{3,2,1,0:T(8,128)(2,1)S(1)} %get-tuple-element.27.refs_2_), custom_call_target="tpu_custom_call" | custom-call | flops 6442450944 | bytes 3145728 | tf_op jit(solution)/shard_map/beam/pallas_call | solution.py:224
  25.2 0.4 collective-permute-start.1
  25.7 2.6 %collective-permute-start.2 = (bf16[1,4,2,32,640]{4,3,2,1,0:T(8,128)(2,1)S(1)}, bf16[1,4,2,32,640]{4,3,2,1,0:T(8,128)(2,1)S(1)}, u32[]{:S(2)}, u32[]{:S(2)}) collective-permute-start(bf16[1,4,2,32,640]{4,3,2,1,0:T(8,128)(2,1)S(1)} %add_convert_fusion.1), channel_id=1, source_target_pairs={{0,8},{4,12},{8,0},{12,4},{1,9},{5,13},{9,1},{13,5},{2,10},{6,14},... | collective-permute-start | bytes 983048 | tf_op jit(solution)/shard_map/ppermute | solution.py:397
  28.3 1.8 %basis.1.refs_1_.refs_2_.refs_3_ = bf16[1024,2048]{1,0:T(8,128)(2,1)S(1)} custom-call(), custom_call_target="tpu_custom_call" | custom-call | flops 1073741824 | bytes 4194304 | tf_op jit(solution)/shard_map/basis/pallas_call | solution.py:264
  30.1 0.1 add_convert_fusion.2
  30.2 0.0 copy-start
  30.3 6.3 %collective-permute-done.2 = bf16[1,4,2,32,640]{4,3,2,1,0:T(8,128)(2,1)S(1)} collective-permute-done((bf16[1,4,2,32,640]{4,3,2,1,0:T(8,128)(2,1)S(1)}, bf16[1,4,2,32,640]{4,3,2,1,0:T(8,128)(2,1)S(1)}, u32[]{:S(2)}, u32[]{:S(2)}) %collective-permute-start.2) | collective-permute-done | bytes 327712 | tf_op jit(solution)/shard_map/ppermute | solution.py:397
  36.5 1.7 %collective-permute-start.3 = (bf16[1,3,2,32,384]{4,3,2,1,0:T(8,128)(2,1)S(1)}, bf16[1,3,2,32,384]{4,3,2,1,0:T(8,128)(2,1)S(1)}, u32[]{:S(2)}, u32[]{:S(2)}) collective-permute-start(bf16[1,3,2,32,384]{4,3,2,1,0:T(8,128)(2,1)S(1)} %slice.69), channel_id=1, source_target_pairs={{0,8},{4,12},{8,0},{12,4},{1,9},{5,13},{9,1},{13,5},{2,10},{6,14},... | collective-permute-start | bytes 442376 | tf_op jit(solution)/shard_map/ppermute | solution.py:397
  38.3 0.1 fusion.refs_0_
  38.4 1.6 %collective-permute-start.5 = (bf16[3,2,32,640]{3,2,1,0:T(8,128)(2,1)S(1)}, bf16[3,2,32,640]{3,2,1,0:T(8,128)(2,1)S(1)}, u32[]{:S(2)}, u32[]{:S(2)}) collective-permute-start(bf16[3,2,32,640]{3,2,1,0:T(8,128)(2,1)S(1)} %slice.71), channel_id=1, source_target_pairs={{0,1},{1,2},{2,3},{3,0},{4,5},{5,6},{6,7},{7,4},{8,9},{9,10},{10,1... | collective-permute-start | bytes 737288 | tf_op jit(solution)/shard_map/ppermute | solution.py:411
  40.1 0.5 %collective-permute-start.6 = (bf16[1,1,2,32,384]{4,3,2,1,0:T(8,128)(2,1)S(1)}, bf16[1,1,2,32,384]{4,3,2,1,0:T(8,128)(2,1)S(1)}, u32[]{:S(2)}, u32[]{:S(2)}) collective-permute-start(bf16[1,1,2,32,384]{4,3,2,1,0:T(8,128)(2,1)S(1)} %slice.73), channel_id=1, source_target_pairs={{0,8},{4,12},{8,0},{12,4},{1,9},{5,13},{9,1},{13,5},{2,10},{6,14},... | collective-permute-start | bytes 147464 | tf_op jit(solution)/shard_map/ppermute | solution.py:397
  40.6 1.4 %shard_map.47.refs_1_ = f32[2,128,1024]{2,1,0:T(8,128)S(1)} custom-call(bf16[4,2,32,640]{3,2,1,0:T(8,128)(2,1)S(1)} %fusion.refs_0_, bf16[1024,2048]{1,0:T(8,128)(2,1)S(1)} %basis.1.refs_1_.refs_2_.refs_3_), custom_call_target="tpu_custom_call" | custom-call | flops 1073741824 | bytes 4194304 | tf_op jit(solution)/shard_map/pallas_call | solution.py:364
  42.1 2.1 %collective-permute-done.6 = bf16[1,1,2,32,384]{4,3,2,1,0:T(8,128)(2,1)S(1)} collective-permute-done((bf16[1,1,2,32,384]{4,3,2,1,0:T(8,128)(2,1)S(1)}, bf16[1,1,2,32,384]{4,3,2,1,0:T(8,128)(2,1)S(1)}, u32[]{:S(2)}, u32[]{:S(2)}) %collective-permute-start.6) | collective-permute-done | bytes 49184 | tf_op jit(solution)/shard_map/ppermute | solution.py:397
  44.2 0.1 fusion.1
  44.3 3.5 %collective-permute-start.4 = (bf16[3,2,32,384]{3,2,1,0:T(8,128)(2,1)S(1)}, bf16[3,2,32,384]{3,2,1,0:T(8,128)(2,1)S(1)}, u32[]{:S(2)}, u32[]{:S(2)}) collective-permute-start(bf16[3,2,32,384]{3,2,1,0:T(8,128)(2,1)S(1)} %fusion.1), channel_id=1, source_target_pairs={{0,1},{1,2},{2,3},{4,5},{5,6},{6,7},{8,9},{9,10},{10,11},{12,13},{... | collective-permute-start | bytes 442376 | tf_op jit(solution)/shard_map/ppermute | solution.py:411
  47.8 1.3 %shard_map.48.refs_2_ = f32[2,4,32,1024]{3,2,1,0:T(8,128)S(1)} custom-call(bf16[4,2,32,384]{3,2,1,0:T(8,128)(2,1)S(1)} %pad_maximum_fusion.refs_0_, f32[2,128,1024]{2,1,0:T(8,128)S(1)} %shard_map.47.refs_1_, bf16[1024,2048]{1,0:T(8,128)(2,1)S(1)} %basis.1.refs_1_.refs_2_.refs_3_, f32[4,1024]{1,0:T(4,128)S(1)} %copy-done), custom_call_target="tpu_custom_call" | custom-call | flops 1073741824 | bytes 4194304 | tf_op jit(solution)/shard_map/pallas_call | solution.py:364
  49.1 0.0 collective-permute-done.5.refs_0_
  49.1 1.2 %shard_map.46.refs_1_ = f32[2,96,1024]{2,1,0:T(8,128)S(1)} custom-call(bf16[3,2,32,640]{3,2,1,0:T(8,128)(2,1)S(1)} %collective-permute-done.5.refs_0_, bf16[1024,2048]{1,0:T(8,128)(2,1)S(1)} %basis.1.refs_1_.refs_2_.refs_3_), custom_call_target="tpu_custom_call" | custom-call | flops 805306368 | bytes 4194304 | tf_op jit(solution)/shard_map/pallas_call | solution.py:364
  50.4 0.0 collective-permute-done.4.refs_0_
  50.4 1.6 %shard_map.49 = bf16[2,32,4,1024]{3,2,1,0:T(4,128)(2,1)} custom-call(bf16[3,2,32,384]{3,2,1,0:T(8,128)(2,1)S(1)} %collective-permute-done.4.refs_0_, f32[2,96,1024]{2,1,0:T(8,128)S(1)} %shard_map.46.refs_1_, f32[2,4,32,1024]{3,2,1,0:T(8,128)S(1)} %shard_map.48.refs_2_, bf16[1024,2048]{1,0:T(8,128)(2,1)S(1)} %basis.1.refs_1_.refs_2_.refs_3_, ...), custom_call_target="tpu_custom_call" | custom-call | flops 805306368 | bytes 4194304 | tf_op jit(solution)/shard_map/pallas_call | solution.py:364
  (8 shorter events, 0.1 us)
Async XLA Ops:
  15.4 2.3 %collective-permute-start = (bf16[2,4,2,32,640]{4,3,2,1,0:T(8,128)(2,1)S(1)}, bf16[2,4,2,32,640]{4,3,2,1,0:T(8,128)(2,1)S(1)}, u32[]{:S(2)}, u32[]{:S(2)}) collective-permute-start(bf16[2,4,2,32,640]{4,3,2,1,0:T(8,128)(2,1)S(1)} %get-tuple-element.24), channel_id=1, source_target_pairs={{0,4},{4,0},{8,12},{12,8},{1,5},{5,1},{9,13},{13,9},{2,6},{6,2},{1... | collective-permute-start | bytes 1966088 | tf_op jit(solution)/shard_map/ppermute | solution.py:397
  25.2 4.9 %collective-permute-start.1 = (bf16[2,4,2,32,384]{4,3,2,1,0:T(8,128)(2,1)S(1)}, bf16[2,4,2,32,384]{4,3,2,1,0:T(8,128)(2,1)S(1)}, u32[]{:S(2)}, u32[]{:S(2)}) collective-permute-start(bf16[2,4,2,32,384]{4,3,2,1,0:T(8,128)(2,1)S(1)} %get-tuple-element.29), channel_id=1, source_target_pairs={{0,4},{4,0},{8,12},{12,8},{1,5},{5,1},{9,13},{13,9},{2,6},{6,2},{1... | collective-permute-start | bytes 1179656 | tf_op jit(solution)/shard_map/ppermute | solution.py:397
  25.7 10.9 %collective-permute-start.2 = (bf16[1,4,2,32,640]{4,3,2,1,0:T(8,128)(2,1)S(1)}, bf16[1,4,2,32,640]{4,3,2,1,0:T(8,128)(2,1)S(1)}, u32[]{:S(2)}, u32[]{:S(2)}) collective-permute-start(bf16[1,4,2,32,640]{4,3,2,1,0:T(8,128)(2,1)S(1)} %add_convert_fusion.1), channel_id=1, source_target_pairs={{0,8},{4,12},{8,0},{12,4},{1,9},{5,13},{9,1},{13,5},{2,10},{6,14},... | collective-permute-start | bytes 983048 | tf_op jit(solution)/shard_map/ppermute | solution.py:397
  30.2 17.5 %copy-start = (f32[4,1024]{1,0:T(4,128)S(1)}, f32[4,1024]{1,0:T(4,128)}, u32[]{:S(2)}) copy-start(f32[4,1024]{1,0:T(4,128)} %refs_4_.1) | copy-start | bytes 49156
  36.5 7.6 %collective-permute-start.3 = (bf16[1,3,2,32,384]{4,3,2,1,0:T(8,128)(2,1)S(1)}, bf16[1,3,2,32,384]{4,3,2,1,0:T(8,128)(2,1)S(1)}, u32[]{:S(2)}, u32[]{:S(2)}) collective-permute-start(bf16[1,3,2,32,384]{4,3,2,1,0:T(8,128)(2,1)S(1)} %slice.69), channel_id=1, source_target_pairs={{0,8},{4,12},{8,0},{12,4},{1,9},{5,13},{9,1},{13,5},{2,10},{6,14},... | collective-permute-start | bytes 442376 | tf_op jit(solution)/shard_map/ppermute | solution.py:397
  38.4 10.7 %collective-permute-start.5 = (bf16[3,2,32,640]{3,2,1,0:T(8,128)(2,1)S(1)}, bf16[3,2,32,640]{3,2,1,0:T(8,128)(2,1)S(1)}, u32[]{:S(2)}, u32[]{:S(2)}) collective-permute-start(bf16[3,2,32,640]{3,2,1,0:T(8,128)(2,1)S(1)} %slice.71), channel_id=1, source_target_pairs={{0,1},{1,2},{2,3},{3,0},{4,5},{5,6},{6,7},{7,4},{8,9},{9,10},{10,1... | collective-permute-start | bytes 737288 | tf_op jit(solution)/shard_map/ppermute | solution.py:411
  40.1 4.1 %collective-permute-start.6 = (bf16[1,1,2,32,384]{4,3,2,1,0:T(8,128)(2,1)S(1)}, bf16[1,1,2,32,384]{4,3,2,1,0:T(8,128)(2,1)S(1)}, u32[]{:S(2)}, u32[]{:S(2)}) collective-permute-start(bf16[1,1,2,32,384]{4,3,2,1,0:T(8,128)(2,1)S(1)} %slice.73), channel_id=1, source_target_pairs={{0,8},{4,12},{8,0},{12,4},{1,9},{5,13},{9,1},{13,5},{2,10},{6,14},... | collective-permute-start | bytes 147464 | tf_op jit(solution)/shard_map/ppermute | solution.py:397
  44.3 6.1 %collective-permute-start.4 = (bf16[3,2,32,384]{3,2,1,0:T(8,128)(2,1)S(1)}, bf16[3,2,32,384]{3,2,1,0:T(8,128)(2,1)S(1)}, u32[]{:S(2)}, u32[]{:S(2)}) collective-permute-start(bf16[3,2,32,384]{3,2,1,0:T(8,128)(2,1)S(1)} %fusion.1), channel_id=1, source_target_pairs={{0,1},{1,2},{2,3},{4,5},{5,6},{6,7},{8,9},{9,10},{10,11},{12,13},{... | collective-permute-start | bytes 442376 | tf_op jit(solution)/shard_map/ppermute | solution.py:411

commit v6 on v5

--- a/solution.py
+++ b/solution.py
@@ -16,6 +16,7 @@
 TABLE = jnp.float32
 BEAM_LIMIT = 24
 AHEAD = 2
+START_CENTRES = 2
 
 
 def turn(phase, steps):
@@ -38,9 +39,8 @@
     return a[0] * b[0] - a[1] * b[1], a[0] * b[1] + a[1] * b[0]
 
 
-def table_kernel_part(copy, position_hbm, steering_hbm, position, steering, small_arrivals, offset_tables, centre_tables, own_beams):
+def table_kernel_part(copy, position_hbm, steering_hbm, position, steering, small_arrivals, offset_tables, centre_tables, stride_table, own_beams):
     feeds, beams = offset_tables.shape[2:]
-    centres = centre_tables.shape[1]
     here = lax.axis_index("chan")
     position_copy = pltpu.make_async_copy(position_hbm, position, small_arrivals.at[0])
     steering_copy = pltpu.make_async_copy(steering_hbm, steering, small_arrivals.at[1])
@@ -79,10 +79,12 @@
                 state = times(state, advance)
         state = turn(((2 * HALF - 1) * delay) & (2 * PHASES - 1), 2 * PHASES)
         advance = turn((4 * HALF * delay) & (2 * PHASES - 1), 2 * PHASES)
-        for centre in range(centres):
+        stride_table[0, pl.ds(at, SLAB), :] = advance[0]
+        stride_table[1, pl.ds(at, SLAB), :] = advance[1]
+        for centre in range(START_CENTRES):
             centre_tables[0, centre, pl.ds(at, SLAB), :] = state[0].astype(TABLE)
             centre_tables[1, centre, pl.ds(at, SLAB), :] = state[1].astype(TABLE)
-            if centre + 1 < centres:
+            if centre + 1 < START_CENTRES:
                 state = times(state, advance)
         return carry
 
@@ -92,7 +94,7 @@
 def beam_kernel(first, make_tables, *refs):
     if make_tables:
         position_hbm, steering_hbm, voltages, keep, send, offset_tables, centre_tables, staged = refs[:8]
-        position, steering, small_arrivals, arrivals = refs[8:12]
+        position, steering, small_arrivals, arrivals, stride_table = refs[8:13]
     else:
         offset_tables, centre_tables, staged, keep, send = refs[:5]
     both_rows, both_sums = refs[-2:]
@@ -107,7 +109,7 @@
 
     if make_tables:
         copy = pltpu.make_async_copy(voltages, staged, arrivals.at[0])
-        table_kernel_part(copy, position_hbm, steering_hbm, position, steering, small_arrivals, offset_tables, centre_tables, own_beams)
+        table_kernel_part(copy, position_hbm, steering_hbm, position, steering, small_arrivals, offset_tables, centre_tables, stride_table, own_beams)
         copy.wait()
 
     width = min(feeds, LANES)
@@ -157,6 +159,19 @@
         less = quarter_turn(c[stride:] - d[stride:])
         sums[upper * stride : (upper + 1) * stride, :] = a[:stride] - b[:stride] + more
         sums[lower * stride : (lower + 1) * stride, :] = a[stride:] + b[stride:] + less
+
+    growth = -(-(centre_tables.shape[1] - START_CENTRES) // blocks)
+
+    def grow(index, at):
+        slab = slice(at * SLAB, (at + 1) * SLAB)
+        advance = (stride_table[0, slab, :], stride_table[1, slab, :])
+        start = START_CENTRES - 1 + index * growth
+        state = (centre_tables[0, start, slab, :], centre_tables[1, start, slab, :])
+        for more in range(growth):
+            state = times(state, advance)
+            target = start + 1 + more
+            centre_tables[0, target, slab, :] = state[0]
+            centre_tables[1, target, slab, :] = state[1]
 
     def one_block(index, parity):
         rows, sums = both_rows.at[parity], both_sums.at[parity]
@@ -173,6 +188,8 @@
             if count % every == 0:
                 give(jnp.maximum(index - 1, 0), other_sums, count // every)
                 take(jnp.minimum(index + 1, blocks - 1), other_rows, count // every)
+            if make_tables and count % 2 == 1 and count // 2 < feeds // SLAB:
+                grow(index, count // 2)
             if count + AHEAD < len(lefts):
                 ready.append(lhs(rows, *lefts[count + AHEAD]))
             pair(ready[count], sums, cosine, sine, local, offset)
@@ -203,11 +220,12 @@
     whole = pl.BlockSpec(memory_space=pltpu.VMEM)
     anywhere = pl.BlockSpec(memory_space=pltpu.HBM)
     out_shape = [shape, shape]
+    growth = -(-(channels // (2 * HALF) - START_CENTRES) // (count // LANES))
     scratch = []
     if tables is None:
         out_shape += [
             jax.ShapeDtypeStruct((2, HALF, feeds, beams), TABLE),
-            jax.ShapeDtypeStruct((2, channels // (2 * HALF), feeds, beams), TABLE),
+            jax.ShapeDtypeStruct((2, START_CENTRES + growth * (count // LANES), feeds, beams), TABLE),
             jax.ShapeDtypeStruct(voltages.shape, jnp.bfloat16),
         ]
         scratch += [
@@ -215,6 +233,7 @@
             pltpu.VMEM(steering.shape, jnp.int32),
             pltpu.SemaphoreType.DMA((2,)),
             pltpu.SemaphoreType.DMA((1,)),
+            pltpu.VMEM((2, feeds, beams), jnp.float32),
         ]
         position = pltpu.with_memory_space_constraint(position, pltpu.HBM)
         steering = pltpu.with_memory_space_constraint(steering, pltpu.HBM)
@@ -237,27 +256,24 @@
 
 def basis_kernel(basis, small):
     channels = basis.shape[0]
-    width = small.shape[2]
-    group = small.shape[1]
-
-    def one_slab(index, carry):
-        first = pl.multiple_of(index * width, width)
+    width = small.shape[3]
+    group = small.shape[2]
+
+    for first in range(0, channels, width):
 
         def phases(rows, factor):
             row = lax.broadcasted_iota(jnp.int32, (rows, width), 0) * factor
             column = first + lax.broadcasted_iota(jnp.int32, (rows, width), 1)
             return (row * column) & (channels - 1)
 
-        small[0], small[1] = turn(phases(group, 1), channels)
+        slab = first // width
+        small[slab, 0], small[slab, 1] = turn(phases(group, 1), channels)
         count = channels // group
         large = turn(phases(count, group), channels)
         for at in range(count):
-            real, imag = times((large[0][at : at + 1], large[1][at : at + 1]), (small[0], small[1]))
+            real, imag = times((large[0][at : at + 1], large[1][at : at + 1]), (small[slab, 0], small[slab, 1]))
             basis[at * group : (at + 1) * group, pl.ds(first, width)] = real.astype(jnp.bfloat16)
-            basis[at * group : (at + 1) * group, pl.ds(pl.multiple_of(channels + first, width), width)] = imag.astype(jnp.bfloat16)
-        return carry
-
-    lax.fori_loop(0, channels // width, one_slab, 0)
+            basis[at * group : (at + 1) * group, pl.ds(channels + first, width)] = imag.astype(jnp.bfloat16)
 
 
 def make_basis(channels):
@@ -265,7 +281,7 @@
         basis_kernel,
         out_specs=pl.BlockSpec(memory_space=pltpu.VMEM),
         out_shape=jax.ShapeDtypeStruct((channels, 2 * channels), jnp.bfloat16),
-        scratch_shapes=[pltpu.VMEM((2, 32, 256), jnp.float32)],
+        scratch_shapes=[pltpu.VMEM((channels // 256, 2, 32, 256), jnp.float32)],
         compiler_params=pltpu.CompilerParams(vmem_limit_bytes=8 * 2**20),
         cost_estimate=pl.CostEstimate(flops=2**30, bytes_accessed=4 * channels * channels, transcendentals=0),
         name="basis",
@@ -296,8 +312,7 @@
     width = min(256, channels)
     scale = 1.0 / math.sqrt(channels)
 
-    def one_slab(index, carry):
-        first = pl.multiple_of(index * width, width)
+    for first in range(0, channels, width):
         for part, value in enumerate(transform(pieces, starts, basis, first, width)):
             value = ((value + others[part, :, pl.ds(first, width)]) * scale).astype(jnp.bfloat16).astype(jnp.float32)
             for t in range(frames):
@@ -306,9 +321,6 @@
                     term = taps[k : k + 1, pl.ds(first, width)] * value[(t - k) * beams : (t - k + 1) * beams]
                     total = term if total is None else total + term
                 out[part, t, :, pl.ds(first, width)] = total
-        return carry
-
-    lax.fori_loop(0, channels // width, one_slab, 0)
 
 
 def part_kernel(starts, wraps, *refs):
@@ -331,31 +343,38 @@
     before, _, beams, _ = pieces[0].shape
     channels = basis.shape[0]
     frames = own.shape[1]
-    slabs = departures.shape[0]
-    width = channels // slabs
+    width = min(256, channels)
+    size = beams // departures.shape[1]
     scale = 1.0 / math.sqrt(channels)
 
-    def departure(index):
-        lanes = pl.ds(index * width, width)
-        return pltpu.make_async_copy(result.at[index], out.at[:, :, :, lanes], departures.at[index])
-
-    for index in range(slabs):
-        lanes = pl.ds(index * width, width)
-        for part, value in enumerate(transform(pieces, starts, basis, index * width, width)):
-            value = ((value + others[part, :, lanes]) * scale).astype(jnp.bfloat16).astype(jnp.float32)
-            for t in range(frames):
-                total = own[part, t, :, lanes]
-                for k in range(t + 1, taps.shape[0]):
-                    at = before + t - k
-                    total = total + taps[k : k + 1, lanes] * value[at * beams : (at + 1) * beams]
-                for at in range(width // LANES):
-                    turned[index, part, at, pl.ds(t, beams, stride=frames), :] = total[:, at * LANES : (at + 1) * LANES]
-            for at in range(width // LANES):
-                value = turned[index, part, at].reshape(beams, frames, LANES).astype(jnp.bfloat16)
-                result[index, part, :, :, at * LANES : (at + 1) * LANES] = value
-        departure(index).start()
-    for index in range(slabs):
-        departure(index).wait()
+    def departure(part, at):
+        place = pl.ds(at * size, size)
+        return pltpu.make_async_copy(result.at[part, place], out.at[part, place], departures.at[part, at])
+
+    values = []
+    for first in range(0, channels, width):
+        both = transform(pieces, starts, basis, first, width)
+        lanes = pl.ds(first, width)
+        values.append([((both[part] + others[part, :, lanes]) * scale).astype(jnp.bfloat16).astype(jnp.float32) for part in range(2)])
+    for part in range(2):
+        for group in range(beams // size):
+            for index, first in enumerate(range(0, channels, width)):
+                lanes = pl.ds(first, width)
+                for t in range(frames):
+                    total = own[part, t, group * size : (group + 1) * size, lanes]
+                    for k in range(t + 1, taps.shape[0]):
+                        at = (before + t - k) * beams + group * size
+                        total = total + taps[k : k + 1, lanes] * values[index][part][at : at + size]
+                    for at in range(width // LANES):
+                        piece = total[:, at * LANES : (at + 1) * LANES]
+                        turned[part, group, first // LANES + at, pl.ds(t, size, stride=frames), :] = piece
+                for at in range(first // LANES, (first + width) // LANES):
+                    value = turned[part, group, at].reshape(size, frames, LANES).astype(jnp.bfloat16)
+                    result[part, group * size : (group + 1) * size, :, at * LANES : (at + 1) * LANES] = value
+            departure(part, group).start()
+    for part in range(2):
+        for group in range(beams // size):
+            departure(part, group).wait()
 
 
 def small_call(kernel, rows, args, out_shape, scratch=(), space=pltpu.VMEM):
@@ -442,11 +461,11 @@
     part_sums = jax.ShapeDtypeStruct((2, before * beams, channels), single)
     others = small_call(functools.partial(part_kernel, starts[:-1], True), before * beams, (*halos[:-1], basis), part_sums)
     out_shape = jax.ShapeDtypeStruct((2, beams, frames, channels), jnp.bfloat16)
-    slabs = channels // 256
+    groups = 2 if beams % 16 == 0 else 1
     scratch = [
-        pltpu.VMEM((slabs, 2, 256 // LANES, frames * beams, LANES), single),
-        pltpu.VMEM((slabs, 2, beams, frames, 256), jnp.bfloat16),
-        pltpu.SemaphoreType.DMA((slabs,)),
+        pltpu.VMEM((2, groups, channels // LANES, frames * beams // groups, LANES), single),
+        pltpu.VMEM((2, beams, frames, channels), jnp.bfloat16),
+        pltpu.SemaphoreType.DMA((2, groups)),
     ]
     args = (*halos[-1:], others, filtered, basis, synthesis_taps)
     return small_call(functools.partial(taps_kernel, starts[-1:]), before * beams, args, out_shape, scratch, pltpu.HBM)

time: 52.4 us -> 52.5 us (level)
  Pallas kernels: 30.3 us -> 29.3 us
  waiting for transfers between devices: 10.2 us -> 11 us
  transfers between devices with their start and end apart: 7 -> 7, of which waited for: 3 -> 4; matrix products, arithmetic and copies ran while one was open for 1% -> 1% of each run, Pallas kernels for 11% -> 9%
where the time goes in v6:
time: 52.5 us; the launch traced here: 52.3 us
  Pallas kernels  29.3 us (56%)
  starting transfers between devices  11 us (21%)
  waiting for transfers between devices  11 us (21%)
  other arithmetic  0.59 us (1%)
    pallas_call x2, Pallas kernels, beamform(): pl.pallas_call(functools.partial(beam_kernel, first, tables is None), in_...  22.7 us
    ppermute x5, waiting for transfers between devices, across(): return lax.ppermute(value, 'chan', [(i, i ^ mask) for i in range(devices)])  10.6 us
    ppermute x5, starting transfers between devices, across(): return lax.ppermute(value, 'chan', [(i, i ^ mask) for i in range(devices)])  5.89 us
    pallas_call x4, Pallas kernels, small_call(): pl.pallas_call(kernel, in_specs=[whole] * len(args), out_specs=pl.BlockSp...  5.17 us
    ppermute x2, starting transfers between devices, ended(): return (own, lax.ppermute(own[own.shape[0] - before:], 'tm', hops))  5.12 us
    pallas_call x1, Pallas kernels, make_basis(): pl.pallas_call(basis_kernel, out_specs=pl.BlockSpec(memory_space=pltpu.VM...  1.39 us
  transfers between devices with their start and end apart: 7, of which 4 were waited for; matrix products, arithmetic and copies ran while one was open for 1% of the time, Pallas kernels for 9%

profile of v6, /device:TPU:0, one launch (start us, length us, event | category | flops | bytes accessed | tf_op | source)
XLA Modules:
  0.0 52.3 jit_solution(6510565031509851640)
XLA Ops:
  0.0 15.3 %beam.2 = (bf16[2,4,2,32,640]{4,3,2,1,0:T(8,128)(2,1)S(1)}, bf16[2,4,2,32,640]{4,3,2,1,0:T(8,128)(2,1)S(1)}, f32[2,32,256,128]{3,2,1,0:T(8,128)S(1)}, f32[2,17,2...) custom-call(s32[2,1024]{1,0:T(2,128)} %bitcast.8, s32[2,128]{1,0:T(2,128)} %bitcast.9, bf16[2,4,256,1024]{3,2,1,0:T(8,128)(2,1)} %refs_2_.1), custom_call_target="tpu_custom_call" | custom-call | flops 10737418240 | bytes 5242880 | tf_op jit(solution)/shard_map/beam/pallas_call | solution.py:243
  15.3 0.6 %collective-permute-start = (bf16[2,4,2,32,640]{4,3,2,1,0:T(8,128)(2,1)S(1)}, bf16[2,4,2,32,640]{4,3,2,1,0:T(8,128)(2,1)S(1)}, u32[]{:S(2)}, u32[]{:S(2)}) collective-permute-start(bf16[2,4,2,32,640]{4,3,2,1,0:T(8,128)(2,1)S(1)} %get-tuple-element.24), channel_id=1, source_target_pairs={{0,4},{4,0},{8,12},{12,8},{1,5},{5,1},{9,13},{13,9},{2,6},{6,2},{1... | collective-permute-start | bytes 1966088 | tf_op jit(solution)/shard_map/ppermute | solution.py:416
  15.9 1.7 %collective-permute-done = bf16[2,4,2,32,640]{4,3,2,1,0:T(8,128)(2,1)S(1)} collective-permute-done((bf16[2,4,2,32,640]{4,3,2,1,0:T(8,128)(2,1)S(1)}, bf16[2,4,2,32,640]{4,3,2,1,0:T(8,128)(2,1)S(1)}, u32[]{:S(2)}, u32[]{:S(2)}) %collective-permute-start) | collective-permute-done | bytes 655392 | tf_op jit(solution)/shard_map/ppermute | solution.py:416
  17.6 0.1 add_convert_fusion.1
  17.7 7.4 %beam.3 = (bf16[2,4,2,32,384]{4,3,2,1,0:T(8,128)(2,1)S(1)}, bf16[2,4,2,32,384]{4,3,2,1,0:T(8,128)(2,1)S(1)}) custom-call(f32[2,32,256,128]{3,2,1,0:T(8,128)S(1)} %get-tuple-element.25.refs_0_, f32[2,17,256,128]{3,2,1,0:T(8,128)S(1)} %get-tuple-element.26.refs_1_, bf16[2,4,256,1024]{3,2,1,0:T(8,128)(2,1)S(1)} %get-tuple-element.27.refs_2_), custom_call_target="tpu_custom_call" | custom-call | flops 6442450944 | bytes 3145728 | tf_op jit(solution)/shard_map/beam/pallas_call | solution.py:243
  25.1 0.4 collective-permute-start.1
  25.5 2.6 %collective-permute-start.2 = (bf16[1,4,2,32,640]{4,3,2,1,0:T(8,128)(2,1)S(1)}, bf16[1,4,2,32,640]{4,3,2,1,0:T(8,128)(2,1)S(1)}, u32[]{:S(2)}, u32[]{:S(2)}) collective-permute-start(bf16[1,4,2,32,640]{4,3,2,1,0:T(8,128)(2,1)S(1)} %add_convert_fusion.1), channel_id=1, source_target_pairs={{0,8},{4,12},{8,0},{12,4},{1,9},{5,13},{9,1},{13,5},{2,10},{6,14},... | collective-permute-start | bytes 983048 | tf_op jit(solution)/shard_map/ppermute | solution.py:416
  28.2 1.4 %basis.1.refs_1_.refs_2_.refs_3_ = bf16[1024,2048]{1,0:T(8,128)(2,1)S(1)} custom-call(), custom_call_target="tpu_custom_call" | custom-call | flops 1073741824 | bytes 4194304 | tf_op jit(solution)/shard_map/basis/pallas_call | solution.py:280
  29.6 0.0 collective-permute-done.1
  29.6 0.1 add_convert_fusion.2
  29.7 0.0 copy-start
  29.7 6.7 %collective-permute-done.2 = bf16[1,4,2,32,640]{4,3,2,1,0:T(8,128)(2,1)S(1)} collective-permute-done((bf16[1,4,2,32,640]{4,3,2,1,0:T(8,128)(2,1)S(1)}, bf16[1,4,2,32,640]{4,3,2,1,0:T(8,128)(2,1)S(1)}, u32[]{:S(2)}, u32[]{:S(2)}) %collective-permute-start.2) | collective-permute-done | bytes 327712 | tf_op jit(solution)/shard_map/ppermute | solution.py:416
  36.4 1.7 %collective-permute-start.3 = (bf16[1,3,2,32,384]{4,3,2,1,0:T(8,128)(2,1)S(1)}, bf16[1,3,2,32,384]{4,3,2,1,0:T(8,128)(2,1)S(1)}, u32[]{:S(2)}, u32[]{:S(2)}) collective-permute-start(bf16[1,3,2,32,384]{4,3,2,1,0:T(8,128)(2,1)S(1)} %slice.69), channel_id=1, source_target_pairs={{0,8},{4,12},{8,0},{12,4},{1,9},{5,13},{9,1},{13,5},{2,10},{6,14},... | collective-permute-start | bytes 442376 | tf_op jit(solution)/shard_map/ppermute | solution.py:416
  38.1 0.3 fusion.refs_0_
  38.5 1.6 %collective-permute-start.5 = (bf16[3,2,32,640]{3,2,1,0:T(8,128)(2,1)S(1)}, bf16[3,2,32,640]{3,2,1,0:T(8,128)(2,1)S(1)}, u32[]{:S(2)}, u32[]{:S(2)}) collective-permute-start(bf16[3,2,32,640]{3,2,1,0:T(8,128)(2,1)S(1)} %slice.71), channel_id=1, source_target_pairs={{0,1},{1,2},{2,3},{3,0},{4,5},{5,6},{6,7},{7,4},{8,9},{9,10},{10,1... | collective-permute-start | bytes 737288 | tf_op jit(solution)/shard_map/ppermute | solution.py:430
  40.2 0.5 %collective-permute-start.6 = (bf16[1,1,2,32,384]{4,3,2,1,0:T(8,128)(2,1)S(1)}, bf16[1,1,2,32,384]{4,3,2,1,0:T(8,128)(2,1)S(1)}, u32[]{:S(2)}, u32[]{:S(2)}) collective-permute-start(bf16[1,1,2,32,384]{4,3,2,1,0:T(8,128)(2,1)S(1)} %slice.73), channel_id=1, source_target_pairs={{0,8},{4,12},{8,0},{12,4},{1,9},{5,13},{9,1},{13,5},{2,10},{6,14},... | collective-permute-start | bytes 147464 | tf_op jit(solution)/shard_map/ppermute | solution.py:416
  40.7 1.4 %shard_map.47.refs_1_ = f32[2,128,1024]{2,1,0:T(8,128)S(1)} custom-call(bf16[4,2,32,640]{3,2,1,0:T(8,128)(2,1)S(1)} %fusion.refs_0_, bf16[1024,2048]{1,0:T(8,128)(2,1)S(1)} %basis.1.refs_1_.refs_2_.refs_3_), custom_call_target="tpu_custom_call" | custom-call | flops 1073741824 | bytes 4194304 | tf_op jit(solution)/shard_map/pallas_call | solution.py:383
  42.1 2.1 %collective-permute-done.6 = bf16[1,1,2,32,384]{4,3,2,1,0:T(8,128)(2,1)S(1)} collective-permute-done((bf16[1,1,2,32,384]{4,3,2,1,0:T(8,128)(2,1)S(1)}, bf16[1,1,2,32,384]{4,3,2,1,0:T(8,128)(2,1)S(1)}, u32[]{:S(2)}, u32[]{:S(2)}) %collective-permute-start.6) | collective-permute-done | bytes 49184 | tf_op jit(solution)/shard_map/ppermute | solution.py:416
  44.3 0.1 fusion.1
  44.4 3.5 %collective-permute-start.4 = (bf16[3,2,32,384]{3,2,1,0:T(8,128)(2,1)S(1)}, bf16[3,2,32,384]{3,2,1,0:T(8,128)(2,1)S(1)}, u32[]{:S(2)}, u32[]{:S(2)}) collective-permute-start(bf16[3,2,32,384]{3,2,1,0:T(8,128)(2,1)S(1)} %fusion.1), channel_id=1, source_target_pairs={{0,1},{1,2},{2,3},{4,5},{5,6},{6,7},{8,9},{9,10},{10,11},{12,13},{... | collective-permute-start | bytes 442376 | tf_op jit(solution)/shard_map/ppermute | solution.py:430
  47.9 0.9 %shard_map.48.refs_2_ = f32[2,4,32,1024]{3,2,1,0:T(8,128)S(1)} custom-call(bf16[4,2,32,384]{3,2,1,0:T(8,128)(2,1)S(1)} %pad_maximum_fusion.refs_0_, f32[2,128,1024]{2,1,0:T(8,128)S(1)} %shard_map.47.refs_1_, bf16[1024,2048]{1,0:T(8,128)(2,1)S(1)} %basis.1.refs_1_.refs_2_.refs_3_, f32[4,1024]{1,0:T(4,128)S(1)} %copy-done), custom_call_target="tpu_custom_call" | custom-call | flops 1073741824 | bytes 4194304 | tf_op jit(solution)/shard_map/pallas_call | solution.py:383
  48.8 1.2 %shard_map.46.refs_1_ = f32[2,96,1024]{2,1,0:T(8,128)S(1)} custom-call(bf16[3,2,32,640]{3,2,1,0:T(8,128)(2,1)S(1)} %collective-permute-done.5.refs_0_, bf16[1024,2048]{1,0:T(8,128)(2,1)S(1)} %basis.1.refs_1_.refs_2_.refs_3_), custom_call_target="tpu_custom_call" | custom-call | flops 805306368 | bytes 4194304 | tf_op jit(solution)/shard_map/pallas_call | solution.py:383
  50.0 0.5 collective-permute-done.4.refs_0_
  50.5 1.6 %shard_map.49 = bf16[2,32,4,1024]{3,2,1,0:T(4,128)(2,1)} custom-call(bf16[3,2,32,384]{3,2,1,0:T(8,128)(2,1)S(1)} %collective-permute-done.4.refs_0_, f32[2,96,1024]{2,1,0:T(8,128)S(1)} %shard_map.46.refs_1_, f32[2,4,32,1024]{3,2,1,0:T(8,128)S(1)} %shard_map.48.refs_2_, bf16[1024,2048]{1,0:T(8,128)(2,1)S(1)} %basis.1.refs_1_.refs_2_.refs_3_, ...), custom_call_target="tpu_custom_call" | custom-call | flops 805306368 | bytes 4194304 | tf_op jit(solution)/shard_map/pallas_call | solution.py:383
  (8 shorter events, 0.1 us)
Async XLA Ops:
  15.3 2.3 %collective-permute-start = (bf16[2,4,2,32,640]{4,3,2,1,0:T(8,128)(2,1)S(1)}, bf16[2,4,2,32,640]{4,3,2,1,0:T(8,128)(2,1)S(1)}, u32[]{:S(2)}, u32[]{:S(2)}) collective-permute-start(bf16[2,4,2,32,640]{4,3,2,1,0:T(8,128)(2,1)S(1)} %get-tuple-element.24), channel_id=1, source_target_pairs={{0,4},{4,0},{8,12},{12,8},{1,5},{5,1},{9,13},{13,9},{2,6},{6,2},{1... | collective-permute-start | bytes 1966088 | tf_op jit(solution)/shard_map/ppermute | solution.py:416
  25.1 4.4 %collective-permute-start.1 = (bf16[2,4,2,32,384]{4,3,2,1,0:T(8,128)(2,1)S(1)}, bf16[2,4,2,32,384]{4,3,2,1,0:T(8,128)(2,1)S(1)}, u32[]{:S(2)}, u32[]{:S(2)}) collective-permute-start(bf16[2,4,2,32,384]{4,3,2,1,0:T(8,128)(2,1)S(1)} %get-tuple-element.29), channel_id=1, source_target_pairs={{0,4},{4,0},{8,12},{12,8},{1,5},{5,1},{9,13},{13,9},{2,6},{6,2},{1... | collective-permute-start | bytes 1179656 | tf_op jit(solution)/shard_map/ppermute | solution.py:416
  25.5 10.9 %collective-permute-start.2 = (bf16[1,4,2,32,640]{4,3,2,1,0:T(8,128)(2,1)S(1)}, bf16[1,4,2,32,640]{4,3,2,1,0:T(8,128)(2,1)S(1)}, u32[]{:S(2)}, u32[]{:S(2)}) collective-permute-start(bf16[1,4,2,32,640]{4,3,2,1,0:T(8,128)(2,1)S(1)} %add_convert_fusion.1), channel_id=1, source_target_pairs={{0,8},{4,12},{8,0},{12,4},{1,9},{5,13},{9,1},{13,5},{2,10},{6,14},... | collective-permute-start | bytes 983048 | tf_op jit(solution)/shard_map/ppermute | solution.py:416
  29.7 18.2 %copy-start = (f32[4,1024]{1,0:T(4,128)S(1)}, f32[4,1024]{1,0:T(4,128)}, u32[]{:S(2)}) copy-start(f32[4,1024]{1,0:T(4,128)} %refs_4_.1) | copy-start | bytes 49156
  36.4 7.9 %collective-permute-start.3 = (bf16[1,3,2,32,384]{4,3,2,1,0:T(8,128)(2,1)S(1)}, bf16[1,3,2,32,384]{4,3,2,1,0:T(8,128)(2,1)S(1)}, u32[]{:S(2)}, u32[]{:S(2)}) collective-permute-start(bf16[1,3,2,32,384]{4,3,2,1,0:T(8,128)(2,1)S(1)} %slice.69), channel_id=1, source_target_pairs={{0,8},{4,12},{8,0},{12,4},{1,9},{5,13},{9,1},{13,5},{2,10},{6,14},... | collective-permute-start | bytes 442376 | tf_op jit(solution)/shard_map/ppermute | solution.py:416
  38.5 10.3 %collective-permute-start.5 = (bf16[3,2,32,640]{3,2,1,0:T(8,128)(2,1)S(1)}, bf16[3,2,32,640]{3,2,1,0:T(8,128)(2,1)S(1)}, u32[]{:S(2)}, u32[]{:S(2)}) collective-permute-start(bf16[3,2,32,640]{3,2,1,0:T(8,128)(2,1)S(1)} %slice.71), channel_id=1, source_target_pairs={{0,1},{1,2},{2,3},{3,0},{4,5},{5,6},{6,7},{7,4},{8,9},{9,10},{10,1... | collective-permute-start | bytes 737288 | tf_op jit(solution)/shard_map/ppermute | solution.py:430
  40.2 4.1 %collective-permute-start.6 = (bf16[1,1,2,32,384]{4,3,2,1,0:T(8,128)(2,1)S(1)}, bf16[1,1,2,32,384]{4,3,2,1,0:T(8,128)(2,1)S(1)}, u32[]{:S(2)}, u32[]{:S(2)}) collective-permute-start(bf16[1,1,2,32,384]{4,3,2,1,0:T(8,128)(2,1)S(1)} %slice.73), channel_id=1, source_target_pairs={{0,8},{4,12},{8,0},{12,4},{1,9},{5,13},{9,1},{13,5},{2,10},{6,14},... | collective-permute-start | bytes 147464 | tf_op jit(solution)/shard_map/ppermute | solution.py:416
  44.4 6.1 %collective-permute-start.4 = (bf16[3,2,32,384]{3,2,1,0:T(8,128)(2,1)S(1)}, bf16[3,2,32,384]{3,2,1,0:T(8,128)(2,1)S(1)}, u32[]{:S(2)}, u32[]{:S(2)}) collective-permute-start(bf16[3,2,32,384]{3,2,1,0:T(8,128)(2,1)S(1)} %fusion.1), channel_id=1, source_target_pairs={{0,1},{1,2},{2,3},{4,5},{5,6},{6,7},{8,9},{9,10},{10,11},{12,13},{... | collective-permute-start | bytes 442376 | tf_op jit(solution)/shard_map/ppermute | solution.py:430

commit v7 on v5

--- a/solution.py
+++ b/solution.py
@@ -237,27 +237,24 @@
 
 def basis_kernel(basis, small):
     channels = basis.shape[0]
-    width = small.shape[2]
-    group = small.shape[1]
-
-    def one_slab(index, carry):
-        first = pl.multiple_of(index * width, width)
+    width = small.shape[3]
+    group = small.shape[2]
+
+    for first in range(0, channels, width):
 
         def phases(rows, factor):
             row = lax.broadcasted_iota(jnp.int32, (rows, width), 0) * factor
             column = first + lax.broadcasted_iota(jnp.int32, (rows, width), 1)
             return (row * column) & (channels - 1)
 
-        small[0], small[1] = turn(phases(group, 1), channels)
+        slab = first // width
+        small[slab, 0], small[slab, 1] = turn(phases(group, 1), channels)
         count = channels // group
         large = turn(phases(count, group), channels)
         for at in range(count):
-            real, imag = times((large[0][at : at + 1], large[1][at : at + 1]), (small[0], small[1]))
+            real, imag = times((large[0][at : at + 1], large[1][at : at + 1]), (small[slab, 0], small[slab, 1]))
             basis[at * group : (at + 1) * group, pl.ds(first, width)] = real.astype(jnp.bfloat16)
-            basis[at * group : (at + 1) * group, pl.ds(pl.multiple_of(channels + first, width), width)] = imag.astype(jnp.bfloat16)
-        return carry
-
-    lax.fori_loop(0, channels // width, one_slab, 0)
+            basis[at * group : (at + 1) * group, pl.ds(channels + first, width)] = imag.astype(jnp.bfloat16)
 
 
 def make_basis(channels):
@@ -265,7 +262,7 @@
         basis_kernel,
         out_specs=pl.BlockSpec(memory_space=pltpu.VMEM),
         out_shape=jax.ShapeDtypeStruct((channels, 2 * channels), jnp.bfloat16),
-        scratch_shapes=[pltpu.VMEM((2, 32, 256), jnp.float32)],
+        scratch_shapes=[pltpu.VMEM((channels // 256, 2, 32, 256), jnp.float32)],
         compiler_params=pltpu.CompilerParams(vmem_limit_bytes=8 * 2**20),
         cost_estimate=pl.CostEstimate(flops=2**30, bytes_accessed=4 * channels * channels, transcendentals=0),
         name="basis",
@@ -296,8 +293,7 @@
     width = min(256, channels)
     scale = 1.0 / math.sqrt(channels)
 
-    def one_slab(index, carry):
-        first = pl.multiple_of(index * width, width)
+    for first in range(0, channels, width):
         for part, value in enumerate(transform(pieces, starts, basis, first, width)):
             value = ((value + others[part, :, pl.ds(first, width)]) * scale).astype(jnp.bfloat16).astype(jnp.float32)
             for t in range(frames):
@@ -306,9 +302,6 @@
                     term = taps[k : k + 1, pl.ds(first, width)] * value[(t - k) * beams : (t - k + 1) * beams]
                     total = term if total is None else total + term
                 out[part, t, :, pl.ds(first, width)] = total
-        return carry
-
-    lax.fori_loop(0, channels // width, one_slab, 0)
 
 
 def part_kernel(starts, wraps, *refs):

time: 52.4 us -> 52.4 us (level)
  Pallas kernels: 30.3 us -> 29.4 us
  waiting for transfers between devices: 10.2 us -> 11 us
  transfers between devices with their start and end apart: 7 -> 7, of which waited for: 3 -> 4; matrix products, arithmetic and copies ran while one was open for 1% -> 1% of each run, Pallas kernels for 11% -> 9%
where the time goes in v7:
time: 52.4 us; the launch traced here: 52.2 us
  Pallas kernels  29.4 us (56%)
  starting transfers between devices  11 us (21%)
  waiting for transfers between devices  11 us (21%)
    pallas_call x2, Pallas kernels, beamform(): pl.pallas_call(functools.partial(beam_kernel, first, tables is None), in_...  22.9 us
    ppermute x5, waiting for transfers between devices, across(): return lax.ppermute(value, 'chan', [(i, i ^ mask) for i in range(devices)])  10.6 us
    ppermute x5, starting transfers between devices, across(): return lax.ppermute(value, 'chan', [(i, i ^ mask) for i in range(devices)])  5.89 us
    pallas_call x4, Pallas kernels, small_call(): pl.pallas_call(kernel, in_specs=[whole] * len(args), out_specs=pl.BlockSp...  5.19 us
    ppermute x2, starting transfers between devices, ended(): return (own, lax.ppermute(own[own.shape[0] - before:], 'tm', hops))  5.12 us
    pallas_call x1, Pallas kernels, make_basis(): pl.pallas_call(basis_kernel, out_specs=pl.BlockSpec(memory_space=pltpu.VM...  1.39 us
  transfers between devices with their start and end apart: 7, of which 4 were waited for; matrix products, arithmetic and copies ran while one was open for 1% of the time, Pallas kernels for 9%

profile of v7, /device:TPU:0, one launch (start us, length us, event | category | flops | bytes accessed | tf_op | source)
XLA Modules:
  0.0 52.2 jit_solution(3171958969242817618)
XLA Ops:
  0.0 15.4 %beam.2 = (bf16[2,4,2,32,640]{4,3,2,1,0:T(8,128)(2,1)S(1)}, bf16[2,4,2,32,640]{4,3,2,1,0:T(8,128)(2,1)S(1)}, f32[2,32,256,128]{3,2,1,0:T(8,128)S(1)}, f32[2,16,2...) custom-call(s32[2,1024]{1,0:T(2,128)} %bitcast.8, s32[2,128]{1,0:T(2,128)} %bitcast.9, bf16[2,4,256,1024]{3,2,1,0:T(8,128)(2,1)} %refs_2_.1), custom_call_target="tpu_custom_call" | custom-call | flops 10737418240 | bytes 5242880 | tf_op jit(solution)/shard_map/beam/pallas_call | solution.py:224
  15.4 0.6 %collective-permute-start = (bf16[2,4,2,32,640]{4,3,2,1,0:T(8,128)(2,1)S(1)}, bf16[2,4,2,32,640]{4,3,2,1,0:T(8,128)(2,1)S(1)}, u32[]{:S(2)}, u32[]{:S(2)}) collective-permute-start(bf16[2,4,2,32,640]{4,3,2,1,0:T(8,128)(2,1)S(1)} %get-tuple-element.24), channel_id=1, source_target_pairs={{0,4},{4,0},{8,12},{12,8},{1,5},{5,1},{9,13},{13,9},{2,6},{6,2},{1... | collective-permute-start | bytes 1966088 | tf_op jit(solution)/shard_map/ppermute | solution.py:390
  16.0 1.7 %collective-permute-done = bf16[2,4,2,32,640]{4,3,2,1,0:T(8,128)(2,1)S(1)} collective-permute-done((bf16[2,4,2,32,640]{4,3,2,1,0:T(8,128)(2,1)S(1)}, bf16[2,4,2,32,640]{4,3,2,1,0:T(8,128)(2,1)S(1)}, u32[]{:S(2)}, u32[]{:S(2)}) %collective-permute-start) | collective-permute-done | bytes 655392 | tf_op jit(solution)/shard_map/ppermute | solution.py:390
  17.7 0.1 add_convert_fusion.1
  17.8 7.4 %beam.3 = (bf16[2,4,2,32,384]{4,3,2,1,0:T(8,128)(2,1)S(1)}, bf16[2,4,2,32,384]{4,3,2,1,0:T(8,128)(2,1)S(1)}) custom-call(f32[2,32,256,128]{3,2,1,0:T(8,128)S(1)} %get-tuple-element.25.refs_0_, f32[2,16,256,128]{3,2,1,0:T(8,128)S(1)} %get-tuple-element.26.refs_1_, bf16[2,4,256,1024]{3,2,1,0:T(8,128)(2,1)S(1)} %get-tuple-element.27.refs_2_), custom_call_target="tpu_custom_call" | custom-call | flops 6442450944 | bytes 3145728 | tf_op jit(solution)/shard_map/beam/pallas_call | solution.py:224
  25.2 0.4 collective-permute-start.1
  25.7 2.6 %collective-permute-start.2 = (bf16[1,4,2,32,640]{4,3,2,1,0:T(8,128)(2,1)S(1)}, bf16[1,4,2,32,640]{4,3,2,1,0:T(8,128)(2,1)S(1)}, u32[]{:S(2)}, u32[]{:S(2)}) collective-permute-start(bf16[1,4,2,32,640]{4,3,2,1,0:T(8,128)(2,1)S(1)} %add_convert_fusion.1), channel_id=1, source_target_pairs={{0,8},{4,12},{8,0},{12,4},{1,9},{5,13},{9,1},{13,5},{2,10},{6,14},... | collective-permute-start | bytes 983048 | tf_op jit(solution)/shard_map/ppermute | solution.py:390
  28.3 1.4 %basis.1.refs_1_.refs_2_.refs_3_ = bf16[1024,2048]{1,0:T(8,128)(2,1)S(1)} custom-call(), custom_call_target="tpu_custom_call" | custom-call | flops 1073741824 | bytes 4194304 | tf_op jit(solution)/shard_map/basis/pallas_call | solution.py:261
  29.7 0.0 collective-permute-done.1
  29.7 0.1 add_convert_fusion.2
  29.8 0.0 copy-start
  29.8 6.7 %collective-permute-done.2 = bf16[1,4,2,32,640]{4,3,2,1,0:T(8,128)(2,1)S(1)} collective-permute-done((bf16[1,4,2,32,640]{4,3,2,1,0:T(8,128)(2,1)S(1)}, bf16[1,4,2,32,640]{4,3,2,1,0:T(8,128)(2,1)S(1)}, u32[]{:S(2)}, u32[]{:S(2)}) %collective-permute-start.2) | collective-permute-done | bytes 327712 | tf_op jit(solution)/shard_map/ppermute | solution.py:390
  36.5 1.7 %collective-permute-start.3 = (bf16[1,3,2,32,384]{4,3,2,1,0:T(8,128)(2,1)S(1)}, bf16[1,3,2,32,384]{4,3,2,1,0:T(8,128)(2,1)S(1)}, u32[]{:S(2)}, u32[]{:S(2)}) collective-permute-start(bf16[1,3,2,32,384]{4,3,2,1,0:T(8,128)(2,1)S(1)} %slice.69), channel_id=1, source_target_pairs={{0,8},{4,12},{8,0},{12,4},{1,9},{5,13},{9,1},{13,5},{2,10},{6,14},... | collective-permute-start | bytes 442376 | tf_op jit(solution)/shard_map/ppermute | solution.py:390
  38.3 0.1 fusion.refs_0_
  38.4 1.6 %collective-permute-start.5 = (bf16[3,2,32,640]{3,2,1,0:T(8,128)(2,1)S(1)}, bf16[3,2,32,640]{3,2,1,0:T(8,128)(2,1)S(1)}, u32[]{:S(2)}, u32[]{:S(2)}) collective-permute-start(bf16[3,2,32,640]{3,2,1,0:T(8,128)(2,1)S(1)} %slice.71), channel_id=1, source_target_pairs={{0,1},{1,2},{2,3},{3,0},{4,5},{5,6},{6,7},{7,4},{8,9},{9,10},{10,1... | collective-permute-start | bytes 737288 | tf_op jit(solution)/shard_map/ppermute | solution.py:404
  40.1 0.5 %collective-permute-start.6 = (bf16[1,1,2,32,384]{4,3,2,1,0:T(8,128)(2,1)S(1)}, bf16[1,1,2,32,384]{4,3,2,1,0:T(8,128)(2,1)S(1)}, u32[]{:S(2)}, u32[]{:S(2)}) collective-permute-start(bf16[1,1,2,32,384]{4,3,2,1,0:T(8,128)(2,1)S(1)} %slice.73), channel_id=1, source_target_pairs={{0,8},{4,12},{8,0},{12,4},{1,9},{5,13},{9,1},{13,5},{2,10},{6,14},... | collective-permute-start | bytes 147464 | tf_op jit(solution)/shard_map/ppermute | solution.py:390
  40.6 1.4 %shard_map.47.refs_1_ = f32[2,128,1024]{2,1,0:T(8,128)S(1)} custom-call(bf16[4,2,32,640]{3,2,1,0:T(8,128)(2,1)S(1)} %fusion.refs_0_, bf16[1024,2048]{1,0:T(8,128)(2,1)S(1)} %basis.1.refs_1_.refs_2_.refs_3_), custom_call_target="tpu_custom_call" | custom-call | flops 1073741824 | bytes 4194304 | tf_op jit(solution)/shard_map/pallas_call | solution.py:357
  42.0 2.1 %collective-permute-done.6 = bf16[1,1,2,32,384]{4,3,2,1,0:T(8,128)(2,1)S(1)} collective-permute-done((bf16[1,1,2,32,384]{4,3,2,1,0:T(8,128)(2,1)S(1)}, bf16[1,1,2,32,384]{4,3,2,1,0:T(8,128)(2,1)S(1)}, u32[]{:S(2)}, u32[]{:S(2)}) %collective-permute-start.6) | collective-permute-done | bytes 49184 | tf_op jit(solution)/shard_map/ppermute | solution.py:390
  44.2 0.1 fusion.1
  44.3 3.5 %collective-permute-start.4 = (bf16[3,2,32,384]{3,2,1,0:T(8,128)(2,1)S(1)}, bf16[3,2,32,384]{3,2,1,0:T(8,128)(2,1)S(1)}, u32[]{:S(2)}, u32[]{:S(2)}) collective-permute-start(bf16[3,2,32,384]{3,2,1,0:T(8,128)(2,1)S(1)} %fusion.1), channel_id=1, source_target_pairs={{0,1},{1,2},{2,3},{4,5},{5,6},{6,7},{8,9},{9,10},{10,11},{12,13},{... | collective-permute-start | bytes 442376 | tf_op jit(solution)/shard_map/ppermute | solution.py:404
  47.8 0.9 %shard_map.48.refs_2_ = f32[2,4,32,1024]{3,2,1,0:T(8,128)S(1)} custom-call(bf16[4,2,32,384]{3,2,1,0:T(8,128)(2,1)S(1)} %pad_maximum_fusion.refs_0_, f32[2,128,1024]{2,1,0:T(8,128)S(1)} %shard_map.47.refs_1_, bf16[1024,2048]{1,0:T(8,128)(2,1)S(1)} %basis.1.refs_1_.refs_2_.refs_3_, f32[4,1024]{1,0:T(4,128)S(1)} %copy-done), custom_call_target="tpu_custom_call" | custom-call | flops 1073741824 | bytes 4194304 | tf_op jit(solution)/shard_map/pallas_call | solution.py:357
  48.7 1.2 %shard_map.46.refs_1_ = f32[2,96,1024]{2,1,0:T(8,128)S(1)} custom-call(bf16[3,2,32,640]{3,2,1,0:T(8,128)(2,1)S(1)} %collective-permute-done.5.refs_0_, bf16[1024,2048]{1,0:T(8,128)(2,1)S(1)} %basis.1.refs_1_.refs_2_.refs_3_), custom_call_target="tpu_custom_call" | custom-call | flops 805306368 | bytes 4194304 | tf_op jit(solution)/shard_map/pallas_call | solution.py:357
  50.0 0.5 collective-permute-done.4.refs_0_
  50.4 1.6 %shard_map.49 = bf16[2,32,4,1024]{3,2,1,0:T(4,128)(2,1)} custom-call(bf16[3,2,32,384]{3,2,1,0:T(8,128)(2,1)S(1)} %collective-permute-done.4.refs_0_, f32[2,96,1024]{2,1,0:T(8,128)S(1)} %shard_map.46.refs_1_, f32[2,4,32,1024]{3,2,1,0:T(8,128)S(1)} %shard_map.48.refs_2_, bf16[1024,2048]{1,0:T(8,128)(2,1)S(1)} %basis.1.refs_1_.refs_2_.refs_3_, ...), custom_call_target="tpu_custom_call" | custom-call | flops 805306368 | bytes 4194304 | tf_op jit(solution)/shard_map/pallas_call | solution.py:357
  (8 shorter events, 0.1 us)
Async XLA Ops:
  15.4 2.3 %collective-permute-start = (bf16[2,4,2,32,640]{4,3,2,1,0:T(8,128)(2,1)S(1)}, bf16[2,4,2,32,640]{4,3,2,1,0:T(8,128)(2,1)S(1)}, u32[]{:S(2)}, u32[]{:S(2)}) collective-permute-start(bf16[2,4,2,32,640]{4,3,2,1,0:T(8,128)(2,1)S(1)} %get-tuple-element.24), channel_id=1, source_target_pairs={{0,4},{4,0},{8,12},{12,8},{1,5},{5,1},{9,13},{13,9},{2,6},{6,2},{1... | collective-permute-start | bytes 1966088 | tf_op jit(solution)/shard_map/ppermute | solution.py:390
  25.2 4.4 %collective-permute-start.1 = (bf16[2,4,2,32,384]{4,3,2,1,0:T(8,128)(2,1)S(1)}, bf16[2,4,2,32,384]{4,3,2,1,0:T(8,128)(2,1)S(1)}, u32[]{:S(2)}, u32[]{:S(2)}) collective-permute-start(bf16[2,4,2,32,384]{4,3,2,1,0:T(8,128)(2,1)S(1)} %get-tuple-element.29), channel_id=1, source_target_pairs={{0,4},{4,0},{8,12},{12,8},{1,5},{5,1},{9,13},{13,9},{2,6},{6,2},{1... | collective-permute-start | bytes 1179656 | tf_op jit(solution)/shard_map/ppermute | solution.py:390
  25.7 10.9 %collective-permute-start.2 = (bf16[1,4,2,32,640]{4,3,2,1,0:T(8,128)(2,1)S(1)}, bf16[1,4,2,32,640]{4,3,2,1,0:T(8,128)(2,1)S(1)}, u32[]{:S(2)}, u32[]{:S(2)}) collective-permute-start(bf16[1,4,2,32,640]{4,3,2,1,0:T(8,128)(2,1)S(1)} %add_convert_fusion.1), channel_id=1, source_target_pairs={{0,8},{4,12},{8,0},{12,4},{1,9},{5,13},{9,1},{13,5},{2,10},{6,14},... | collective-permute-start | bytes 983048 | tf_op jit(solution)/shard_map/ppermute | solution.py:390
  29.8 18.0 %copy-start = (f32[4,1024]{1,0:T(4,128)S(1)}, f32[4,1024]{1,0:T(4,128)}, u32[]{:S(2)}) copy-start(f32[4,1024]{1,0:T(4,128)} %refs_4_.1) | copy-start | bytes 49156
  36.5 7.6 %collective-permute-start.3 = (bf16[1,3,2,32,384]{4,3,2,1,0:T(8,128)(2,1)S(1)}, bf16[1,3,2,32,384]{4,3,2,1,0:T(8,128)(2,1)S(1)}, u32[]{:S(2)}, u32[]{:S(2)}) collective-permute-start(bf16[1,3,2,32,384]{4,3,2,1,0:T(8,128)(2,1)S(1)} %slice.69), channel_id=1, source_target_pairs={{0,8},{4,12},{8,0},{12,4},{1,9},{5,13},{9,1},{13,5},{2,10},{6,14},... | collective-permute-start | bytes 442376 | tf_op jit(solution)/shard_map/ppermute | solution.py:390
  38.4 10.3 %collective-permute-start.5 = (bf16[3,2,32,640]{3,2,1,0:T(8,128)(2,1)S(1)}, bf16[3,2,32,640]{3,2,1,0:T(8,128)(2,1)S(1)}, u32[]{:S(2)}, u32[]{:S(2)}) collective-permute-start(bf16[3,2,32,640]{3,2,1,0:T(8,128)(2,1)S(1)} %slice.71), channel_id=1, source_target_pairs={{0,1},{1,2},{2,3},{3,0},{4,5},{5,6},{6,7},{7,4},{8,9},{9,10},{10,1... | collective-permute-start | bytes 737288 | tf_op jit(solution)/shard_map/ppermute | solution.py:404
  40.1 4.1 %collective-permute-start.6 = (bf16[1,1,2,32,384]{4,3,2,1,0:T(8,128)(2,1)S(1)}, bf16[1,1,2,32,384]{4,3,2,1,0:T(8,128)(2,1)S(1)}, u32[]{:S(2)}, u32[]{:S(2)}) collective-permute-start(bf16[1,1,2,32,384]{4,3,2,1,0:T(8,128)(2,1)S(1)} %slice.73), channel_id=1, source_target_pairs={{0,8},{4,12},{8,0},{12,4},{1,9},{5,13},{9,1},{13,5},{2,10},{6,14},... | collective-permute-start | bytes 147464 | tf_op jit(solution)/shard_map/ppermute | solution.py:390
  44.3 6.1 %collective-permute-start.4 = (bf16[3,2,32,384]{3,2,1,0:T(8,128)(2,1)S(1)}, bf16[3,2,32,384]{3,2,1,0:T(8,128)(2,1)S(1)}, u32[]{:S(2)}, u32[]{:S(2)}) collective-permute-start(bf16[3,2,32,384]{3,2,1,0:T(8,128)(2,1)S(1)} %fusion.1), channel_id=1, source_target_pairs={{0,1},{1,2},{2,3},{4,5},{5,6},{6,7},{8,9},{9,10},{10,11},{12,13},{... | collective-permute-start | bytes 442376 | tf_op jit(solution)/shard_map/ppermute | solution.py:404
